TPU v7x, 32 devices: a whole 2x2x4 slice. The times are simulated.
32 devices in a mesh: row: 8 (over y, x, core), col: 4 (over z).
Axes of the slice: x: 2, y: 2, z: 4, core: 2. Of those that a mesh axis runs over, the one named last changes fastest.
Arguments:
- density: bfloat16 [4096, 4096], P('row', 'col'), as said below
- pattern: int32 [32, 32], P('row', 'col'), may hold values from 0 to 1, as said below
Outputs:
- purified: float32 [4096, 4096], P('row', 'col')
- occupation: float32 [], replicated
Inputs may be any that keep to these rules, and one draw needn't show every extreme that they name: density is symmetric. pattern is symmetric, 0 or 1, with every diagonal block kept.
All inputs are finite; a program needn't handle non-finite values.
Results may differ from a plain program's by a relative error of at most 0.0047.
Values may be sent and summed in bfloat16 or wider, within the bound.
No kernel may reach another device: no remote copies, remote signals or barrier semaphores. Data moves between devices by JAX's collectives and lax.ppermute only.
A program may use at most 64 MiB of HBM per device.

v0:
```python
import jax
import jax.numpy as jnp
from jax import lax
from jax.experimental import pallas as pl
from jax.experimental.pallas import tpu as pltpu
from jax.sharding import PartitionSpec as P


B = 128


def filtered(values, pattern):
    block_rows, block_cols = pattern.shape
    blocked = (
        values.reshape(block_rows, B, block_cols, B) * pattern.astype(jnp.float32)[:, None, :, None]
    )
    return blocked.reshape(block_rows * B, block_cols * B)


def general(density, pattern):
    masked = filtered(density.astype(jnp.float32), pattern).astype(jnp.bfloat16)
    row_count = masked.shape[0]
    col_count = masked.shape[1]
    column = lax.all_gather(masked, "row", axis=0, tiled=True)

    def multiply(factor):
        return jnp.dot(
            lax.all_gather(factor, "col", axis=1, tiled=True),
            column,
            preferred_element_type=jnp.float32,
        )

    squared = filtered(multiply(masked), pattern).astype(jnp.bfloat16)
    cubic_term = filtered(multiply(squared), pattern)
    purified = 3.0 * squared.astype(jnp.float32) - 2.0 * cubic_term
    row_index = lax.axis_index("row") * row_count + jnp.arange(row_count, dtype=jnp.int32)
    col_index = lax.axis_index("col") * col_count + jnp.arange(col_count, dtype=jnp.int32)
    diagonal_sum = jnp.sum(jnp.where(row_index[:, None] == col_index[None, :], purified, 0.0))
    total_trace = lax.psum(diagonal_sum, ("row", "col"))
    occupation = total_trace / (row_count * lax.axis_size("row"))
    return (purified, occupation)


TILE = 256
EXTRA = 16


def multiply(acc, left, right, fresh):
    rows, columns = acc.shape

    @pl.loop(0, columns // TILE)
    def _(n):
        lanes = pl.ds(pl.multiple_of(n * TILE, TILE), TILE)
        part = jnp.dot(
            left[:rows, :rows], right[0, :, lanes], preferred_element_type=jnp.float32
        ) + jnp.dot(left[:rows, rows:], right[1, :, lanes], preferred_element_type=jnp.float32)
        if fresh:
            acc[:, lanes] = part
        else:
            acc[:, lanes] += part


def blocks(rows, columns, body):
    @pl.loop(0, (rows // B) * (columns // B))
    def _(block):
        a = block // (columns // B)
        b = block % (columns // B)
        body(
            a,
            b,
            (pl.ds(pl.multiple_of(a * B, B), B), pl.ds(pl.multiple_of(b * B, B), B)),
        )


def square_early_kernel(where, own, pair, middle2, outer2, *refs):
    rights = refs[:8]
    acc, panel, right, left_sem, right_sem = refs[8:]
    row, col = where[0], where[1]
    pltpu.make_async_copy(own, panel.at[0], left_sem.at[0]).start()
    pltpu.make_async_copy(pair, panel.at[1], left_sem.at[1]).start()
    inner = (col == 1) | (col == 2)

    @pl.when(inner)
    def _():
        pltpu.make_async_copy(middle2, panel.at[2], left_sem.at[2]).start()

    @pl.when(jnp.logical_not(inner))
    def _():
        pltpu.make_async_copy(outer2, panel.at[2], left_sem.at[2]).start()

    for k in range(8):
        slot = row ^ k
        pltpu.make_async_copy(rights[k], right.at[slot], right_sem.at[slot]).start()
    for d in range(3):
        slot = 2 * (col ^ d)
        pltpu.make_async_copy(panel.at[d], panel.at[d], left_sem.at[d]).wait()
        for t in range(2):
            there = right.at[slot + t]
            pltpu.make_async_copy(there, there, right_sem.at[slot + t]).wait()
        multiply(acc, panel.at[d], right.at[pl.ds(slot, 2)], d == 0)
    slot = 2 * (col ^ 3)
    for t in range(2):
        there = right.at[slot + t]
        pltpu.make_async_copy(there, there, right_sem.at[slot + t]).wait()


def square_late_kernel(where, pattern, own, acc_in, middle1, outer3, right_all, *refs):
    squared_ref, sum_ref, far, right, acc, left_sem, right_sem = refs
    row, col = where[0], where[1]
    rows, columns = acc.shape
    inner = (col == 1) | (col == 2)

    @pl.when(inner)
    def _():
        pltpu.make_async_copy(middle1, far, left_sem).start()

    @pl.when(jnp.logical_not(inner))
    def _():
        pltpu.make_async_copy(outer3, far, left_sem).start()

    fetch = pltpu.make_async_copy(right_all.at[pl.ds(2 * (col ^ 3), 2)], right, right_sem)
    fetch.start()
    pltpu.make_async_copy(far, far, left_sem).wait()
    fetch.wait()
    multiply(acc, far, right, True)
    sum_ref[...] = jnp.zeros_like(sum_ref)

    def body(a, b, part):
        kept = pattern[a, b].astype(jnp.float32)
        squared = ((acc_in[part] + acc[part]) * kept).astype(jnp.bfloat16)
        squared_ref[part] = squared
        wide = squared.astype(jnp.float32)
        masked = own[part].astype(jnp.float32)
        offset = row * rows + a * B - (col * columns + b * B)
        diagonal = (
            lax.broadcasted_iota(jnp.int32, (B, B), 0) + offset
            == lax.broadcasted_iota(jnp.int32, (B, B), 1)
        )
        term = jnp.where(diagonal, 3.0 * wide, 0.0) - 2.0 * wide * masked
        sum_ref[...] += jnp.sum(term.reshape(B // 8, 8, B), axis=0)

    blocks(rows, columns, body)


def turn_kernel(where, squared, same_ref, cross_ref):
    core = where[0] % 2
    half = same_ref.shape[0]

    def body(a, b, part):
        for out, h in ((same_ref, core), (cross_ref, 1 - core)):
            lanes = pl.ds(pl.multiple_of(h * half + b * B, B), B)
            out[part[1], part[0]] = squared[part[0], lanes].T

    blocks(half, half, body)


def own_square_kernel(where, panel, other, far, far_other, out):
    row, col = where[0], where[1]
    core, chip = row % 2, row // 2
    rows = out.shape[0]
    d = col ^ chip
    for source, last, h in ((panel, far, core), (other, far_other, 1 - core)):
        total = None
        for left, right in [(panel.at[d], source.at[d]) for d in range(3)] + [(far, last)]:
            part = lax.dot_general(
                left[:rows, :],
                right[:rows, :],
                (((1,), (1,)), ((), ())),
                preferred_element_type=jnp.float32,
            )
            total = part if total is None else total + part
        lanes = pl.ds(pl.multiple_of(h * rows, rows), rows)
        near = panel[jnp.minimum(d, 2), rows : rows + EXTRA, lanes].astype(jnp.float32)
        kept = jnp.where(d == 3, far[rows : rows + EXTRA, lanes].astype(jnp.float32), near)
        for a in range(rows // B):
            out[a * B : (a + 1) * B, lanes] = (
                total[a * B : (a + 1) * B] * kept[a : a + 1]
            ).astype(jnp.bfloat16)


def cubic_early_kernel(where, squared, local_square, right_all, acc, right, sem):
    row, col = where[0], where[1]
    chip = row // 2
    first = pltpu.make_async_copy(right_all.at[pl.ds(2 * col, 2)], right.at[0], sem.at[0])
    second = pltpu.make_async_copy(right_all.at[pl.ds(2 * chip, 2)], right.at[1], sem.at[1])
    first.start()
    second.start()
    first.wait()
    second.wait()
    multiply(acc, squared, right.at[0], True)

    @pl.when(chip != col)
    def _():
        multiply(acc, local_square, right.at[1], False)


def cubic_late_kernel(where, pattern, squared, acc_in, turn1, turn2, *refs):
    sides, right_all, purified_ref = refs[:6], refs[6], refs[7]
    left, right, acc, left_sem, right_sem = refs[8:]
    row, col = where[0], where[1]
    core, chip = row % 2, row // 2
    rows, columns = acc.shape
    corner = chip == col
    place = col - (col > chip).astype(jnp.int32)
    sources = []
    for i in range(3):
        index = (place + 2 - i) % 3
        source = jnp.where(corner, col ^ (i + 1), index + (index >= chip).astype(jnp.int32))
        sources.append(source)

    def fetch(i):
        return pltpu.make_async_copy(
            right_all.at[pl.ds(2 * sources[i], 2)], right.at[i], right_sem.at[i]
        )

    fetch(0).start()
    fetch(1).start()

    @pl.when(jnp.logical_not(corner))
    def _():
        pltpu.make_async_copy(turn1, left.at[0], left_sem.at[0]).start()
        pltpu.make_async_copy(turn2, left.at[1], left_sem.at[1]).start()

    @pl.when(corner)
    def _():
        for i in range(3):
            for u in range(2):
                lanes = pl.ds(pl.multiple_of((core ^ u) * rows, rows), rows)
                pltpu.make_async_copy(
                    sides[2 * i + u], left.at[i, :, lanes], left_sem.at[i]
                ).start()
        fetch(2).start()

    for i in range(2):
        pltpu.make_async_copy(left.at[i], left.at[i], left_sem.at[i]).wait()
        fetch(i).wait()
        multiply(acc, left.at[i], right.at[i], i == 0)

    @pl.when(corner)
    def _():
        pltpu.make_async_copy(left.at[2], left.at[2], left_sem.at[2]).wait()
        fetch(2).wait()
        multiply(acc, left.at[2], right.at[2], False)

    def body(a, b, part):
        kept = pattern[a, b].astype(jnp.float32)
        wide = squared[part].astype(jnp.float32)
        purified_ref[part] = 3.0 * wide - 2.0 * ((acc_in[part] + acc[part]) * kept)

    blocks(rows, columns, body)


ANYWHERE = pl.BlockSpec(memory_space=pl.ANY)
SCALARS = pl.BlockSpec(memory_space=pltpu.SMEM)
WHOLE = pl.BlockSpec(memory_space=pltpu.VMEM)
DMA = pltpu.SemaphoreType.DMA


def call(kernel, specs, args, outs, scratch, flops, moved):
    return pl.pallas_call(
        kernel,
        out_shape=outs,
        in_specs=specs,
        out_specs=jax.tree.map(lambda _: WHOLE, outs),
        scratch_shapes=scratch,
        compiler_params=pltpu.CompilerParams(vmem_limit_bytes=24 << 20),
        cost_estimate=pl.CostEstimate(flops=flops, bytes_accessed=moved, transcendentals=0),
    )(*args)


def swap(x, k):
    return lax.ppermute(x, "row", [(i, i ^ k) for i in range(8)])


def column_gather(x):
    by_x = swap(x, 2)
    by_y = swap(x, 4)
    core = swap(x, 1)
    by_x_core = swap(by_x, 1)
    by_y_core = swap(by_y, 1)
    diagonal = swap(by_x, 4)
    return [x, core, by_x, by_x_core, by_y, by_y_core, diagonal, swap(diagonal, 1)]


def rotate(x, step):
    pairs = []
    for row in range(8):
        planes = [c for c in range(4) if c != row // 2]
        for i in range(3):
            pairs.append((row * 4 + planes[i], row * 4 + planes[(i + step) % 3]))
    return lax.ppermute(x, ("row", "col"), pairs)


def to_corner(x, j, u):
    pairs = []
    for col in range(4):
        for core in range(2):
            source = (col ^ j) * 2 + core
            target = col * 2 + (core ^ u)
            pairs.append((source * 4 + col, target * 4 + col))
    return lax.ppermute(x, ("row", "col"), pairs)


def local(density, pattern):
    masked = filtered(density.astype(jnp.float32), pattern).astype(jnp.bfloat16)
    rows, columns = masked.shape
    row, col = lax.axis_index("row"), lax.axis_index("col")
    where = jnp.stack([row, col]).astype(jnp.int32)
    kept = jnp.repeat(pattern.astype(jnp.bfloat16), B, axis=1)
    kept = jnp.pad(kept, ((0, EXTRA - kept.shape[0]), (0, 0)))
    own = jnp.concatenate([masked, kept], axis=0)
    pair = lax.ppermute(own, "col", [(0, 1), (1, 0), (2, 3), (3, 2)])
    middle1 = lax.ppermute(own, "col", [(1, 2), (2, 1)])
    outer2 = lax.ppermute(middle1, "col", [(2, 3), (1, 0)])
    middle2 = lax.ppermute(pair, "col", [(1, 2), (2, 1)])
    outer3 = lax.ppermute(middle2, "col", [(2, 3), (1, 0)])
    rights = column_gather(masked)

    flops = 2 * 2 * rows * rows * columns
    size = 2 * rows * columns
    tile = jax.ShapeDtypeStruct((rows, columns), jnp.bfloat16)
    wide = jax.ShapeDtypeStruct((rows, columns), jnp.float32)
    extended = jax.ShapeDtypeStruct((rows + EXTRA, columns), jnp.bfloat16)
    acc = pltpu.VMEM((rows, columns), jnp.float32)
    partial, panel, right = call(
        square_early_kernel,
        [SCALARS] + [ANYWHERE] * 12,
        (where, own, pair, middle2, outer2, *rights),
        (
            wide,
            jax.ShapeDtypeStruct((3, rows + EXTRA, columns), jnp.bfloat16),
            jax.ShapeDtypeStruct((8, rows, columns), jnp.bfloat16),
        ),
        [DMA((3,)), DMA((8,))],
        3 * flops,
        24 * size,
    )
    other = swap(panel, 1)
    squared, sums, far = call(
        square_late_kernel,
        [SCALARS, SCALARS, WHOLE, WHOLE] + [ANYWHERE] * 3,
        (where, pattern, own, partial, middle1, outer3, right),
        (tile, jax.ShapeDtypeStruct((8, B), jnp.float32), extended),
        [pltpu.VMEM((2, rows, columns), jnp.bfloat16), acc, DMA(()), DMA(())],
        flops,
        8 * size,
    )
    turns = [rotate(squared, 1), rotate(squared, 2)]
    total = jnp.sum(sums)
    for k in (1, 2, 4):
        total = total + swap(total, k)
    quarter = jax.ShapeDtypeStruct((rows, rows), jnp.bfloat16)
    turned = call(
        turn_kernel,
        [SCALARS, WHOLE],
        (where, squared),
        (quarter, quarter),
        [],
        0,
        2 * size,
    )
    same, cross, total = lax.optimization_barrier((*turned, total))
    sides = [to_corner((same, cross)[u], j, u) for j in (1, 2, 3) for u in (0, 1)]
    local_square = call(
        own_square_kernel,
        [SCALARS] + [WHOLE] * 4,
        (where, panel, other, far, swap(far, 1)),
        tile,
        [],
        4 * flops,
        9 * size,
    )
    cubic = call(
        cubic_early_kernel,
        [SCALARS, WHOLE, WHOLE, ANYWHERE],
        (where, squared, local_square, right),
        wide,
        [pltpu.VMEM((2, 2, rows, columns), jnp.bfloat16), DMA((2,))],
        2 * flops,
        8 * size,
    )
    turns[0], turns[1], total = lax.optimization_barrier((*turns, total))
    for k in (1, 2):
        total = total + lax.ppermute(total, "col", [(i, i ^ k) for i in range(4)])
    purified = call(
        cubic_late_kernel,
        [SCALARS, SCALARS, WHOLE, WHOLE] + [ANYWHERE] * 9,
        (where, pattern, squared, cubic, *turns, *sides, right),
        wide,
        [
            pltpu.VMEM((3, rows, columns), jnp.bfloat16),
            pltpu.VMEM((3, 2, rows, columns), jnp.bfloat16),
            acc,
            DMA((3,)),
            DMA((3,)),
        ],
        3 * flops,
        16 * size,
    )
    return (purified, total / (rows * lax.axis_size("row")))


def solution(mesh):
    placed = (P("row", "col"), P("row", "col"))
    body = local if (mesh.shape["row"], mesh.shape["col"]) == (8, 4) else general
    return jax.shard_map(
        body, mesh=mesh, in_specs=placed, out_specs=(P("row", "col"), P()), check_vma=False
    )
```

profile of v0, /device:TPU:0, one launch (start us, length us, event | category | flops | bytes accessed | tf_op | source)
XLA Modules:
  0.0 216.9 jit_solution(11918860305541694031)
XLA Ops:
  2.6 3.0 %collective-permute-start.5 = (bf16[512,1024]{1,0:T(8,128)(2,1)S(1)}, bf16[512,1024]{1,0:T(8,128)(2,1)}, u32[]{:S(2)}, u32[]{:S(2)}) collective-permute-start(bf16[512,1024]{1,0:T(8,128)(2,1)S(1)} %fusion.1.refs_0_), channel_id=1, source_target_pairs={{0,8},{4,12},{8,0},{12,4},{16,24},{20,28},{24,16},{28,20},{1,9},{5... | collective-permute-start | bytes 3145736 | tf_op jit(solution)/shard_map/ppermute | solution.py:272
  5.8 1.6 collective-permute-start
  8.2 1.6 collective-permute-start.7
  9.7 19.1 %collective-permute-done.5.refs_2_ = bf16[512,1024]{1,0:T(8,128)(2,1)} collective-permute-done((bf16[512,1024]{1,0:T(8,128)(2,1)S(1)}, bf16[512,1024]{1,0:T(8,128)(2,1)}, u32[]{:S(2)}, u32[]{:S(2)}) %collective-permute-start.5) | collective-permute-done | bytes 1048608 | tf_op jit(solution)/shard_map/ppermute | solution.py:272
  28.9 1.8 collective-permute-start.9
  31.3 1.7 collective-permute-start.1
  35.8 19.3 %collective-permute-done.9.refs_6_ = bf16[512,1024]{1,0:T(8,128)(2,1)} collective-permute-done((bf16[512,1024]{1,0:T(8,128)(2,1)}, bf16[512,1024]{1,0:T(8,128)(2,1)}, u32[]{:S(2)}, u32[]{:S(2)}) %collective-permute-start.9) | collective-permute-done | bytes 1048608 | tf_op jit(solution)/shard_map/ppermute | solution.py:272
  55.2 4.9 %collective-permute-done.3.outer2 = bf16[528,1024]{1,0:T(8,128)(2,1)} collective-permute-done((bf16[528,1024]{1,0:T(8,128)(2,1)S(1)}, bf16[528,1024]{1,0:T(8,128)(2,1)}, u32[]{:S(2)}, u32[]{:S(2)}) %collective-permute-start.3) | collective-permute-done | bytes 1081376 | tf_op jit(solution)/shard_map/ppermute | solution.py:314
  61.4 8.3 %shard_map.41 = (f32[512,1024]{1,0:T(8,128)S(1)}, bf16[3,528,1024]{2,1,0:T(8,128)(2,1)}, bf16[8,512,1024]{2,1,0:T(8,128)(2,1)S(1)}) custom-call(s32[2]{0:T(128)S(1)} %pad_add_fusion.where, bf16[528,1024]{1,0:T(8,128)(2,1)S(1)} %fusion.2.own, bf16[528,1024]{1,0:T(8,128)(2,1)} %collective-permute-done.pair, bf16[528,1024]{1,0:T(8,128)(2,1)} %collective-permute-done.1.middle2, ...), custom_call_target="tpu_custom_call" | custom-call | flops 3221225472 | bytes 25165824 | tf_op jit(solution)/shard_map/pallas_call | solution.py:260
  69.8 1.3 collective-permute-start.11
  71.1 28.5 %collective-permute-done.11.outer3 = bf16[528,1024]{1,0:T(8,128)(2,1)S(1)} collective-permute-done((bf16[528,1024]{1,0:T(8,128)(2,1)}, bf16[528,1024]{1,0:T(8,128)(2,1)S(1)}, u32[]{:S(2)}, u32[]{:S(2)}) %collective-permute-start.11) | collective-permute-done | bytes 1081376 | tf_op jit(solution)/shard_map/ppermute | solution.py:316
  99.6 5.1 %shard_map.42 = (bf16[512,1024]{1,0:T(8,128)(2,1)S(1)}, f32[8,128]{1,0:T(8,128)S(1)}, bf16[528,1024]{1,0:T(8,128)(2,1)}) custom-call(s32[2]{0:T(128)S(1)} %pad_add_fusion.where, s32[4,8]{1,0:T(4,128)S(1)} %copy-done.4, bf16[528,1024]{1,0:T(8,128)(2,1)S(1)} %fusion.2.own, f32[512,1024]{1,0:T(8,128)S(1)} %get-tuple-element.16.acc_in, ...), custom_call_target="tpu_custom_call" | custom-call | flops 1073741824 | bytes 8388608 | tf_op jit(solution)/shard_map/pallas_call | solution.py:260
  106.3 1.8 shard_map.45
  113.2 8.6 %collective-permute-start.17 = (f32[]{:T(128)}, f32[]{:T(128)}, u32[]{:S(2)}, u32[]{:S(2)}) collective-permute-start(f32[]{:T(128)} %add.17), channel_id=1, source_target_pairs={{0,8},{4,12},{8,0},{12,4},{16,24},{20,28},{24,16},{28,20},{1,9},{5... | collective-permute-start | bytes 20 | tf_op jit(solution)/shard_map/ppermute | solution.py:272
  122.8 4.9 %collective-permute-start.18 = (f32[]{:T(128)}, f32[]{:T(128)}, u32[]{:S(2)}, u32[]{:S(2)}) collective-permute-start(f32[]{:T(128)} %add.18), channel_id=1, source_target_pairs={{0,16},{4,20},{8,24},{12,28},{16,0},{20,4},{24,8},{28,12},{1,17},{... | collective-permute-start | bytes 20 | tf_op jit(solution)/shard_map/ppermute | solution.py:272
  128.7 1.3 collective-permute-start.19
  130.0 1.3 collective-permute-start.21
  131.3 27.9 %collective-permute-start.25 = (f32[]{:T(128)}, f32[]{:T(128)}, u32[]{:S(2)}, u32[]{:S(2)}) collective-permute-start(f32[]{:T(128)} %add.19), channel_id=1, source_target_pairs={{0,1},{1,0},{2,3},{3,2},{4,5},{5,4},{6,7},{7,6},{8,9},{9,8},{10,11... | collective-permute-start | bytes 20 | tf_op jit(solution)/shard_map/ppermute | solution.py:384
  160.1 4.7 %collective-permute-start.26 = (f32[]{:T(128)}, f32[]{:T(128)}, u32[]{:S(2)}, u32[]{:S(2)}) collective-permute-start(f32[]{:T(128)} %add.20), channel_id=1, source_target_pairs={{0,2},{1,3},{2,0},{3,1},{4,6},{5,7},{6,4},{7,5},{8,10},{9,11},{10,... | collective-permute-start | bytes 20 | tf_op jit(solution)/shard_map/ppermute | solution.py:384
  168.4 1.3 collective-permute-start.23
  171.0 8.1 %shard_map.43.local_square = bf16[512,1024]{1,0:T(8,128)(2,1)S(1)} custom-call(s32[2]{0:T(128)S(1)} %pad_add_fusion.where, bf16[3,528,1024]{2,1,0:T(8,128)(2,1)} %get-tuple-element.19.panel, bf16[3,528,1024]{2,1,0:T(8,128)(2,1)} %collective-permute-done.12.other, bf16[528,1024]{1,0:T(8,128)(2,1)} %get-tuple-element.20.far, ...), custom_call_target="tpu_custom_call" | custom-call | flops 4294967296 | bytes 9437184 | tf_op jit(solution)/shard_map/pallas_call | solution.py:260
  179.2 2.7 %shard_map.44.acc_in = f32[512,1024]{1,0:T(8,128)S(1)} custom-call(s32[2]{0:T(128)S(1)} %pad_add_fusion.where, bf16[512,1024]{1,0:T(8,128)(2,1)S(1)} %get-tuple-element.18.squared, bf16[512,1024]{1,0:T(8,128)(2,1)S(1)} %shard_map.43.local_square, bf16[8,512,1024]{2,1,0:T(8,128)(2,1)S(1)} %copy-done.1), custom_call_target="tpu_custom_call" | custom-call | flops 2147483648 | bytes 8388608 | tf_op jit(solution)/shard_map/pallas_call | solution.py:260
  181.9 23.8 %collective-permute-done.22.refs_3_ = bf16[512,512]{1,0:T(8,128)(2,1)S(1)} collective-permute-done((bf16[512,512]{1,0:T(8,128)(2,1)}, bf16[512,512]{1,0:T(8,128)(2,1)S(1)}, u32[]{:S(2)}, u32[]{:S(2)}) %collective-permute-start.22) | collective-permute-done | bytes 524320 | tf_op jit(solution)/shard_map/ppermute | solution.py:301
  205.6 10.1 %shard_map.46 = f32[512,1024]{1,0:T(8,128)} custom-call(s32[2]{0:T(128)S(1)} %pad_add_fusion.where, s32[4,8]{1,0:T(4,128)S(1)} %copy-done.4, bf16[512,1024]{1,0:T(8,128)(2,1)S(1)} %get-tuple-element.18.squared, f32[512,1024]{1,0:T(8,128)S(1)} %shard_map.44.acc_in, bf16[512,1024]{1,0:T(8,128)(2,1)S(1)} %collective-permute-done.14.turn1, ...), custom_call_target="tpu_custom_call" | custom-call | flops 3221225472 | bytes 16777216 | tf_op jit(solution)/shard_map/pallas_call | solution.py:260
  (60 shorter events, 18.0 us)
Async XLA Ops:
  2.6 26.3 %collective-permute-start.5 = (bf16[512,1024]{1,0:T(8,128)(2,1)S(1)}, bf16[512,1024]{1,0:T(8,128)(2,1)}, u32[]{:S(2)}, u32[]{:S(2)}) collective-permute-start(bf16[512,1024]{1,0:T(8,128)(2,1)S(1)} %fusion.1.refs_0_), channel_id=1, source_target_pairs={{0,8},{4,12},{8,0},{12,4},{16,24},{20,28},{24,16},{28,20},{1,9},{5... | collective-permute-start | bytes 3145736 | tf_op jit(solution)/shard_map/ppermute | solution.py:272
  5.8 25.5 %collective-permute-start = (bf16[528,1024]{1,0:T(8,128)(2,1)S(1)}, bf16[528,1024]{1,0:T(8,128)(2,1)}, u32[]{:S(2)}, u32[]{:S(2)}) collective-permute-start(bf16[528,1024]{1,0:T(8,128)(2,1)S(1)} %fusion.2.own), channel_id=1, source_target_pairs={{0,1},{1,0},{2,3},{3,2},{4,5},{5,4},{6,7},{7,6},{8,9},{9,8},{10,11... | collective-permute-start | bytes 3244040 | tf_op jit(solution)/shard_map/ppermute | solution.py:312
  7.4 25.5 %collective-permute-start.2 = (bf16[528,1024]{1,0:T(8,128)(2,1)S(1)}, bf16[528,1024]{1,0:T(8,128)(2,1)S(1)}, u32[]{:S(2)}, u32[]{:S(2)}) collective-permute-start(bf16[528,1024]{1,0:T(8,128)(2,1)S(1)} %fusion.2.own), channel_id=1, source_target_pairs={{1,2},{2,1},{5,6},{6,5},{9,10},{10,9},{13,14},{14,13},{17,18},{18,... | collective-permute-start | bytes 3244040 | tf_op jit(solution)/shard_map/ppermute | solution.py:313
  8.2 26.1 %collective-permute-start.7 = (bf16[512,1024]{1,0:T(8,128)(2,1)S(1)}, bf16[512,1024]{1,0:T(8,128)(2,1)}, u32[]{:S(2)}, u32[]{:S(2)}) collective-permute-start(bf16[512,1024]{1,0:T(8,128)(2,1)S(1)} %fusion.1.refs_0_), channel_id=1, source_target_pairs={{0,16},{4,20},{8,24},{12,28},{16,0},{20,4},{24,8},{28,12},{1,17},{... | collective-permute-start | bytes 3145736 | tf_op jit(solution)/shard_map/ppermute | solution.py:272
  9.7 24.6 %collective-permute-start.4 = (bf16[512,1024]{1,0:T(8,128)(2,1)S(1)}, bf16[512,1024]{1,0:T(8,128)(2,1)S(1)}, u32[]{:S(2)}, u32[]{:S(2)}) collective-permute-start(bf16[512,1024]{1,0:T(8,128)(2,1)S(1)} %fusion.1.refs_0_), channel_id=1, source_target_pairs={{0,4},{4,0},{8,12},{12,8},{16,20},{20,16},{24,28},{28,24},{1,5},{5... | collective-permute-start | bytes 3145736 | tf_op jit(solution)/shard_map/ppermute | solution.py:272
  28.9 26.3 %collective-permute-start.9 = (bf16[512,1024]{1,0:T(8,128)(2,1)}, bf16[512,1024]{1,0:T(8,128)(2,1)}, u32[]{:S(2)}, u32[]{:S(2)}) collective-permute-start(bf16[512,1024]{1,0:T(8,128)(2,1)} %collective-permute-done.5.refs_2_), channel_id=1, source_target_pairs={{0,16},{4,20},{8,24},{12,28},{16,0},{20,4},{24,8},{28,12},{1,17},{... | collective-permute-start | bytes 3145736 | tf_op jit(solution)/shard_map/ppermute | solution.py:272
  31.3 23.9 %collective-permute-start.1 = (bf16[528,1024]{1,0:T(8,128)(2,1)}, bf16[528,1024]{1,0:T(8,128)(2,1)}, u32[]{:S(2)}, u32[]{:S(2)}) collective-permute-start(bf16[528,1024]{1,0:T(8,128)(2,1)} %collective-permute-done.pair), channel_id=1, source_target_pairs={{1,2},{2,1},{5,6},{6,5},{9,10},{10,9},{13,14},{14,13},{17,18},{18,... | collective-permute-start | bytes 3244040 | tf_op jit(solution)/shard_map/ppermute | solution.py:315
  33.0 27.2 %collective-permute-start.3 = (bf16[528,1024]{1,0:T(8,128)(2,1)S(1)}, bf16[528,1024]{1,0:T(8,128)(2,1)}, u32[]{:S(2)}, u32[]{:S(2)}) collective-permute-start(bf16[528,1024]{1,0:T(8,128)(2,1)S(1)} %collective-permute-done.2.middle1), channel_id=1, source_target_pairs={{2,3},{1,0},{6,7},{5,4},{10,11},{9,8},{14,15},{13,12},{18,19},{17,... | collective-permute-start | bytes 3244040 | tf_op jit(solution)/shard_map/ppermute | solution.py:314
  34.3 20.9 %collective-permute-start.6 = (bf16[512,1024]{1,0:T(8,128)(2,1)}, bf16[512,1024]{1,0:T(8,128)(2,1)}, u32[]{:S(2)}, u32[]{:S(2)}) collective-permute-start(bf16[512,1024]{1,0:T(8,128)(2,1)} %collective-permute-done.5.refs_2_), channel_id=1, source_target_pairs={{0,4},{4,0},{8,12},{12,8},{16,20},{20,16},{24,28},{28,24},{1,5},{5... | collective-permute-start | bytes 3145736 | tf_op jit(solution)/shard_map/ppermute | solution.py:272
  35.3 19.9 %collective-permute-start.8 = (bf16[512,1024]{1,0:T(8,128)(2,1)}, bf16[512,1024]{1,0:T(8,128)(2,1)}, u32[]{:S(2)}, u32[]{:S(2)}) collective-permute-start(bf16[512,1024]{1,0:T(8,128)(2,1)} %collective-permute-done.7.refs_4_), channel_id=1, source_target_pairs={{0,4},{4,0},{8,12},{12,8},{16,20},{20,16},{24,28},{28,24},{1,5},{5... | collective-permute-start | bytes 3145736 | tf_op jit(solution)/shard_map/ppermute | solution.py:272
  69.7 100.0 %collective-permute-start.12 = (bf16[3,528,1024]{2,1,0:T(8,128)(2,1)}, bf16[3,528,1024]{2,1,0:T(8,128)(2,1)}, u32[]{:S(2)}, u32[]{:S(2)}) collective-permute-start(bf16[3,528,1024]{2,1,0:T(8,128)(2,1)} %get-tuple-element.19.panel), channel_id=1, source_target_pairs={{0,4},{4,0},{8,12},{12,8},{16,20},{20,16},{24,28},{28,24},{1,5},{5... | collective-permute-start | bytes 9732104 | tf_op jit(solution)/shard_map/ppermute | solution.py:272
  69.8 29.8 %collective-permute-start.11 = (bf16[528,1024]{1,0:T(8,128)(2,1)}, bf16[528,1024]{1,0:T(8,128)(2,1)S(1)}, u32[]{:S(2)}, u32[]{:S(2)}) collective-permute-start(bf16[528,1024]{1,0:T(8,128)(2,1)} %collective-permute-done.1.middle2), channel_id=1, source_target_pairs={{2,3},{1,0},{6,7},{5,4},{10,11},{9,8},{14,15},{13,12},{18,19},{17,... | collective-permute-start | bytes 3244040 | tf_op jit(solution)/shard_map/ppermute | solution.py:316
  104.7 63.7 %collective-permute-start.13 = (bf16[528,1024]{1,0:T(8,128)(2,1)}, bf16[528,1024]{1,0:T(8,128)(2,1)}, u32[]{:S(2)}, u32[]{:S(2)}) collective-permute-start(bf16[528,1024]{1,0:T(8,128)(2,1)} %get-tuple-element.20.far), channel_id=1, source_target_pairs={{0,4},{4,0},{8,12},{12,8},{16,20},{20,16},{24,28},{28,24},{1,5},{5... | collective-permute-start | bytes 3244040 | tf_op jit(solution)/shard_map/ppermute | solution.py:272
  104.8 25.2 %collective-permute-start.14 = (bf16[512,1024]{1,0:T(8,128)(2,1)S(1)}, bf16[512,1024]{1,0:T(8,128)(2,1)S(1)}, u32[]{:S(2)}, u32[]{:S(2)}) collective-permute-start(bf16[512,1024]{1,0:T(8,128)(2,1)S(1)} %get-tuple-element.18.squared), channel_id=1, source_target_pairs={{1,2},{2,3},{3,1},{5,6},{6,7},{7,5},{8,10},{10,11},{11,8},{12,14},... | collective-permute-start | bytes 3145736 | tf_op jit(solution)/shard_map/ppermute | solution.py:291
  105.5 25.8 %collective-permute-start.15 = (bf16[512,1024]{1,0:T(8,128)(2,1)S(1)}, bf16[512,1024]{1,0:T(8,128)(2,1)S(1)}, u32[]{:S(2)}, u32[]{:S(2)}) collective-permute-start(bf16[512,1024]{1,0:T(8,128)(2,1)S(1)} %get-tuple-element.18.squared), channel_id=1, source_target_pairs={{1,3},{2,1},{3,2},{5,7},{6,5},{7,6},{8,11},{10,8},{11,10},{12,15},... | collective-permute-start | bytes 3145736 | tf_op jit(solution)/shard_map/ppermute | solution.py:291
  113.2 9.0 %collective-permute-start.17 = (f32[]{:T(128)}, f32[]{:T(128)}, u32[]{:S(2)}, u32[]{:S(2)}) collective-permute-start(f32[]{:T(128)} %add.17), channel_id=1, source_target_pairs={{0,8},{4,12},{8,0},{12,4},{16,24},{20,28},{24,16},{28,20},{1,9},{5... | collective-permute-start | bytes 20 | tf_op jit(solution)/shard_map/ppermute | solution.py:272
  122.8 5.3 %collective-permute-start.18 = (f32[]{:T(128)}, f32[]{:T(128)}, u32[]{:S(2)}, u32[]{:S(2)}) collective-permute-start(f32[]{:T(128)} %add.18), channel_id=1, source_target_pairs={{0,16},{4,20},{8,24},{12,28},{16,0},{20,4},{24,8},{28,12},{1,17},{... | collective-permute-start | bytes 20 | tf_op jit(solution)/shard_map/ppermute | solution.py:272
  128.7 38.4 %collective-permute-start.19 = (bf16[512,512]{1,0:T(8,128)(2,1)}, bf16[512,512]{1,0:T(8,128)(2,1)}, u32[]{:S(2)}, u32[]{:S(2)}) collective-permute-start(bf16[512,512]{1,0:T(8,128)(2,1)} %copy-done.6), channel_id=1, source_target_pairs={{8,0},{12,4},{1,9},{5,13},{26,18},{30,22},{19,27},{23,31}} | collective-permute-start | bytes 1572872 | tf_op jit(solution)/shard_map/ppermute | solution.py:301
  130.0 51.8 %collective-permute-start.21 = (bf16[512,512]{1,0:T(8,128)(2,1)}, bf16[512,512]{1,0:T(8,128)(2,1)}, u32[]{:S(2)}, u32[]{:S(2)}) collective-permute-start(bf16[512,512]{1,0:T(8,128)(2,1)} %copy-done.6), channel_id=1, source_target_pairs={{16,0},{20,4},{25,9},{29,13},{2,18},{6,22},{11,27},{15,31}} | collective-permute-start | bytes 1572872 | tf_op jit(solution)/shard_map/ppermute | solution.py:301
  131.3 28.1 %collective-permute-start.25 = (f32[]{:T(128)}, f32[]{:T(128)}, u32[]{:S(2)}, u32[]{:S(2)}) collective-permute-start(f32[]{:T(128)} %add.19), channel_id=1, source_target_pairs={{0,1},{1,0},{2,3},{3,2},{4,5},{5,4},{6,7},{7,6},{8,9},{9,8},{10,11... | collective-permute-start | bytes 20 | tf_op jit(solution)/shard_map/ppermute | solution.py:384
  165.1 16.7 %collective-permute-start.20 = (bf16[512,512]{1,0:T(8,128)(2,1)}, bf16[512,512]{1,0:T(8,128)(2,1)}, u32[]{:S(2)}, u32[]{:S(2)}) collective-permute-start(bf16[512,512]{1,0:T(8,128)(2,1)} %copy-done.5), channel_id=1, source_target_pairs={{8,4},{12,0},{1,13},{5,9},{26,22},{30,18},{19,31},{23,27}} | collective-permute-start | bytes 1572872 | tf_op jit(solution)/shard_map/ppermute | solution.py:301
  167.1 38.5 %collective-permute-start.22 = (bf16[512,512]{1,0:T(8,128)(2,1)}, bf16[512,512]{1,0:T(8,128)(2,1)S(1)}, u32[]{:S(2)}, u32[]{:S(2)}) collective-permute-start(bf16[512,512]{1,0:T(8,128)(2,1)} %copy-done.5), channel_id=1, source_target_pairs={{16,4},{20,0},{25,13},{29,9},{2,22},{6,18},{11,31},{15,27}} | collective-permute-start | bytes 1572872 | tf_op jit(solution)/shard_map/ppermute | solution.py:301
  168.4 37.2 %collective-permute-start.23 = (bf16[512,512]{1,0:T(8,128)(2,1)}, bf16[512,512]{1,0:T(8,128)(2,1)S(1)}, u32[]{:S(2)}, u32[]{:S(2)}) collective-permute-start(bf16[512,512]{1,0:T(8,128)(2,1)} %copy-done.6), channel_id=1, source_target_pairs={{24,0},{28,4},{17,9},{21,13},{10,18},{14,22},{3,27},{7,31}} | collective-permute-start | bytes 1572872 | tf_op jit(solution)/shard_map/ppermute | solution.py:301
  169.7 35.9 %collective-permute-start.24 = (bf16[512,512]{1,0:T(8,128)(2,1)}, bf16[512,512]{1,0:T(8,128)(2,1)S(1)}, u32[]{:S(2)}, u32[]{:S(2)}) collective-permute-start(bf16[512,512]{1,0:T(8,128)(2,1)} %copy-done.5), channel_id=1, source_target_pairs={{24,4},{28,0},{17,13},{21,9},{10,22},{14,18},{3,31},{7,27}} | collective-permute-start | bytes 1572872 | tf_op jit(solution)/shard_map/ppermute | solution.py:301
  (11 other events, 104.3 us)
where the time goes:
time: 217 us
  waiting for transfers between devices  98.6 us (45%)
  starting transfers between devices  69.6 us (32%)
  Pallas kernels  36.1 us (17%)
  between operations  6.01 us (3%)
  local copies, waits for them, and re-layouts  4.35 us (2%)
  other arithmetic  2.24 us (1%)
    ppermute x12, waiting for transfers between devices, swap(): return lax.ppermute(x, 'row', [(i, i ^ k) for i in range(8)])  40.3 us
    pallas_call x6, Pallas kernels, call(): pl.pallas_call(kernel, out_shape=outs, in_specs=specs, out_specs=jax.tree...  36.1 us
    ppermute x2, starting transfers between devices, local(): total = total + lax.ppermute(total, 'col', [(i, i ^ k) for i in range(4)])  32.7 us
    ppermute x1, waiting for transfers between devices, local(): outer3 = lax.ppermute(middle2, 'col', [(2, 3), (1, 0)])  28.5 us
    ppermute x6, waiting for transfers between devices, to_corner(): return lax.ppermute(x, ('row', 'col'), pairs)  23.8 us
    ppermute x12, starting transfers between devices, swap(): return lax.ppermute(x, 'row', [(i, i ^ k) for i in range(8)])  21.1 us
    ppermute x6, starting transfers between devices, to_corner(): return lax.ppermute(x, ('row', 'col'), pairs)  7.74 us
    ppermute x1, waiting for transfers between devices, local(): outer2 = lax.ppermute(middle1, 'col', [(2, 3), (1, 0)])  4.95 us
  transfers between devices with their start and end apart: 27, of which 11 were waited for; matrix products, arithmetic and copies ran while one was open for 0% of the time, Pallas kernels for 8%

commit v1 on v0

--- a/solution.py
+++ b/solution.py
@@ -74,7 +74,7 @@
 
 def square_early_kernel(where, own, pair, middle2, outer2, *refs):
     rights = refs[:8]
-    acc, panel, right, left_sem, right_sem = refs[8:]
+    acc, panel, right, ahead, left_sem, right_sem, ahead_sem = refs[8:]
     row, col = where[0], where[1]
     pltpu.make_async_copy(own, panel.at[0], left_sem.at[0]).start()
     pltpu.make_async_copy(pair, panel.at[1], left_sem.at[1]).start()
@@ -91,6 +91,12 @@
     for k in range(8):
         slot = row ^ k
         pltpu.make_async_copy(rights[k], right.at[slot], right_sem.at[slot]).start()
+    slot = 2 * (col ^ 3)
+    for t in range(2):
+        there = right.at[slot + t]
+        pltpu.make_async_copy(there, there, right_sem.at[slot + t]).wait()
+    hand_over = pltpu.make_async_copy(right.at[pl.ds(slot, 2)], ahead, ahead_sem)
+    hand_over.start()
     for d in range(3):
         slot = 2 * (col ^ d)
         pltpu.make_async_copy(panel.at[d], panel.at[d], left_sem.at[d]).wait()
@@ -98,16 +104,20 @@
             there = right.at[slot + t]
             pltpu.make_async_copy(there, there, right_sem.at[slot + t]).wait()
         multiply(acc, panel.at[d], right.at[pl.ds(slot, 2)], d == 0)
-    slot = 2 * (col ^ 3)
-    for t in range(2):
-        there = right.at[slot + t]
-        pltpu.make_async_copy(there, there, right_sem.at[slot + t]).wait()
-
-
-def square_late_kernel(where, pattern, own, acc_in, middle1, outer3, right_all, *refs):
-    squared_ref, sum_ref, far, right, acc, left_sem, right_sem = refs
+    hand_over.wait()
+
+
+def piece(left, right, lanes):
+    rows = right.shape[1]
+    return jnp.dot(
+        left[:rows, :rows], right[0, :, lanes], preferred_element_type=jnp.float32
+    ) + jnp.dot(left[:rows, rows:], right[1, :, lanes], preferred_element_type=jnp.float32)
+
+
+def square_late_kernel(where, own, acc_in, right, middle1, outer3, *refs):
+    squared_ref, sum_ref, far, left_sem = refs
     row, col = where[0], where[1]
-    rows, columns = acc.shape
+    rows, columns = squared_ref.shape
     inner = (col == 1) | (col == 2)
 
     @pl.when(inner)
@@ -118,28 +128,32 @@
     def _():
         pltpu.make_async_copy(outer3, far, left_sem).start()
 
-    fetch = pltpu.make_async_copy(right_all.at[pl.ds(2 * (col ^ 3), 2)], right, right_sem)
-    fetch.start()
     pltpu.make_async_copy(far, far, left_sem).wait()
-    fetch.wait()
-    multiply(acc, far, right, True)
-    sum_ref[...] = jnp.zeros_like(sum_ref)
-
-    def body(a, b, part):
-        kept = pattern[a, b].astype(jnp.float32)
-        squared = ((acc_in[part] + acc[part]) * kept).astype(jnp.bfloat16)
-        squared_ref[part] = squared
-        wide = squared.astype(jnp.float32)
-        masked = own[part].astype(jnp.float32)
-        offset = row * rows + a * B - (col * columns + b * B)
-        diagonal = (
-            lax.broadcasted_iota(jnp.int32, (B, B), 0) + offset
-            == lax.broadcasted_iota(jnp.int32, (B, B), 1)
+    sums = jnp.zeros((8, TILE), jnp.float32)
+    for n in range(columns // TILE):
+        lanes = slice(n * TILE, (n + 1) * TILE)
+        total = acc_in[:, lanes] + piece(far, right, lanes)
+        kept = own[rows : rows + EXTRA, lanes].astype(jnp.float32)
+        for a in range(rows // B):
+            part = slice(a * B, (a + 1) * B)
+            squared = (total[part] * kept[a : a + 1]).astype(jnp.bfloat16)
+            squared_ref[part, lanes] = squared
+            term = squared.astype(jnp.float32) * own[part, lanes].astype(jnp.float32)
+            sums -= 2.0 * jnp.sum(term.reshape(B // 8, 8, TILE), axis=0)
+    sum_ref[...] = sums[:, :B]
+    for n in range(1, TILE // B):
+        sum_ref[...] += sums[:, n * B : (n + 1) * B]
+
+    @pl.when(row // 2 == col)
+    def _():
+        same = lax.broadcasted_iota(jnp.int32, (B, B), 0) == lax.broadcasted_iota(
+            jnp.int32, (B, B), 1
         )
-        term = jnp.where(diagonal, 3.0 * wide, 0.0) - 2.0 * wide * masked
-        sum_ref[...] += jnp.sum(term.reshape(B // 8, 8, B), axis=0)
-
-    blocks(rows, columns, body)
+        for a in range(rows // B):
+            lanes = pl.ds(pl.multiple_of(row * rows - col * columns + a * B, B), B)
+            squared = squared_ref[a * B : (a + 1) * B, lanes].astype(jnp.float32)
+            term = jnp.where(same, 3.0 * squared, 0.0)
+            sum_ref[...] += jnp.sum(term.reshape(B // 8, 8, B), axis=0)
 
 
 def turn_kernel(where, squared, same_ref, cross_ref):
@@ -178,6 +192,17 @@
             ).astype(jnp.bfloat16)
 
 
+def late_sources(row, col):
+    chip = row // 2
+    place = col - (col > chip).astype(jnp.int32)
+    sources = []
+    for i in range(3):
+        index = (place + 2 - i) % 3
+        other = index + (index >= chip).astype(jnp.int32)
+        sources.append(jnp.where(chip == col, col ^ (i + 1), other))
+    return sources
+
+
 def cubic_early_kernel(where, squared, local_square, right_all, acc, right, sem):
     row, col = where[0], where[1]
     chip = row // 2
@@ -186,84 +211,75 @@
     first.start()
     second.start()
     first.wait()
+    multiply(acc, squared, right.at[0], True)
     second.wait()
-    multiply(acc, squared, right.at[0], True)
 
     @pl.when(chip != col)
     def _():
         multiply(acc, local_square, right.at[1], False)
 
 
-def cubic_late_kernel(where, pattern, squared, acc_in, turn1, turn2, *refs):
-    sides, right_all, purified_ref = refs[:6], refs[6], refs[7]
-    left, right, acc, left_sem, right_sem = refs[8:]
+def cubic_late_kernel(where, own, squared, acc_in, turn1, turn2, *refs):
+    sides, right_all, purified_ref, left, right, sem, right_sem = (
+        refs[:6],
+        *refs[6:],
+    )
     row, col = where[0], where[1]
     core, chip = row % 2, row // 2
-    rows, columns = acc.shape
+    rows, columns = squared.shape
     corner = chip == col
-    place = col - (col > chip).astype(jnp.int32)
-    sources = []
-    for i in range(3):
-        index = (place + 2 - i) % 3
-        source = jnp.where(corner, col ^ (i + 1), index + (index >= chip).astype(jnp.int32))
-        sources.append(source)
-
-    def fetch(i):
-        return pltpu.make_async_copy(
-            right_all.at[pl.ds(2 * sources[i], 2)], right.at[i], right_sem.at[i]
-        )
-
-    fetch(0).start()
-    fetch(1).start()
+    fetches = [
+        pltpu.make_async_copy(right_all.at[pl.ds(2 * source, 2)], right.at[i], right_sem.at[i])
+        for i, source in enumerate(late_sources(row, col))
+    ]
+    for fetch in fetches:
+        fetch.start()
+
+    def finish(lefts):
+        for n in range(columns // TILE):
+            lanes = slice(n * TILE, (n + 1) * TILE)
+            total = acc_in[:, lanes]
+            for i, ref in enumerate(lefts):
+                if n == 0:
+                    fetches[i].wait()
+                total = total + piece(ref, right.at[i], lanes)
+            kept = own[rows : rows + EXTRA, lanes].astype(jnp.float32)
+            for a in range(rows // B):
+                part = slice(a * B, (a + 1) * B)
+                wide = squared[part, lanes].astype(jnp.float32)
+                purified_ref[part, lanes] = 3.0 * wide - 2.0 * (total[part] * kept[a : a + 1])
 
     @pl.when(jnp.logical_not(corner))
     def _():
-        pltpu.make_async_copy(turn1, left.at[0], left_sem.at[0]).start()
-        pltpu.make_async_copy(turn2, left.at[1], left_sem.at[1]).start()
+        finish([turn1, turn2])
+        fetches[2].wait()
 
     @pl.when(corner)
     def _():
         for i in range(3):
             for u in range(2):
                 lanes = pl.ds(pl.multiple_of((core ^ u) * rows, rows), rows)
-                pltpu.make_async_copy(
-                    sides[2 * i + u], left.at[i, :, lanes], left_sem.at[i]
-                ).start()
-        fetch(2).start()
-
-    for i in range(2):
-        pltpu.make_async_copy(left.at[i], left.at[i], left_sem.at[i]).wait()
-        fetch(i).wait()
-        multiply(acc, left.at[i], right.at[i], i == 0)
-
-    @pl.when(corner)
-    def _():
-        pltpu.make_async_copy(left.at[2], left.at[2], left_sem.at[2]).wait()
-        fetch(2).wait()
-        multiply(acc, left.at[2], right.at[2], False)
-
-    def body(a, b, part):
-        kept = pattern[a, b].astype(jnp.float32)
-        wide = squared[part].astype(jnp.float32)
-        purified_ref[part] = 3.0 * wide - 2.0 * ((acc_in[part] + acc[part]) * kept)
-
-    blocks(rows, columns, body)
+                pltpu.make_async_copy(sides[2 * i + u], left.at[i, :, lanes], sem.at[i]).start()
+        for i in range(3):
+            pltpu.make_async_copy(left.at[i], left.at[i], sem.at[i]).wait()
+        finish([left.at[i] for i in range(3)])
 
 
 ANYWHERE = pl.BlockSpec(memory_space=pl.ANY)
+AWAY = pl.BlockSpec(memory_space=pltpu.HBM)
 SCALARS = pl.BlockSpec(memory_space=pltpu.SMEM)
 WHOLE = pl.BlockSpec(memory_space=pltpu.VMEM)
 DMA = pltpu.SemaphoreType.DMA
 
 
-def call(kernel, specs, args, outs, scratch, flops, moved):
+def call(kernel, specs, args, outs, scratch, flops, moved, grant=24):
     return pl.pallas_call(
         kernel,
         out_shape=outs,
         in_specs=specs,
         out_specs=jax.tree.map(lambda _: WHOLE, outs),
         scratch_shapes=scratch,
-        compiler_params=pltpu.CompilerParams(vmem_limit_bytes=24 << 20),
+        compiler_params=pltpu.CompilerParams(vmem_limit_bytes=grant << 20),
         cost_estimate=pl.CostEstimate(flops=flops, bytes_accessed=moved, transcendentals=0),
     )(*args)
 
@@ -322,7 +338,7 @@
     wide = jax.ShapeDtypeStruct((rows, columns), jnp.float32)
     extended = jax.ShapeDtypeStruct((rows + EXTRA, columns), jnp.bfloat16)
     acc = pltpu.VMEM((rows, columns), jnp.float32)
-    partial, panel, right = call(
+    partial, panel, right, ahead = call(
         square_early_kernel,
         [SCALARS] + [ANYWHERE] * 12,
         (where, own, pair, middle2, outer2, *rights),
@@ -330,18 +346,19 @@
             wide,
             jax.ShapeDtypeStruct((3, rows + EXTRA, columns), jnp.bfloat16),
             jax.ShapeDtypeStruct((8, rows, columns), jnp.bfloat16),
+            jax.ShapeDtypeStruct((2, rows, columns), jnp.bfloat16),
         ),
-        [DMA((3,)), DMA((8,))],
+        [DMA((3,)), DMA((8,)), DMA(())],
         3 * flops,
         24 * size,
     )
     other = swap(panel, 1)
     squared, sums, far = call(
         square_late_kernel,
-        [SCALARS, SCALARS, WHOLE, WHOLE] + [ANYWHERE] * 3,
-        (where, pattern, own, partial, middle1, outer3, right),
+        [SCALARS, WHOLE, WHOLE, WHOLE] + [ANYWHERE] * 2,
+        (where, own, partial, ahead, middle1, outer3),
         (tile, jax.ShapeDtypeStruct((8, B), jnp.float32), extended),
-        [pltpu.VMEM((2, rows, columns), jnp.bfloat16), acc, DMA(()), DMA(())],
+        [DMA(())],
         flops,
         8 * size,
     )
@@ -359,8 +376,7 @@
         0,
         2 * size,
     )
-    same, cross, total = lax.optimization_barrier((*turned, total))
-    sides = [to_corner((same, cross)[u], j, u) for j in (1, 2, 3) for u in (0, 1)]
+    sides = [to_corner(turned[u], j, u) for j in (1, 2, 3) for u in (0, 1)]
     local_square = call(
         own_square_kernel,
         [SCALARS] + [WHOLE] * 4,
@@ -369,33 +385,34 @@
         [],
         4 * flops,
         9 * size,
+        48,
     )
     cubic = call(
         cubic_early_kernel,
-        [SCALARS, WHOLE, WHOLE, ANYWHERE],
+        [SCALARS, WHOLE, WHOLE, AWAY],
         (where, squared, local_square, right),
         wide,
         [pltpu.VMEM((2, 2, rows, columns), jnp.bfloat16), DMA((2,))],
         2 * flops,
         8 * size,
-    )
-    turns[0], turns[1], total = lax.optimization_barrier((*turns, total))
-    for k in (1, 2):
+        48,
+    )
+    for k in (2, 1):
         total = total + lax.ppermute(total, "col", [(i, i ^ k) for i in range(4)])
     purified = call(
         cubic_late_kernel,
-        [SCALARS, SCALARS, WHOLE, WHOLE] + [ANYWHERE] * 9,
-        (where, pattern, squared, cubic, *turns, *sides, right),
+        [SCALARS] + [WHOLE] * 5 + [ANYWHERE] * 6 + [AWAY],
+        (where, own, squared, cubic, *turns, *sides, right),
         wide,
         [
             pltpu.VMEM((3, rows, columns), jnp.bfloat16),
             pltpu.VMEM((3, 2, rows, columns), jnp.bfloat16),
-            acc,
             DMA((3,)),
             DMA((3,)),
         ],
         3 * flops,
         16 * size,
+        48,
     )
     return (purified, total / (rows * lax.axis_size("row")))
 

time: 217 us -> 213 us (0.982)
  starting transfers between devices: 69.6 us -> 34.1 us
  waiting for transfers between devices: 98.6 us -> 122 us
  Pallas kernels: 36.1 us -> 40.4 us
  local copies, waits for them, and re-layouts: 4.35 us -> 7.36 us
    ppermute x2, starting transfers between devices: 32.7 us -> 3.74 us  [local(): total = total + lax.ppermute(total, 'col', [(i, i ^ k) for i in range(4)])]
    ppermute x12, waiting for transfers between devices: 40.3 us -> 59.8 us  [swap(): return lax.ppermute(x, 'row', [(i, i ^ k) for i in range(8)])]
    ppermute x12, starting transfers between devices: 21.1 us -> 12.7 us  [swap(): return lax.ppermute(x, 'row', [(i, i ^ k) for i in range(8)])]
    pallas_call x6, Pallas kernels: 36.1 us -> 40.4 us  [call(): pl.pallas_call(kernel, out_shape=outs, in_specs=specs, out_specs=jax.tree...]
    ppermute x2, waiting for transfers between devices: 0.41 us -> 4.48 us  [local(): total = total + lax.ppermute(total, 'col', [(i, i ^ k) for i in range(4)])]
    unnamed x18 -> x14, local copies, waits for them, and re-layouts: 4.15 us -> 7.16 us
    ppermute x6, waiting for transfers between devices: 23.8 us -> 26 us  [to_corner(): return lax.ppermute(x, ('row', 'col'), pairs)]
  transfers between devices with their start and end apart: 27 -> 27, of which waited for: 11 -> 13; matrix products, arithmetic and copies ran while one was open for 0% -> 0% of each run, Pallas kernels for 8% -> 8%
where the time goes in v1:
time: 213 us; the launch traced here: 212 us
  waiting for transfers between devices  122 us (57%)
  Pallas kernels  40.4 us (19%)
  starting transfers between devices  34.1 us (16%)
  local copies, waits for them, and re-layouts  7.36 us (3%)
  between operations  5.9 us (3%)
  other arithmetic  2.27 us (1%)
    ppermute x12, waiting for transfers between devices, swap(): return lax.ppermute(x, 'row', [(i, i ^ k) for i in range(8)])  59.8 us
    pallas_call x6, Pallas kernels, call(): pl.pallas_call(kernel, out_shape=outs, in_specs=specs, out_specs=jax.tree...  40.4 us
    ppermute x1, waiting for transfers between devices, local(): outer3 = lax.ppermute(middle2, 'col', [(2, 3), (1, 0)])  27.1 us
    ppermute x6, waiting for transfers between devices, to_corner(): return lax.ppermute(x, ('row', 'col'), pairs)  26 us
    ppermute x12, starting transfers between devices, swap(): return lax.ppermute(x, 'row', [(i, i ^ k) for i in range(8)])  12.7 us
    ppermute x6, starting transfers between devices, to_corner(): return lax.ppermute(x, ('row', 'col'), pairs)  7.72 us
    unnamed x14, local copies, waits for them, and re-layouts  7.16 us
    ppermute x2, waiting for transfers between devices, local(): total = total + lax.ppermute(total, 'col', [(i, i ^ k) for i in range(4)])  4.48 us
  transfers between devices with their start and end apart: 27, of which 13 were waited for; matrix products, arithmetic and copies ran while one was open for 0% of the time, Pallas kernels for 8%

profile of v1, /device:TPU:0, one launch (start us, length us, event | category | flops | bytes accessed | tf_op | source)
XLA Modules:
  0.0 212.3 jit_solution(6354136212093757733)
XLA Ops:
  2.6 3.0 %collective-permute-start.5 = (bf16[512,1024]{1,0:T(8,128)(2,1)S(1)}, bf16[512,1024]{1,0:T(8,128)(2,1)}, u32[]{:S(2)}, u32[]{:S(2)}) collective-permute-start(bf16[512,1024]{1,0:T(8,128)(2,1)S(1)} %fusion.1.refs_0_), channel_id=1, source_target_pairs={{0,8},{4,12},{8,0},{12,4},{16,24},{20,28},{24,16},{28,20},{1,9},{5... | collective-permute-start | bytes 3145736 | tf_op jit(solution)/shard_map/ppermute | solution.py:288
  7.5 1.6 collective-permute-start.2
  10.6 18.3 %collective-permute-done.5.refs_2_ = bf16[512,1024]{1,0:T(8,128)(2,1)} collective-permute-done((bf16[512,1024]{1,0:T(8,128)(2,1)S(1)}, bf16[512,1024]{1,0:T(8,128)(2,1)}, u32[]{:S(2)}, u32[]{:S(2)}) %collective-permute-start.5) | collective-permute-done | bytes 1048608 | tf_op jit(solution)/shard_map/ppermute | solution.py:288
  28.9 1.8 collective-permute-start.9
  31.2 1.7 collective-permute-start.1
  36.7 19.3 %collective-permute-done.9.refs_6_ = bf16[512,1024]{1,0:T(8,128)(2,1)} collective-permute-done((bf16[512,1024]{1,0:T(8,128)(2,1)}, bf16[512,1024]{1,0:T(8,128)(2,1)}, u32[]{:S(2)}, u32[]{:S(2)}) %collective-permute-start.9) | collective-permute-done | bytes 1048608 | tf_op jit(solution)/shard_map/ppermute | solution.py:288
  56.1 4.3 %collective-permute-done.3.outer2 = bf16[528,1024]{1,0:T(8,128)(2,1)} collective-permute-done((bf16[528,1024]{1,0:T(8,128)(2,1)}, bf16[528,1024]{1,0:T(8,128)(2,1)}, u32[]{:S(2)}, u32[]{:S(2)}) %collective-permute-start.3) | collective-permute-done | bytes 1081376 | tf_op jit(solution)/shard_map/ppermute | solution.py:330
  61.7 11.3 %shard_map.41 = (f32[512,1024]{1,0:T(8,128)S(1)}, bf16[3,528,1024]{2,1,0:T(8,128)(2,1)}, bf16[8,512,1024]{2,1,0:T(8,128)(2,1)S(1)}, bf16[2,512,1024]{2,1,0:T(8,128)(2,1)S(1)}) custom-call(s32[2]{0:T(128)S(1)} %pad_add_fusion.where, bf16[528,1024]{1,0:T(8,128)(2,1)S(1)} %fusion.2.own, bf16[528,1024]{1,0:T(8,128)(2,1)S(1)} %collective-permute-done.pair, ...), custom_call_target="tpu_custom_call" | custom-call | flops 3221225472 | bytes 25165824 | tf_op jit(solution)/shard_map/pallas_call | solution.py:276
  73.0 3.3 %copy-done = bf16[8,512,1024]{2,1,0:T(8,128)(2,1)} copy-done((bf16[8,512,1024]{2,1,0:T(8,128)(2,1)}, bf16[8,512,1024]{2,1,0:T(8,128)(2,1)S(1)}, u32[]{:S(2)}) %copy-start) | copy-done | bytes 8388632
  77.5 27.1 %collective-permute-done.11.outer3 = bf16[528,1024]{1,0:T(8,128)(2,1)S(1)} collective-permute-done((bf16[528,1024]{1,0:T(8,128)(2,1)}, bf16[528,1024]{1,0:T(8,128)(2,1)S(1)}, u32[]{:S(2)}, u32[]{:S(2)}) %collective-permute-start.11) | collective-permute-done | bytes 1081376 | tf_op jit(solution)/shard_map/ppermute | solution.py:332
  104.6 3.2 %shard_map.42 = (bf16[512,1024]{1,0:T(8,128)(2,1)S(1)}, f32[8,128]{1,0:T(8,128)S(1)}, bf16[528,1024]{1,0:T(8,128)(2,1)}) custom-call(s32[2]{0:T(128)S(1)} %pad_add_fusion.where, bf16[528,1024]{1,0:T(8,128)(2,1)S(1)} %fusion.2.own, f32[512,1024]{1,0:T(8,128)S(1)} %get-tuple-element.11.acc_in, bf16[2,512,1024]{2,1,0:T(8,128)(2,1)S(1)} %get-tuple-element.12.right, ...), custom_call_target="tpu_custom_call" | custom-call | flops 1073741824 | bytes 8388608 | tf_op jit(solution)/shard_map/pallas_call | solution.py:276
  107.9 2.8 %shard_map.45 = (bf16[512,512]{1,0:T(8,128)(2,1)}, bf16[512,512]{1,0:T(8,128)(2,1)}) custom-call(s32[2]{0:T(128)S(1)} %pad_add_fusion.where, bf16[512,1024]{1,0:T(8,128)(2,1)S(1)} %get-tuple-element.13.squared), custom_call_target="tpu_custom_call" | custom-call | bytes 2097152 | tf_op jit(solution)/shard_map/pallas_call | solution.py:276
  116.8 4.0 %collective-permute-start.23 = (f32[]{:T(128)}, f32[]{:T(128)}, u32[]{:S(2)}, u32[]{:S(2)}) collective-permute-start(f32[]{:T(128)} %add.17), channel_id=1, source_target_pairs={{0,8},{4,12},{8,0},{12,4},{16,24},{20,28},{24,16},{28,20},{1,9},{5... | collective-permute-start | bytes 20 | tf_op jit(solution)/shard_map/ppermute | solution.py:288
  120.8 17.7 %collective-permute-done.23 = f32[]{:T(128)} collective-permute-done((f32[]{:T(128)}, f32[]{:T(128)}, u32[]{:S(2)}, u32[]{:S(2)}) %collective-permute-start.23) | collective-permute-done | bytes 36 | tf_op jit(solution)/shard_map/ppermute | solution.py:288
  140.5 2.4 %collective-permute-done.24 = f32[]{:T(128)} collective-permute-done((f32[]{:T(128)}, f32[]{:T(128)}, u32[]{:S(2)}, u32[]{:S(2)}) %collective-permute-start.24) | collective-permute-done | bytes 36 | tf_op jit(solution)/shard_map/ppermute | solution.py:288
  143.5 2.4 %collective-permute-start.25 = (f32[]{:T(128)}, f32[]{:T(128)}, u32[]{:S(2)}, u32[]{:S(2)}) collective-permute-start(f32[]{:T(128)} %add.19), channel_id=1, source_target_pairs={{0,2},{1,3},{2,0},{3,1},{4,6},{5,7},{6,4},{7,5},{8,10},{9,11},{10,... | collective-permute-start | bytes 20 | tf_op jit(solution)/shard_map/ppermute | solution.py:401
  145.9 2.3 %collective-permute-done.25 = f32[]{:T(128)} collective-permute-done((f32[]{:T(128)}, f32[]{:T(128)}, u32[]{:S(2)}, u32[]{:S(2)}) %collective-permute-start.25) | collective-permute-done | bytes 36 | tf_op jit(solution)/shard_map/ppermute | solution.py:401
  150.2 2.2 %collective-permute-done.26 = f32[]{:T(128)} collective-permute-done((f32[]{:T(128)}, f32[]{:T(128)}, u32[]{:S(2)}, u32[]{:S(2)}) %collective-permute-start.26) | collective-permute-done | bytes 36 | tf_op jit(solution)/shard_map/ppermute | solution.py:401
  154.4 1.7 collective-permute-start.15
  156.8 7.5 %collective-permute-done.18.refs_2_ = bf16[512,512]{1,0:T(8,128)(2,1)} collective-permute-done((bf16[512,512]{1,0:T(8,128)(2,1)}, bf16[512,512]{1,0:T(8,128)(2,1)}, u32[]{:S(2)}, u32[]{:S(2)}) %collective-permute-start.18) | collective-permute-done | bytes 524320 | tf_op jit(solution)/shard_map/ppermute | solution.py:317
  168.2 8.0 %shard_map.43.local_square = bf16[512,1024]{1,0:T(8,128)(2,1)S(1)} custom-call(s32[2]{0:T(128)S(1)} %pad_add_fusion.where, bf16[3,528,1024]{2,1,0:T(8,128)(2,1)} %get-tuple-element.14.panel, bf16[3,528,1024]{2,1,0:T(8,128)(2,1)} %collective-permute-done.12.other, bf16[528,1024]{1,0:T(8,128)(2,1)} %get-tuple-element.15.far, ...), custom_call_target="tpu_custom_call" | custom-call | flops 4294967296 | bytes 9437184 | tf_op jit(solution)/shard_map/pallas_call | solution.py:276
  176.2 4.0 %shard_map.44.acc_in = f32[512,1024]{1,0:T(8,128)S(1)} custom-call(s32[2]{0:T(128)S(1)} %pad_add_fusion.where, bf16[512,1024]{1,0:T(8,128)(2,1)S(1)} %get-tuple-element.13.squared, bf16[512,1024]{1,0:T(8,128)(2,1)S(1)} %shard_map.43.local_square, bf16[8,512,1024]{2,1,0:T(8,128)(2,1)} %copy-done), custom_call_target="tpu_custom_call" | custom-call | flops 2147483648 | bytes 8388608 | tf_op jit(solution)/shard_map/pallas_call | solution.py:276
  181.6 18.4 %collective-permute-done.19.refs_3_ = bf16[512,512]{1,0:T(8,128)(2,1)S(1)} collective-permute-done((bf16[512,512]{1,0:T(8,128)(2,1)}, bf16[512,512]{1,0:T(8,128)(2,1)S(1)}, u32[]{:S(2)}, u32[]{:S(2)}) %collective-permute-start.19) | collective-permute-done | bytes 524320 | tf_op jit(solution)/shard_map/ppermute | solution.py:317
  200.0 11.2 %shard_map.46 = f32[512,1024]{1,0:T(8,128)} custom-call(s32[2]{0:T(128)S(1)} %pad_add_fusion.where, bf16[528,1024]{1,0:T(8,128)(2,1)} %copy-done.1, bf16[512,1024]{1,0:T(8,128)(2,1)S(1)} %get-tuple-element.13.squared, f32[512,1024]{1,0:T(8,128)} %copy-done.2, bf16[512,1024]{1,0:T(8,128)(2,1)S(1)} %collective-permute-done.14.turn1, ...), custom_call_target="tpu_custom_call" | custom-call | flops 3221225472 | bytes 16777216 | tf_op jit(solution)/shard_map/pallas_call | solution.py:276
  (56 shorter events, 27.1 us)
Async XLA Ops:
  2.6 26.3 %collective-permute-start.5 = (bf16[512,1024]{1,0:T(8,128)(2,1)S(1)}, bf16[512,1024]{1,0:T(8,128)(2,1)}, u32[]{:S(2)}, u32[]{:S(2)}) collective-permute-start(bf16[512,1024]{1,0:T(8,128)(2,1)S(1)} %fusion.1.refs_0_), channel_id=1, source_target_pairs={{0,8},{4,12},{8,0},{12,4},{16,24},{20,28},{24,16},{28,20},{1,9},{5... | collective-permute-start | bytes 3145736 | tf_op jit(solution)/shard_map/ppermute | solution.py:288
  5.8 25.4 %collective-permute-start = (bf16[528,1024]{1,0:T(8,128)(2,1)S(1)}, bf16[528,1024]{1,0:T(8,128)(2,1)S(1)}, u32[]{:S(2)}, u32[]{:S(2)}) collective-permute-start(bf16[528,1024]{1,0:T(8,128)(2,1)S(1)} %fusion.2.own), channel_id=1, source_target_pairs={{0,1},{1,0},{2,3},{3,2},{4,5},{5,4},{6,7},{7,6},{8,9},{9,8},{10,11... | collective-permute-start | bytes 3244040 | tf_op jit(solution)/shard_map/ppermute | solution.py:328
  7.5 25.4 %collective-permute-start.2 = (bf16[528,1024]{1,0:T(8,128)(2,1)S(1)}, bf16[528,1024]{1,0:T(8,128)(2,1)}, u32[]{:S(2)}, u32[]{:S(2)}) collective-permute-start(bf16[528,1024]{1,0:T(8,128)(2,1)S(1)} %fusion.2.own), channel_id=1, source_target_pairs={{1,2},{2,1},{5,6},{6,5},{9,10},{10,9},{13,14},{14,13},{17,18},{18,... | collective-permute-start | bytes 3244040 | tf_op jit(solution)/shard_map/ppermute | solution.py:329
  9.1 26.1 %collective-permute-start.7 = (bf16[512,1024]{1,0:T(8,128)(2,1)S(1)}, bf16[512,1024]{1,0:T(8,128)(2,1)}, u32[]{:S(2)}, u32[]{:S(2)}) collective-permute-start(bf16[512,1024]{1,0:T(8,128)(2,1)S(1)} %fusion.1.refs_0_), channel_id=1, source_target_pairs={{0,16},{4,20},{8,24},{12,28},{16,0},{20,4},{24,8},{28,12},{1,17},{... | collective-permute-start | bytes 3145736 | tf_op jit(solution)/shard_map/ppermute | solution.py:288
  10.6 24.6 %collective-permute-start.4 = (bf16[512,1024]{1,0:T(8,128)(2,1)S(1)}, bf16[512,1024]{1,0:T(8,128)(2,1)S(1)}, u32[]{:S(2)}, u32[]{:S(2)}) collective-permute-start(bf16[512,1024]{1,0:T(8,128)(2,1)S(1)} %fusion.1.refs_0_), channel_id=1, source_target_pairs={{0,4},{4,0},{8,12},{12,8},{16,20},{20,16},{24,28},{28,24},{1,5},{5... | collective-permute-start | bytes 3145736 | tf_op jit(solution)/shard_map/ppermute | solution.py:288
  28.9 27.1 %collective-permute-start.9 = (bf16[512,1024]{1,0:T(8,128)(2,1)}, bf16[512,1024]{1,0:T(8,128)(2,1)}, u32[]{:S(2)}, u32[]{:S(2)}) collective-permute-start(bf16[512,1024]{1,0:T(8,128)(2,1)} %collective-permute-done.5.refs_2_), channel_id=1, source_target_pairs={{0,16},{4,20},{8,24},{12,28},{16,0},{20,4},{24,8},{28,12},{1,17},{... | collective-permute-start | bytes 3145736 | tf_op jit(solution)/shard_map/ppermute | solution.py:288
  31.2 24.9 %collective-permute-start.1 = (bf16[528,1024]{1,0:T(8,128)(2,1)S(1)}, bf16[528,1024]{1,0:T(8,128)(2,1)}, u32[]{:S(2)}, u32[]{:S(2)}) collective-permute-start(bf16[528,1024]{1,0:T(8,128)(2,1)S(1)} %collective-permute-done.pair), channel_id=1, source_target_pairs={{1,2},{2,1},{5,6},{6,5},{9,10},{10,9},{13,14},{14,13},{17,18},{18,... | collective-permute-start | bytes 3244040 | tf_op jit(solution)/shard_map/ppermute | solution.py:331
  32.9 27.5 %collective-permute-start.3 = (bf16[528,1024]{1,0:T(8,128)(2,1)}, bf16[528,1024]{1,0:T(8,128)(2,1)}, u32[]{:S(2)}, u32[]{:S(2)}) collective-permute-start(bf16[528,1024]{1,0:T(8,128)(2,1)} %collective-permute-done.2.middle1), channel_id=1, source_target_pairs={{2,3},{1,0},{6,7},{5,4},{10,11},{9,8},{14,15},{13,12},{18,19},{17,... | collective-permute-start | bytes 3244040 | tf_op jit(solution)/shard_map/ppermute | solution.py:330
  35.3 20.9 %collective-permute-start.6 = (bf16[512,1024]{1,0:T(8,128)(2,1)}, bf16[512,1024]{1,0:T(8,128)(2,1)}, u32[]{:S(2)}, u32[]{:S(2)}) collective-permute-start(bf16[512,1024]{1,0:T(8,128)(2,1)} %collective-permute-done.5.refs_2_), channel_id=1, source_target_pairs={{0,4},{4,0},{8,12},{12,8},{16,20},{20,16},{24,28},{28,24},{1,5},{5... | collective-permute-start | bytes 3145736 | tf_op jit(solution)/shard_map/ppermute | solution.py:288
  36.2 19.9 %collective-permute-start.8 = (bf16[512,1024]{1,0:T(8,128)(2,1)}, bf16[512,1024]{1,0:T(8,128)(2,1)}, u32[]{:S(2)}, u32[]{:S(2)}) collective-permute-start(bf16[512,1024]{1,0:T(8,128)(2,1)} %collective-permute-done.7.refs_4_), channel_id=1, source_target_pairs={{0,4},{4,0},{8,12},{12,8},{16,20},{20,16},{24,28},{28,24},{1,5},{5... | collective-permute-start | bytes 3145736 | tf_op jit(solution)/shard_map/ppermute | solution.py:288
  56.0 4.4 %collective-permute-start.10 = (bf16[512,1024]{1,0:T(8,128)(2,1)}, bf16[512,1024]{1,0:T(8,128)(2,1)}, u32[]{:S(2)}, u32[]{:S(2)}) collective-permute-start(bf16[512,1024]{1,0:T(8,128)(2,1)} %collective-permute-done.9.refs_6_), channel_id=1, source_target_pairs={{0,4},{4,0},{8,12},{12,8},{16,20},{20,16},{24,28},{28,24},{1,5},{5... | collective-permute-start | bytes 3145736 | tf_op jit(solution)/shard_map/ppermute | solution.py:288
  76.2 90.7 %collective-permute-start.12 = (bf16[3,528,1024]{2,1,0:T(8,128)(2,1)}, bf16[3,528,1024]{2,1,0:T(8,128)(2,1)}, u32[]{:S(2)}, u32[]{:S(2)}) collective-permute-start(bf16[3,528,1024]{2,1,0:T(8,128)(2,1)} %get-tuple-element.14.panel), channel_id=1, source_target_pairs={{0,4},{4,0},{8,12},{12,8},{16,20},{20,16},{24,28},{28,24},{1,5},{5... | collective-permute-start | bytes 9732104 | tf_op jit(solution)/shard_map/ppermute | solution.py:288
  76.2 28.4 %collective-permute-start.11 = (bf16[528,1024]{1,0:T(8,128)(2,1)}, bf16[528,1024]{1,0:T(8,128)(2,1)S(1)}, u32[]{:S(2)}, u32[]{:S(2)}) collective-permute-start(bf16[528,1024]{1,0:T(8,128)(2,1)} %collective-permute-done.1.middle2), channel_id=1, source_target_pairs={{2,3},{1,0},{6,7},{5,4},{10,11},{9,8},{14,15},{13,12},{18,19},{17,... | collective-permute-start | bytes 3244040 | tf_op jit(solution)/shard_map/ppermute | solution.py:332
  107.8 57.8 %collective-permute-start.13 = (bf16[528,1024]{1,0:T(8,128)(2,1)}, bf16[528,1024]{1,0:T(8,128)(2,1)}, u32[]{:S(2)}, u32[]{:S(2)}) collective-permute-start(bf16[528,1024]{1,0:T(8,128)(2,1)} %get-tuple-element.15.far), channel_id=1, source_target_pairs={{0,4},{4,0},{8,12},{12,8},{16,20},{20,16},{24,28},{28,24},{1,5},{5... | collective-permute-start | bytes 3244040 | tf_op jit(solution)/shard_map/ppermute | solution.py:288
  110.7 42.9 %collective-permute-start.16 = (bf16[512,512]{1,0:T(8,128)(2,1)}, bf16[512,512]{1,0:T(8,128)(2,1)S(1)}, u32[]{:S(2)}, u32[]{:S(2)}) collective-permute-start(bf16[512,512]{1,0:T(8,128)(2,1)} %get-tuple-element.17), channel_id=1, source_target_pairs={{8,0},{12,4},{1,9},{5,13},{26,18},{30,22},{19,27},{23,31}} | collective-permute-start | bytes 1572872 | tf_op jit(solution)/shard_map/ppermute | solution.py:317
  112.0 42.4 %collective-permute-start.17 = (bf16[512,512]{1,0:T(8,128)(2,1)}, bf16[512,512]{1,0:T(8,128)(2,1)S(1)}, u32[]{:S(2)}, u32[]{:S(2)}) collective-permute-start(bf16[512,512]{1,0:T(8,128)(2,1)} %get-tuple-element.18), channel_id=1, source_target_pairs={{8,4},{12,0},{1,13},{5,9},{26,22},{30,18},{19,31},{23,27}} | collective-permute-start | bytes 1572872 | tf_op jit(solution)/shard_map/ppermute | solution.py:317
  116.8 21.7 %collective-permute-start.23 = (f32[]{:T(128)}, f32[]{:T(128)}, u32[]{:S(2)}, u32[]{:S(2)}) collective-permute-start(f32[]{:T(128)} %add.17), channel_id=1, source_target_pairs={{0,8},{4,12},{8,0},{12,4},{16,24},{20,28},{24,16},{28,20},{1,9},{5... | collective-permute-start | bytes 20 | tf_op jit(solution)/shard_map/ppermute | solution.py:288
  143.5 4.6 %collective-permute-start.25 = (f32[]{:T(128)}, f32[]{:T(128)}, u32[]{:S(2)}, u32[]{:S(2)}) collective-permute-start(f32[]{:T(128)} %add.19), channel_id=1, source_target_pairs={{0,2},{1,3},{2,0},{3,1},{4,6},{5,7},{6,4},{7,5},{8,10},{9,11},{10,... | collective-permute-start | bytes 20 | tf_op jit(solution)/shard_map/ppermute | solution.py:401
  152.4 11.9 %collective-permute-start.18 = (bf16[512,512]{1,0:T(8,128)(2,1)}, bf16[512,512]{1,0:T(8,128)(2,1)}, u32[]{:S(2)}, u32[]{:S(2)}) collective-permute-start(bf16[512,512]{1,0:T(8,128)(2,1)} %get-tuple-element.17), channel_id=1, source_target_pairs={{16,0},{20,4},{25,9},{29,13},{2,18},{6,22},{11,27},{15,31}} | collective-permute-start | bytes 1572872 | tf_op jit(solution)/shard_map/ppermute | solution.py:317
  153.7 46.3 %collective-permute-start.14 = (bf16[512,1024]{1,0:T(8,128)(2,1)S(1)}, bf16[512,1024]{1,0:T(8,128)(2,1)S(1)}, u32[]{:S(2)}, u32[]{:S(2)}) collective-permute-start(bf16[512,1024]{1,0:T(8,128)(2,1)S(1)} %get-tuple-element.13.squared), channel_id=1, source_target_pairs={{1,2},{2,3},{3,1},{5,6},{6,7},{7,5},{8,10},{10,11},{11,8},{12,14},... | collective-permute-start | bytes 3145736 | tf_op jit(solution)/shard_map/ppermute | solution.py:307
  154.4 45.6 %collective-permute-start.15 = (bf16[512,1024]{1,0:T(8,128)(2,1)S(1)}, bf16[512,1024]{1,0:T(8,128)(2,1)}, u32[]{:S(2)}, u32[]{:S(2)}) collective-permute-start(bf16[512,1024]{1,0:T(8,128)(2,1)S(1)} %get-tuple-element.13.squared), channel_id=1, source_target_pairs={{1,3},{2,1},{3,2},{5,7},{6,5},{7,6},{8,11},{10,8},{11,10},{12,15},... | collective-permute-start | bytes 3145736 | tf_op jit(solution)/shard_map/ppermute | solution.py:307
  164.3 35.7 %collective-permute-start.19 = (bf16[512,512]{1,0:T(8,128)(2,1)}, bf16[512,512]{1,0:T(8,128)(2,1)S(1)}, u32[]{:S(2)}, u32[]{:S(2)}) collective-permute-start(bf16[512,512]{1,0:T(8,128)(2,1)} %get-tuple-element.18), channel_id=1, source_target_pairs={{16,4},{20,0},{25,13},{29,9},{2,22},{6,18},{11,31},{15,27}} | collective-permute-start | bytes 1572872 | tf_op jit(solution)/shard_map/ppermute | solution.py:317
  165.6 34.4 %collective-permute-start.20 = (bf16[512,512]{1,0:T(8,128)(2,1)}, bf16[512,512]{1,0:T(8,128)(2,1)S(1)}, u32[]{:S(2)}, u32[]{:S(2)}) collective-permute-start(bf16[512,512]{1,0:T(8,128)(2,1)} %get-tuple-element.17), channel_id=1, source_target_pairs={{24,0},{28,4},{17,9},{21,13},{10,18},{14,22},{3,27},{7,31}} | collective-permute-start | bytes 1572872 | tf_op jit(solution)/shard_map/ppermute | solution.py:317
  166.9 33.1 %collective-permute-start.21 = (bf16[512,512]{1,0:T(8,128)(2,1)}, bf16[512,512]{1,0:T(8,128)(2,1)S(1)}, u32[]{:S(2)}, u32[]{:S(2)}) collective-permute-start(bf16[512,512]{1,0:T(8,128)(2,1)} %get-tuple-element.18), channel_id=1, source_target_pairs={{24,4},{28,0},{17,13},{21,9},{10,22},{14,18},{3,31},{7,27}} | collective-permute-start | bytes 1572872 | tf_op jit(solution)/shard_map/ppermute | solution.py:317
  (9 other events, 115.8 us)

commit v2 on v1

--- a/solution.py
+++ b/solution.py
@@ -41,6 +41,8 @@
     return (purified, occupation)
 
 
+NEAR = (0, 1, 3)
+LAST = 2
 TILE = 256
 EXTRA = 16
 
@@ -72,38 +74,29 @@
         )
 
 
-def square_early_kernel(where, own, pair, middle2, outer2, *refs):
+def square_early_kernel(where, own, pair, cross, *refs):
     rights = refs[:8]
     acc, panel, right, ahead, left_sem, right_sem, ahead_sem = refs[8:]
     row, col = where[0], where[1]
-    pltpu.make_async_copy(own, panel.at[0], left_sem.at[0]).start()
-    pltpu.make_async_copy(pair, panel.at[1], left_sem.at[1]).start()
-    inner = (col == 1) | (col == 2)
-
-    @pl.when(inner)
-    def _():
-        pltpu.make_async_copy(middle2, panel.at[2], left_sem.at[2]).start()
-
-    @pl.when(jnp.logical_not(inner))
-    def _():
-        pltpu.make_async_copy(outer2, panel.at[2], left_sem.at[2]).start()
+    for i, ref in enumerate((own, pair, cross)):
+        pltpu.make_async_copy(ref, panel.at[i], left_sem.at[i]).start()
 
     for k in range(8):
         slot = row ^ k
         pltpu.make_async_copy(rights[k], right.at[slot], right_sem.at[slot]).start()
-    slot = 2 * (col ^ 3)
+    slot = 2 * (col ^ LAST)
     for t in range(2):
         there = right.at[slot + t]
         pltpu.make_async_copy(there, there, right_sem.at[slot + t]).wait()
     hand_over = pltpu.make_async_copy(right.at[pl.ds(slot, 2)], ahead, ahead_sem)
     hand_over.start()
-    for d in range(3):
+    for i, d in enumerate(NEAR):
         slot = 2 * (col ^ d)
-        pltpu.make_async_copy(panel.at[d], panel.at[d], left_sem.at[d]).wait()
+        pltpu.make_async_copy(panel.at[i], panel.at[i], left_sem.at[i]).wait()
         for t in range(2):
             there = right.at[slot + t]
             pltpu.make_async_copy(there, there, right_sem.at[slot + t]).wait()
-        multiply(acc, panel.at[d], right.at[pl.ds(slot, 2)], d == 0)
+        multiply(acc, panel.at[i], right.at[pl.ds(slot, 2)], i == 0)
     hand_over.wait()
 
 
@@ -114,7 +107,7 @@
     ) + jnp.dot(left[:rows, rows:], right[1, :, lanes], preferred_element_type=jnp.float32)
 
 
-def square_late_kernel(where, own, acc_in, right, middle1, outer3, *refs):
+def square_late_kernel(where, own, acc_in, right, middle2, outer2, *refs):
     squared_ref, sum_ref, far, left_sem = refs
     row, col = where[0], where[1]
     rows, columns = squared_ref.shape
@@ -122,11 +115,11 @@
 
     @pl.when(inner)
     def _():
-        pltpu.make_async_copy(middle1, far, left_sem).start()
+        pltpu.make_async_copy(middle2, far, left_sem).start()
 
     @pl.when(jnp.logical_not(inner))
     def _():
-        pltpu.make_async_copy(outer3, far, left_sem).start()
+        pltpu.make_async_copy(outer2, far, left_sem).start()
 
     pltpu.make_async_copy(far, far, left_sem).wait()
     sums = jnp.zeros((8, TILE), jnp.float32)
@@ -175,7 +168,7 @@
     d = col ^ chip
     for source, last, h in ((panel, far, core), (other, far_other, 1 - core)):
         total = None
-        for left, right in [(panel.at[d], source.at[d]) for d in range(3)] + [(far, last)]:
+        for left, right in [(panel.at[i], source.at[i]) for i in range(3)] + [(far, last)]:
             part = lax.dot_general(
                 left[:rows, :],
                 right[:rows, :],
@@ -185,7 +178,7 @@
             total = part if total is None else total + part
         lanes = pl.ds(pl.multiple_of(h * rows, rows), rows)
         near = panel[jnp.minimum(d, 2), rows : rows + EXTRA, lanes].astype(jnp.float32)
-        kept = jnp.where(d == 3, far[rows : rows + EXTRA, lanes].astype(jnp.float32), near)
+        kept = jnp.where(d == LAST, far[rows : rows + EXTRA, lanes].astype(jnp.float32), near)
         for a in range(rows // B):
             out[a * B : (a + 1) * B, lanes] = (
                 total[a * B : (a + 1) * B] * kept[a : a + 1]
@@ -220,10 +213,8 @@
 
 
 def cubic_late_kernel(where, own, squared, acc_in, turn1, turn2, *refs):
-    sides, right_all, purified_ref, left, right, sem, right_sem = (
-        refs[:6],
-        *refs[6:],
-    )
+    sides = refs[:6]
+    right_all, purified_ref, left, right, acc, sem, right_sem = refs[6:]
     row, col = where[0], where[1]
     core, chip = row % 2, row // 2
     rows, columns = squared.shape
@@ -232,17 +223,13 @@
         pltpu.make_async_copy(right_all.at[pl.ds(2 * source, 2)], right.at[i], right_sem.at[i])
         for i, source in enumerate(late_sources(row, col))
     ]
-    for fetch in fetches:
-        fetch.start()
-
-    def finish(lefts):
+    fetches[0].start()
+    fetches[1].start()
+
+    def finish(last):
         for n in range(columns // TILE):
             lanes = slice(n * TILE, (n + 1) * TILE)
-            total = acc_in[:, lanes]
-            for i, ref in enumerate(lefts):
-                if n == 0:
-                    fetches[i].wait()
-                total = total + piece(ref, right.at[i], lanes)
+            total = acc_in[:, lanes] + acc[:, lanes] + piece(last, right.at[1], lanes)
             kept = own[rows : rows + EXTRA, lanes].astype(jnp.float32)
             for a in range(rows // B):
                 part = slice(a * B, (a + 1) * B)
@@ -251,18 +238,24 @@
 
     @pl.when(jnp.logical_not(corner))
     def _():
-        finish([turn1, turn2])
-        fetches[2].wait()
+        fetches[0].wait()
+        multiply(acc, turn1, right.at[0], True)
+        fetches[1].wait()
+        finish(turn2)
 
     @pl.when(corner)
     def _():
+        fetches[2].start()
         for i in range(3):
             for u in range(2):
                 lanes = pl.ds(pl.multiple_of((core ^ u) * rows, rows), rows)
                 pltpu.make_async_copy(sides[2 * i + u], left.at[i, :, lanes], sem.at[i]).start()
-        for i in range(3):
+        for i in (0, 2, 1):
             pltpu.make_async_copy(left.at[i], left.at[i], sem.at[i]).wait()
-        finish([left.at[i] for i in range(3)])
+            fetches[i].wait()
+            if i != 1:
+                multiply(acc, left.at[i], right.at[i], i == 0)
+        finish(left.at[1])
 
 
 ANYWHERE = pl.BlockSpec(memory_space=pl.ANY)
@@ -307,14 +300,22 @@
     return lax.ppermute(x, ("row", "col"), pairs)
 
 
-def to_corner(x, j, u):
+def in_plane(x, source, target, u):
     pairs = []
     for col in range(4):
         for core in range(2):
-            source = (col ^ j) * 2 + core
-            target = col * 2 + (core ^ u)
-            pairs.append((source * 4 + col, target * 4 + col))
+            here = (col ^ source) * 2 + core
+            there = (col ^ target) * 2 + (core ^ u)
+            pairs.append((here * 4 + col, there * 4 + col))
     return lax.ppermute(x, ("row", "col"), pairs)
+
+
+def to_corner(same, cross):
+    by_y = [in_plane(same, 2, 0, 0), in_plane(cross, 2, 0, 1)]
+    half_way = in_plane(cross, 3, 1, 0)
+    by_x = [in_plane(same, 1, 0, 0), in_plane(cross, 1, 0, 1)]
+    direct = in_plane(same, 3, 0, 0)
+    return [*by_x, *by_y, direct, in_plane(half_way, 1, 0, 1)]
 
 
 def local(density, pattern):
@@ -325,11 +326,10 @@
     kept = jnp.repeat(pattern.astype(jnp.bfloat16), B, axis=1)
     kept = jnp.pad(kept, ((0, EXTRA - kept.shape[0]), (0, 0)))
     own = jnp.concatenate([masked, kept], axis=0)
-    pair = lax.ppermute(own, "col", [(0, 1), (1, 0), (2, 3), (3, 2)])
-    middle1 = lax.ppermute(own, "col", [(1, 2), (2, 1)])
-    outer2 = lax.ppermute(middle1, "col", [(2, 3), (1, 0)])
+    pair = lax.ppermute(own, "col", [(i, i ^ 1) for i in range(4)])
+    cross = lax.ppermute(own, "col", [(i, i ^ 3) for i in range(4)])
     middle2 = lax.ppermute(pair, "col", [(1, 2), (2, 1)])
-    outer3 = lax.ppermute(middle2, "col", [(2, 3), (1, 0)])
+    outer2 = lax.ppermute(cross, "col", [(2, 3), (1, 0)])
     rights = column_gather(masked)
 
     flops = 2 * 2 * rows * rows * columns
@@ -340,8 +340,8 @@
     acc = pltpu.VMEM((rows, columns), jnp.float32)
     partial, panel, right, ahead = call(
         square_early_kernel,
-        [SCALARS] + [ANYWHERE] * 12,
-        (where, own, pair, middle2, outer2, *rights),
+        [SCALARS] + [ANYWHERE] * 11,
+        (where, own, pair, cross, *rights),
         (
             wide,
             jax.ShapeDtypeStruct((3, rows + EXTRA, columns), jnp.bfloat16),
@@ -356,7 +356,7 @@
     squared, sums, far = call(
         square_late_kernel,
         [SCALARS, WHOLE, WHOLE, WHOLE] + [ANYWHERE] * 2,
-        (where, own, partial, ahead, middle1, outer3),
+        (where, own, partial, ahead, middle2, outer2),
         (tile, jax.ShapeDtypeStruct((8, B), jnp.float32), extended),
         [DMA(())],
         flops,
@@ -364,7 +364,7 @@
     )
     turns = [rotate(squared, 1), rotate(squared, 2)]
     total = jnp.sum(sums)
-    for k in (1, 2, 4):
+    for k in (1, 4, 2):
         total = total + swap(total, k)
     quarter = jax.ShapeDtypeStruct((rows, rows), jnp.bfloat16)
     turned = call(
@@ -376,7 +376,7 @@
         0,
         2 * size,
     )
-    sides = [to_corner(turned[u], j, u) for j in (1, 2, 3) for u in (0, 1)]
+    sides = to_corner(*turned)
     local_square = call(
         own_square_kernel,
         [SCALARS] + [WHOLE] * 4,
@@ -407,6 +407,7 @@
         [
             pltpu.VMEM((3, rows, columns), jnp.bfloat16),
             pltpu.VMEM((3, 2, rows, columns), jnp.bfloat16),
+            acc,
             DMA((3,)),
             DMA((3,)),
         ],

time: 213 us -> 226 us (1.061)
  the two profiles are of different devices: /device:TPU:0 before, /device:TPU:3 now
where the time goes in v2:
time: 226 us; the launch traced here: 225 us
  waiting for transfers between devices  123 us (54%)
  starting transfers between devices  47.1 us (21%)
  Pallas kernels  39.4 us (17%)
  local copies, waits for them, and re-layouts  7.35 us (3%)
  between operations  5.8 us (3%)
  other arithmetic  2.27 us (1%)
    ppermute x12, waiting for transfers between devices, swap(): return lax.ppermute(x, 'row', [(i, i ^ k) for i in range(8)])  46.6 us
    pallas_call x6, Pallas kernels, call(): pl.pallas_call(kernel, out_shape=outs, in_specs=specs, out_specs=jax.tree...  39.4 us
    ppermute x1, waiting for transfers between devices, local(): outer2 = lax.ppermute(cross, 'col', [(2, 3), (1, 0)])  25.5 us
    ppermute x1, waiting for transfers between devices, local(): cross = lax.ppermute(own, 'col', [(i, i ^ 3) for i in range(4)])  24.8 us
    ppermute x2, waiting for transfers between devices, rotate(): return lax.ppermute(x, ('row', 'col'), pairs)  17.4 us
    ppermute x7, starting transfers between devices, in_plane(): return lax.ppermute(x, ('row', 'col'), pairs)  17.4 us
    ppermute x12, starting transfers between devices, swap(): return lax.ppermute(x, 'row', [(i, i ^ k) for i in range(8)])  15.8 us
    unnamed x16, local copies, waits for them, and re-layouts  7.15 us
  transfers between devices with their start and end apart: 27, of which 10 were waited for; matrix products, arithmetic and copies ran while one was open for 0% of the time, Pallas kernels for 9%

profile of v2, /device:TPU:3, one launch (start us, length us, event | category | flops | bytes accessed | tf_op | source)
XLA Modules:
  0.0 225.1 jit_solution(8918960111639400524)
XLA Ops:
  5.4 21.4 %collective-permute-done.3.refs_2_ = bf16[512,1024]{1,0:T(8,128)(2,1)S(1)} collective-permute-done((bf16[512,1024]{1,0:T(8,128)(2,1)S(1)}, bf16[512,1024]{1,0:T(8,128)(2,1)S(1)}, u32[]{:S(2)}, u32[]{:S(2)}) %collective-permute-start.3) | collective-permute-done | bytes 1048608 | tf_op jit(solution)/shard_map/ppermute | solution.py:281
  29.6 2.2 collective-permute-start.1
  31.8 2.3 %collective-permute-start.4 = (bf16[512,1024]{1,0:T(8,128)(2,1)S(1)}, bf16[512,1024]{1,0:T(8,128)(2,1)}, u32[]{:S(2)}, u32[]{:S(2)}) collective-permute-start(bf16[512,1024]{1,0:T(8,128)(2,1)S(1)} %collective-permute-done.3.refs_2_), channel_id=1, source_target_pairs={{0,4},{4,0},{8,12},{12,8},{16,20},{20,16},{24,28},{28,24},{1,5},{5... | collective-permute-start | bytes 3145736 | tf_op jit(solution)/shard_map/ppermute | solution.py:281
  35.1 15.2 %collective-permute-done.7.refs_6_ = bf16[512,1024]{1,0:T(8,128)(2,1)} collective-permute-done((bf16[512,1024]{1,0:T(8,128)(2,1)S(1)}, bf16[512,1024]{1,0:T(8,128)(2,1)}, u32[]{:S(2)}, u32[]{:S(2)}) %collective-permute-start.7) | collective-permute-done | bytes 1048608 | tf_op jit(solution)/shard_map/ppermute | solution.py:281
  50.2 2.3 %collective-permute-start.8 = (bf16[512,1024]{1,0:T(8,128)(2,1)}, bf16[512,1024]{1,0:T(8,128)(2,1)}, u32[]{:S(2)}, u32[]{:S(2)}) collective-permute-start(bf16[512,1024]{1,0:T(8,128)(2,1)} %collective-permute-done.7.refs_6_), channel_id=1, source_target_pairs={{0,4},{4,0},{8,12},{12,8},{16,20},{20,16},{24,28},{28,24},{1,5},{5... | collective-permute-start | bytes 3145736 | tf_op jit(solution)/shard_map/ppermute | solution.py:281
  52.6 24.8 %collective-permute-done.1.cross = bf16[528,1024]{1,0:T(8,128)(2,1)} collective-permute-done((bf16[528,1024]{1,0:T(8,128)(2,1)S(1)}, bf16[528,1024]{1,0:T(8,128)(2,1)}, u32[]{:S(2)}, u32[]{:S(2)}) %collective-permute-start.1) | collective-permute-done | bytes 1081376 | tf_op jit(solution)/shard_map/ppermute | solution.py:330
  78.6 11.2 %shard_map.41 = (f32[512,1024]{1,0:T(8,128)S(1)}, bf16[3,528,1024]{2,1,0:T(8,128)(2,1)}, bf16[8,512,1024]{2,1,0:T(8,128)(2,1)S(1)}, bf16[2,512,1024]{2,1,0:T(8,128)(2,1)S(1)}) custom-call(s32[2]{0:T(128)S(1)} %pad_add_fusion.where, bf16[528,1024]{1,0:T(8,128)(2,1)S(1)} %fusion.2.own, bf16[528,1024]{1,0:T(8,128)(2,1)} %collective-permute-done.pair, ...), custom_call_target="tpu_custom_call" | custom-call | flops 3221225472 | bytes 25165824 | tf_op jit(solution)/shard_map/pallas_call | solution.py:269
  89.9 3.3 %copy-done = bf16[8,512,1024]{2,1,0:T(8,128)(2,1)} copy-done((bf16[8,512,1024]{2,1,0:T(8,128)(2,1)}, bf16[8,512,1024]{2,1,0:T(8,128)(2,1)S(1)}, u32[]{:S(2)}) %copy-start) | copy-done | bytes 8388632
  93.1 2.6 %collective-permute-start.11 = (bf16[3,528,1024]{2,1,0:T(8,128)(2,1)}, bf16[3,528,1024]{2,1,0:T(8,128)(2,1)}, u32[]{:S(2)}, u32[]{:S(2)}) collective-permute-start(bf16[3,528,1024]{2,1,0:T(8,128)(2,1)} %get-tuple-element.14.panel), channel_id=1, source_target_pairs={{0,4},{4,0},{8,12},{12,8},{16,20},{20,16},{24,28},{28,24},{1,5},{5... | collective-permute-start | bytes 9732104 | tf_op jit(solution)/shard_map/ppermute | solution.py:281
  97.8 25.5 %collective-permute-done.10.outer2 = bf16[528,1024]{1,0:T(8,128)(2,1)S(1)} collective-permute-done((bf16[528,1024]{1,0:T(8,128)(2,1)}, bf16[528,1024]{1,0:T(8,128)(2,1)S(1)}, u32[]{:S(2)}, u32[]{:S(2)}) %collective-permute-start.10) | collective-permute-done | bytes 1081376 | tf_op jit(solution)/shard_map/ppermute | solution.py:332
  123.3 3.2 %shard_map.42 = (bf16[512,1024]{1,0:T(8,128)(2,1)S(1)}, f32[8,128]{1,0:T(8,128)S(1)}, bf16[528,1024]{1,0:T(8,128)(2,1)}) custom-call(s32[2]{0:T(128)S(1)} %pad_add_fusion.where, bf16[528,1024]{1,0:T(8,128)(2,1)S(1)} %fusion.2.own, f32[512,1024]{1,0:T(8,128)S(1)} %get-tuple-element.11.acc_in, bf16[2,512,1024]{2,1,0:T(8,128)(2,1)S(1)} %get-tuple-element.12.right, ...), custom_call_target="tpu_custom_call" | custom-call | flops 1073741824 | bytes 8388608 | tf_op jit(solution)/shard_map/pallas_call | solution.py:269
  127.4 2.8 %shard_map.45 = (bf16[512,512]{1,0:T(8,128)(2,1)}, bf16[512,512]{1,0:T(8,128)(2,1)}) custom-call(s32[2]{0:T(128)S(1)} %pad_add_fusion.where, bf16[512,1024]{1,0:T(8,128)(2,1)S(1)} %get-tuple-element.13.squared), custom_call_target="tpu_custom_call" | custom-call | bytes 2097152 | tf_op jit(solution)/shard_map/pallas_call | solution.py:269
  134.7 2.8 %collective-permute-start.23 = (f32[]{:T(128)}, f32[]{:T(128)}, u32[]{:S(2)}, u32[]{:S(2)}) collective-permute-start(f32[]{:T(128)} %add.17), channel_id=1, source_target_pairs={{0,16},{4,20},{8,24},{12,28},{16,0},{20,4},{24,8},{28,12},{1,17},{... | collective-permute-start | bytes 20 | tf_op jit(solution)/shard_map/ppermute | solution.py:281
  137.5 8.2 %collective-permute-done.23 = f32[]{:T(128)} collective-permute-done((f32[]{:T(128)}, f32[]{:T(128)}, u32[]{:S(2)}, u32[]{:S(2)}) %collective-permute-start.23) | collective-permute-done | bytes 36 | tf_op jit(solution)/shard_map/ppermute | solution.py:281
  149.6 1.9 collective-permute-start.25
  153.7 2.6 %collective-permute-start.26 = (f32[]{:T(128)}, f32[]{:T(128)}, u32[]{:S(2)}, u32[]{:S(2)}) collective-permute-start(f32[]{:T(128)} %add.20), channel_id=1, source_target_pairs={{0,1},{1,0},{2,3},{3,2},{4,5},{5,4},{6,7},{7,6},{8,9},{9,8},{10,11... | collective-permute-start | bytes 20 | tf_op jit(solution)/shard_map/ppermute | solution.py:401
  156.6 6.7 %collective-permute-start.16 = (bf16[512,512]{1,0:T(8,128)(2,1)}, bf16[512,512]{1,0:T(8,128)(2,1)S(1)}, u32[]{:S(2)}, u32[]{:S(2)}) collective-permute-start(bf16[512,512]{1,0:T(8,128)(2,1)} %get-tuple-element.18), channel_id=1, source_target_pairs={{8,4},{12,0},{1,13},{5,9},{26,22},{30,18},{19,31},{23,27}} | collective-permute-start | bytes 1572872 | tf_op jit(solution)/shard_map/ppermute | solution.py:310
  164.8 1.9 collective-permute-start.13
  166.7 7.0 %collective-permute-done.16.refs_1_ = bf16[512,512]{1,0:T(8,128)(2,1)S(1)} collective-permute-done((bf16[512,512]{1,0:T(8,128)(2,1)}, bf16[512,512]{1,0:T(8,128)(2,1)S(1)}, u32[]{:S(2)}, u32[]{:S(2)}) %collective-permute-start.16) | collective-permute-done | bytes 524320 | tf_op jit(solution)/shard_map/ppermute | solution.py:310
  177.7 5.2 %collective-permute-start.21 = (bf16[512,512]{1,0:T(8,128)(2,1)}, bf16[512,512]{1,0:T(8,128)(2,1)S(1)}, u32[]{:S(2)}, u32[]{:S(2)}) collective-permute-start(bf16[512,512]{1,0:T(8,128)(2,1)} %copy-done.6), channel_id=1, source_target_pairs={{8,4},{12,0},{1,13},{5,9},{26,22},{30,18},{19,31},{23,27}} | collective-permute-start | bytes 1572872 | tf_op jit(solution)/shard_map/ppermute | solution.py:310
  182.9 8.0 %shard_map.43.local_square = bf16[512,1024]{1,0:T(8,128)(2,1)S(1)} custom-call(s32[2]{0:T(128)S(1)} %pad_add_fusion.where, bf16[3,528,1024]{2,1,0:T(8,128)(2,1)} %get-tuple-element.14.panel, bf16[3,528,1024]{2,1,0:T(8,128)(2,1)} %collective-permute-done.11.other, bf16[528,1024]{1,0:T(8,128)(2,1)} %get-tuple-element.15.far, ...), custom_call_target="tpu_custom_call" | custom-call | flops 4294967296 | bytes 9437184 | tf_op jit(solution)/shard_map/pallas_call | solution.py:269
  190.9 5.8 %shard_map.44.acc_in = f32[512,1024]{1,0:T(8,128)S(1)} custom-call(s32[2]{0:T(128)S(1)} %pad_add_fusion.where, bf16[512,1024]{1,0:T(8,128)(2,1)S(1)} %get-tuple-element.13.squared, bf16[512,1024]{1,0:T(8,128)(2,1)S(1)} %shard_map.43.local_square, bf16[8,512,1024]{2,1,0:T(8,128)(2,1)} %copy-done), custom_call_target="tpu_custom_call" | custom-call | flops 2147483648 | bytes 8388608 | tf_op jit(solution)/shard_map/pallas_call | solution.py:269
  198.1 17.4 %collective-permute-done.14.turn2 = bf16[512,1024]{1,0:T(8,128)(2,1)} collective-permute-done((bf16[512,1024]{1,0:T(8,128)(2,1)S(1)}, bf16[512,1024]{1,0:T(8,128)(2,1)}, u32[]{:S(2)}, u32[]{:S(2)}) %collective-permute-start.14) | collective-permute-done | bytes 1048608 | tf_op jit(solution)/shard_map/ppermute | solution.py:300
  215.5 8.5 %shard_map.46 = f32[512,1024]{1,0:T(8,128)} custom-call(s32[2]{0:T(128)S(1)} %pad_add_fusion.where, bf16[528,1024]{1,0:T(8,128)(2,1)} %copy-done.1, bf16[512,1024]{1,0:T(8,128)(2,1)S(1)} %get-tuple-element.13.squared, f32[512,1024]{1,0:T(8,128)} %copy-done.2, bf16[512,1024]{1,0:T(8,128)(2,1)S(1)} %collective-permute-done.13.turn1, ...), custom_call_target="tpu_custom_call" | custom-call | flops 3221225472 | bytes 16777216 | tf_op jit(solution)/shard_map/pallas_call | solution.py:269
  (58 shorter events, 26.6 us)
Async XLA Ops:
  2.6 24.2 %collective-permute-start.3 = (bf16[512,1024]{1,0:T(8,128)(2,1)S(1)}, bf16[512,1024]{1,0:T(8,128)(2,1)S(1)}, u32[]{:S(2)}, u32[]{:S(2)}) collective-permute-start(bf16[512,1024]{1,0:T(8,128)(2,1)S(1)} %fusion.1.refs_0_), channel_id=1, source_target_pairs={{0,8},{4,12},{8,0},{12,4},{16,24},{20,28},{24,16},{28,20},{1,9},{5... | collective-permute-start | bytes 3145736 | tf_op jit(solution)/shard_map/ppermute | solution.py:281
  2.7 29.1 %collective-permute-start.5 = (bf16[512,1024]{1,0:T(8,128)(2,1)S(1)}, bf16[512,1024]{1,0:T(8,128)(2,1)}, u32[]{:S(2)}, u32[]{:S(2)}) collective-permute-start(bf16[512,1024]{1,0:T(8,128)(2,1)S(1)} %fusion.1.refs_0_), channel_id=1, source_target_pairs={{0,16},{4,20},{8,24},{12,28},{16,0},{20,4},{24,8},{28,12},{1,17},{... | collective-permute-start | bytes 3145736 | tf_op jit(solution)/shard_map/ppermute | solution.py:281
  4.2 29.9 %collective-permute-start.2 = (bf16[512,1024]{1,0:T(8,128)(2,1)S(1)}, bf16[512,1024]{1,0:T(8,128)(2,1)S(1)}, u32[]{:S(2)}, u32[]{:S(2)}) collective-permute-start(bf16[512,1024]{1,0:T(8,128)(2,1)S(1)} %fusion.1.refs_0_), channel_id=1, source_target_pairs={{0,4},{4,0},{8,12},{12,8},{16,20},{20,16},{24,28},{28,24},{1,5},{5... | collective-permute-start | bytes 3145736 | tf_op jit(solution)/shard_map/ppermute | solution.py:281
  26.8 23.4 %collective-permute-start.7 = (bf16[512,1024]{1,0:T(8,128)(2,1)S(1)}, bf16[512,1024]{1,0:T(8,128)(2,1)}, u32[]{:S(2)}, u32[]{:S(2)}) collective-permute-start(bf16[512,1024]{1,0:T(8,128)(2,1)S(1)} %collective-permute-done.3.refs_2_), channel_id=1, source_target_pairs={{0,16},{4,20},{8,24},{12,28},{16,0},{20,4},{24,8},{28,12},{1,17},{... | collective-permute-start | bytes 3145736 | tf_op jit(solution)/shard_map/ppermute | solution.py:281
  28.2 24.3 %collective-permute-start = (bf16[528,1024]{1,0:T(8,128)(2,1)S(1)}, bf16[528,1024]{1,0:T(8,128)(2,1)}, u32[]{:S(2)}, u32[]{:S(2)}) collective-permute-start(bf16[528,1024]{1,0:T(8,128)(2,1)S(1)} %fusion.2.own), channel_id=1, source_target_pairs={{0,1},{1,0},{2,3},{3,2},{4,5},{5,4},{6,7},{7,6},{8,9},{9,8},{10,11... | collective-permute-start | bytes 3244040 | tf_op jit(solution)/shard_map/ppermute | solution.py:329
  29.6 47.8 %collective-permute-start.1 = (bf16[528,1024]{1,0:T(8,128)(2,1)S(1)}, bf16[528,1024]{1,0:T(8,128)(2,1)}, u32[]{:S(2)}, u32[]{:S(2)}) collective-permute-start(bf16[528,1024]{1,0:T(8,128)(2,1)S(1)} %fusion.2.own), channel_id=1, source_target_pairs={{0,3},{1,2},{2,1},{3,0},{4,7},{5,6},{6,5},{7,4},{8,11},{9,10},{10,... | collective-permute-start | bytes 3244040 | tf_op jit(solution)/shard_map/ppermute | solution.py:330
  31.8 45.6 %collective-permute-start.4 = (bf16[512,1024]{1,0:T(8,128)(2,1)S(1)}, bf16[512,1024]{1,0:T(8,128)(2,1)}, u32[]{:S(2)}, u32[]{:S(2)}) collective-permute-start(bf16[512,1024]{1,0:T(8,128)(2,1)S(1)} %collective-permute-done.3.refs_2_), channel_id=1, source_target_pairs={{0,4},{4,0},{8,12},{12,8},{16,20},{20,16},{24,28},{28,24},{1,5},{5... | collective-permute-start | bytes 3145736 | tf_op jit(solution)/shard_map/ppermute | solution.py:281
  35.0 42.3 %collective-permute-start.6 = (bf16[512,1024]{1,0:T(8,128)(2,1)}, bf16[512,1024]{1,0:T(8,128)(2,1)}, u32[]{:S(2)}, u32[]{:S(2)}) collective-permute-start(bf16[512,1024]{1,0:T(8,128)(2,1)} %collective-permute-done.5.refs_4_), channel_id=1, source_target_pairs={{0,4},{4,0},{8,12},{12,8},{16,20},{20,16},{24,28},{28,24},{1,5},{5... | collective-permute-start | bytes 3145736 | tf_op jit(solution)/shard_map/ppermute | solution.py:281
  50.2 27.2 %collective-permute-start.8 = (bf16[512,1024]{1,0:T(8,128)(2,1)}, bf16[512,1024]{1,0:T(8,128)(2,1)}, u32[]{:S(2)}, u32[]{:S(2)}) collective-permute-start(bf16[512,1024]{1,0:T(8,128)(2,1)} %collective-permute-done.7.refs_6_), channel_id=1, source_target_pairs={{0,4},{4,0},{8,12},{12,8},{16,20},{20,16},{24,28},{28,24},{1,5},{5... | collective-permute-start | bytes 3145736 | tf_op jit(solution)/shard_map/ppermute | solution.py:281
  93.1 84.5 %collective-permute-start.11 = (bf16[3,528,1024]{2,1,0:T(8,128)(2,1)}, bf16[3,528,1024]{2,1,0:T(8,128)(2,1)}, u32[]{:S(2)}, u32[]{:S(2)}) collective-permute-start(bf16[3,528,1024]{2,1,0:T(8,128)(2,1)} %get-tuple-element.14.panel), channel_id=1, source_target_pairs={{0,4},{4,0},{8,12},{12,8},{16,20},{20,16},{24,28},{28,24},{1,5},{5... | collective-permute-start | bytes 9732104 | tf_op jit(solution)/shard_map/ppermute | solution.py:281
  95.7 27.5 %collective-permute-start.10 = (bf16[528,1024]{1,0:T(8,128)(2,1)}, bf16[528,1024]{1,0:T(8,128)(2,1)S(1)}, u32[]{:S(2)}, u32[]{:S(2)}) collective-permute-start(bf16[528,1024]{1,0:T(8,128)(2,1)} %collective-permute-done.1.cross), channel_id=1, source_target_pairs={{2,3},{1,0},{6,7},{5,4},{10,11},{9,8},{14,15},{13,12},{18,19},{17,... | collective-permute-start | bytes 3244040 | tf_op jit(solution)/shard_map/ppermute | solution.py:332
  97.0 26.2 %collective-permute-start.9 = (bf16[528,1024]{1,0:T(8,128)(2,1)}, bf16[528,1024]{1,0:T(8,128)(2,1)S(1)}, u32[]{:S(2)}, u32[]{:S(2)}) collective-permute-start(bf16[528,1024]{1,0:T(8,128)(2,1)} %collective-permute-done.pair), channel_id=1, source_target_pairs={{1,2},{2,1},{5,6},{6,5},{9,10},{10,9},{13,14},{14,13},{17,18},{18,... | collective-permute-start | bytes 3244040 | tf_op jit(solution)/shard_map/ppermute | solution.py:331
  126.5 50.5 %collective-permute-start.12 = (bf16[528,1024]{1,0:T(8,128)(2,1)}, bf16[528,1024]{1,0:T(8,128)(2,1)}, u32[]{:S(2)}, u32[]{:S(2)}) collective-permute-start(bf16[528,1024]{1,0:T(8,128)(2,1)} %get-tuple-element.15.far), channel_id=1, source_target_pairs={{0,4},{4,0},{8,12},{12,8},{16,20},{20,16},{24,28},{28,24},{1,5},{5... | collective-permute-start | bytes 3244040 | tf_op jit(solution)/shard_map/ppermute | solution.py:281
  130.2 33.2 %collective-permute-start.20 = (bf16[512,512]{1,0:T(8,128)(2,1)}, bf16[512,512]{1,0:T(8,128)(2,1)S(1)}, u32[]{:S(2)}, u32[]{:S(2)}) collective-permute-start(bf16[512,512]{1,0:T(8,128)(2,1)} %get-tuple-element.18), channel_id=1, source_target_pairs={{24,8},{28,12},{17,1},{21,5},{10,26},{14,30},{3,19},{7,23}} | collective-permute-start | bytes 1572872 | tf_op jit(solution)/shard_map/ppermute | solution.py:310
  132.1 32.7 %collective-permute-start.15 = (bf16[512,512]{1,0:T(8,128)(2,1)}, bf16[512,512]{1,0:T(8,128)(2,1)S(1)}, u32[]{:S(2)}, u32[]{:S(2)}) collective-permute-start(bf16[512,512]{1,0:T(8,128)(2,1)} %get-tuple-element.17), channel_id=1, source_target_pairs={{8,0},{12,4},{1,9},{5,13},{26,18},{30,22},{19,27},{23,31}} | collective-permute-start | bytes 1572872 | tf_op jit(solution)/shard_map/ppermute | solution.py:310
  134.7 11.1 %collective-permute-start.23 = (f32[]{:T(128)}, f32[]{:T(128)}, u32[]{:S(2)}, u32[]{:S(2)}) collective-permute-start(f32[]{:T(128)} %add.17), channel_id=1, source_target_pairs={{0,16},{4,20},{8,24},{12,28},{16,0},{20,4},{24,8},{28,12},{1,17},{... | collective-permute-start | bytes 20 | tf_op jit(solution)/shard_map/ppermute | solution.py:281
  149.6 3.5 %collective-permute-start.25 = (f32[]{:T(128)}, f32[]{:T(128)}, u32[]{:S(2)}, u32[]{:S(2)}) collective-permute-start(f32[]{:T(128)} %add.19), channel_id=1, source_target_pairs={{0,2},{1,3},{2,0},{3,1},{4,6},{5,7},{6,4},{7,5},{8,10},{9,11},{10,... | collective-permute-start | bytes 20 | tf_op jit(solution)/shard_map/ppermute | solution.py:401
  156.6 17.1 %collective-permute-start.16 = (bf16[512,512]{1,0:T(8,128)(2,1)}, bf16[512,512]{1,0:T(8,128)(2,1)S(1)}, u32[]{:S(2)}, u32[]{:S(2)}) collective-permute-start(bf16[512,512]{1,0:T(8,128)(2,1)} %get-tuple-element.18), channel_id=1, source_target_pairs={{8,4},{12,0},{1,13},{5,9},{26,22},{30,18},{19,31},{23,27}} | collective-permute-start | bytes 1572872 | tf_op jit(solution)/shard_map/ppermute | solution.py:310
  163.4 12.9 %collective-permute-start.17 = (bf16[512,512]{1,0:T(8,128)(2,1)}, bf16[512,512]{1,0:T(8,128)(2,1)}, u32[]{:S(2)}, u32[]{:S(2)}) collective-permute-start(bf16[512,512]{1,0:T(8,128)(2,1)} %get-tuple-element.17), channel_id=1, source_target_pairs={{16,0},{20,4},{25,9},{29,13},{2,18},{6,22},{11,27},{15,31}} | collective-permute-start | bytes 1572872 | tf_op jit(solution)/shard_map/ppermute | solution.py:310
  164.8 33.3 %collective-permute-start.13 = (bf16[512,1024]{1,0:T(8,128)(2,1)S(1)}, bf16[512,1024]{1,0:T(8,128)(2,1)S(1)}, u32[]{:S(2)}, u32[]{:S(2)}) collective-permute-start(bf16[512,1024]{1,0:T(8,128)(2,1)S(1)} %get-tuple-element.13.squared), channel_id=1, source_target_pairs={{1,2},{2,3},{3,1},{5,6},{6,7},{7,5},{8,10},{10,11},{11,8},{12,14},... | collective-permute-start | bytes 3145736 | tf_op jit(solution)/shard_map/ppermute | solution.py:300
  173.7 41.8 %collective-permute-start.14 = (bf16[512,1024]{1,0:T(8,128)(2,1)S(1)}, bf16[512,1024]{1,0:T(8,128)(2,1)}, u32[]{:S(2)}, u32[]{:S(2)}) collective-permute-start(bf16[512,1024]{1,0:T(8,128)(2,1)S(1)} %get-tuple-element.13.squared), channel_id=1, source_target_pairs={{1,3},{2,1},{3,2},{5,7},{6,5},{7,6},{8,11},{10,8},{11,10},{12,15},... | collective-permute-start | bytes 3145736 | tf_op jit(solution)/shard_map/ppermute | solution.py:300
  176.3 21.8 %collective-permute-start.18 = (bf16[512,512]{1,0:T(8,128)(2,1)}, bf16[512,512]{1,0:T(8,128)(2,1)S(1)}, u32[]{:S(2)}, u32[]{:S(2)}) collective-permute-start(bf16[512,512]{1,0:T(8,128)(2,1)} %get-tuple-element.18), channel_id=1, source_target_pairs={{16,4},{20,0},{25,13},{29,9},{2,22},{6,18},{11,31},{15,27}} | collective-permute-start | bytes 1572872 | tf_op jit(solution)/shard_map/ppermute | solution.py:310
  177.0 21.1 %collective-permute-start.19 = (bf16[512,512]{1,0:T(8,128)(2,1)}, bf16[512,512]{1,0:T(8,128)(2,1)S(1)}, u32[]{:S(2)}, u32[]{:S(2)}) collective-permute-start(bf16[512,512]{1,0:T(8,128)(2,1)} %get-tuple-element.17), channel_id=1, source_target_pairs={{24,0},{28,4},{17,9},{21,13},{10,18},{14,22},{3,27},{7,31}} | collective-permute-start | bytes 1572872 | tf_op jit(solution)/shard_map/ppermute | solution.py:310
  177.7 20.4 %collective-permute-start.21 = (bf16[512,512]{1,0:T(8,128)(2,1)}, bf16[512,512]{1,0:T(8,128)(2,1)S(1)}, u32[]{:S(2)}, u32[]{:S(2)}) collective-permute-start(bf16[512,512]{1,0:T(8,128)(2,1)} %copy-done.6), channel_id=1, source_target_pairs={{8,4},{12,0},{1,13},{5,9},{26,22},{30,18},{19,31},{23,27}} | collective-permute-start | bytes 1572872 | tf_op jit(solution)/shard_map/ppermute | solution.py:310
  (10 other events, 111.4 us)

commit v3 on v2

--- a/solution.py
+++ b/solution.py
@@ -212,24 +212,58 @@
         multiply(acc, local_square, right.at[1], False)
 
 
-def cubic_late_kernel(where, own, squared, acc_in, turn1, turn2, *refs):
-    sides = refs[:6]
-    right_all, purified_ref, left, right, acc, sem, right_sem = refs[6:]
-    row, col = where[0], where[1]
-    core, chip = row % 2, row // 2
+def load_side(pieces, left, sem, core):
+    for u, ref in enumerate(pieces):
+        half = ref.shape[0]
+        lanes = pl.ds(pl.multiple_of((core ^ u) * half, half), half)
+        pltpu.make_async_copy(ref, left.at[:, lanes], sem).start()
+
+
+def fetch_right(right_all, source, right, sem):
+    return pltpu.make_async_copy(right_all.at[pl.ds(2 * source, 2)], right, sem)
+
+
+def cubic_middle_kernel(where, acc_in, turn, *refs):
+    sides, right_all, acc, left, right, sem, right_sem = refs[:4], *refs[4:]
+    row, col = where[0], where[1]
+    corner = row // 2 == col
+    sources = late_sources(row, col)
+    first = fetch_right(right_all, sources[0], right.at[0], right_sem.at[0])
+    second = fetch_right(right_all, sources[1], right.at[1], right_sem.at[1])
+    first.start()
+    acc[...] = acc_in[...]
+
+    @pl.when(jnp.logical_not(corner))
+    def _():
+        first.wait()
+        multiply(acc, turn, right.at[0], False)
+
+    @pl.when(corner)
+    def _():
+        second.start()
+        for i in range(2):
+            load_side(sides[2 * i : 2 * i + 2], left.at[i], sem.at[i], row % 2)
+        for i, fetch in enumerate((first, second)):
+            pltpu.make_async_copy(left.at[i], left.at[i], sem.at[i]).wait()
+            fetch.wait()
+            multiply(acc, left.at[i], right.at[i], False)
+
+
+def cubic_late_kernel(where, own, squared, acc, turn, *refs):
+    sides, right_all, purified_ref, left, right, sem, right_sem = refs[:2], *refs[2:]
+    row, col = where[0], where[1]
     rows, columns = squared.shape
-    corner = chip == col
-    fetches = [
-        pltpu.make_async_copy(right_all.at[pl.ds(2 * source, 2)], right.at[i], right_sem.at[i])
-        for i, source in enumerate(late_sources(row, col))
-    ]
-    fetches[0].start()
-    fetches[1].start()
+    corner = row // 2 == col
+    sources = late_sources(row, col)
+    fetch = fetch_right(
+        right_all, jnp.where(corner, sources[2], sources[1]), right, right_sem
+    )
+    fetch.start()
 
     def finish(last):
         for n in range(columns // TILE):
             lanes = slice(n * TILE, (n + 1) * TILE)
-            total = acc_in[:, lanes] + acc[:, lanes] + piece(last, right.at[1], lanes)
+            total = acc[:, lanes] + piece(last, right, lanes)
             kept = own[rows : rows + EXTRA, lanes].astype(jnp.float32)
             for a in range(rows // B):
                 part = slice(a * B, (a + 1) * B)
@@ -238,24 +272,15 @@
 
     @pl.when(jnp.logical_not(corner))
     def _():
-        fetches[0].wait()
-        multiply(acc, turn1, right.at[0], True)
-        fetches[1].wait()
-        finish(turn2)
+        fetch.wait()
+        finish(turn)
 
     @pl.when(corner)
     def _():
-        fetches[2].start()
-        for i in range(3):
-            for u in range(2):
-                lanes = pl.ds(pl.multiple_of((core ^ u) * rows, rows), rows)
-                pltpu.make_async_copy(sides[2 * i + u], left.at[i, :, lanes], sem.at[i]).start()
-        for i in (0, 2, 1):
-            pltpu.make_async_copy(left.at[i], left.at[i], sem.at[i]).wait()
-            fetches[i].wait()
-            if i != 1:
-                multiply(acc, left.at[i], right.at[i], i == 0)
-        finish(left.at[1])
+        load_side(sides, left, sem, row % 2)
+        pltpu.make_async_copy(left, left, sem).wait()
+        fetch.wait()
+        finish(left)
 
 
 ANYWHERE = pl.BlockSpec(memory_space=pl.ANY)
@@ -337,7 +362,6 @@
     tile = jax.ShapeDtypeStruct((rows, columns), jnp.bfloat16)
     wide = jax.ShapeDtypeStruct((rows, columns), jnp.float32)
     extended = jax.ShapeDtypeStruct((rows + EXTRA, columns), jnp.bfloat16)
-    acc = pltpu.VMEM((rows, columns), jnp.float32)
     partial, panel, right, ahead = call(
         square_early_kernel,
         [SCALARS] + [ANYWHERE] * 11,
@@ -399,20 +423,34 @@
     )
     for k in (2, 1):
         total = total + lax.ppermute(total, "col", [(i, i ^ k) for i in range(4)])
+    cubic = call(
+        cubic_middle_kernel,
+        [SCALARS] + [WHOLE] * 2 + [ANYWHERE] * 4 + [AWAY],
+        (where, cubic, turns[0], *sides[:4], right),
+        wide,
+        [
+            pltpu.VMEM((2, rows, columns), jnp.bfloat16),
+            pltpu.VMEM((2, 2, rows, columns), jnp.bfloat16),
+            DMA((2,)),
+            DMA((2,)),
+        ],
+        2 * flops,
+        10 * size,
+        48,
+    )
     purified = call(
         cubic_late_kernel,
-        [SCALARS] + [WHOLE] * 5 + [ANYWHERE] * 6 + [AWAY],
-        (where, own, squared, cubic, *turns, *sides, right),
+        [SCALARS] + [WHOLE] * 4 + [ANYWHERE] * 2 + [AWAY],
+        (where, own, squared, cubic, turns[1], *sides[4:], right),
         wide,
         [
-            pltpu.VMEM((3, rows, columns), jnp.bfloat16),
-            pltpu.VMEM((3, 2, rows, columns), jnp.bfloat16),
-            acc,
-            DMA((3,)),
-            DMA((3,)),
+            pltpu.VMEM((rows, columns), jnp.bfloat16),
+            pltpu.VMEM((2, rows, columns), jnp.bfloat16),
+            DMA(()),
+            DMA(()),
         ],
-        3 * flops,
-        16 * size,
+        flops,
+        9 * size,
         48,
     )
     return (purified, total / (rows * lax.axis_size("row")))

time: 226 us -> 229 us (1.013)
  the two profiles are of different devices: /device:TPU:3 before, /device:TPU:0 now
where the time goes in v3:
time: 229 us; the launch traced here: 227 us
  waiting for transfers between devices  129 us (56%)
  Pallas kernels  41.5 us (18%)
  starting transfers between devices  36.6 us (16%)
  local copies, waits for them, and re-layouts  11.1 us (5%)
  between operations  5.82 us (3%)
    ppermute x12, waiting for transfers between devices, swap(): return lax.ppermute(x, 'row', [(i, i ^ k) for i in range(8)])  55.4 us
    pallas_call x7, Pallas kernels, call(): pl.pallas_call(kernel, out_shape=outs, in_specs=specs, out_specs=jax.tree...  41.5 us
    ppermute x1, waiting for transfers between devices, local(): outer2 = lax.ppermute(cross, 'col', [(2, 3), (1, 0)])  26.3 us
    ppermute x1, waiting for transfers between devices, local(): cross = lax.ppermute(own, 'col', [(i, i ^ 3) for i in range(4)])  24.1 us
    ppermute x7, waiting for transfers between devices, in_plane(): return lax.ppermute(x, ('row', 'col'), pairs)  17 us
    ppermute x12, starting transfers between devices, swap(): return lax.ppermute(x, 'row', [(i, i ^ k) for i in range(8)])  12.7 us
    unnamed x26, local copies, waits for them, and re-layouts  10.9 us
    ppermute x7, starting transfers between devices, in_plane(): return lax.ppermute(x, ('row', 'col'), pairs)  9.19 us
  transfers between devices with their start and end apart: 27, of which 12 were waited for; matrix products, arithmetic and copies ran while one was open for 0% of the time, Pallas kernels for 11%

profile of v3, /device:TPU:0, one launch (start us, length us, event | category | flops | bytes accessed | tf_op | source)
XLA Modules:
  0.0 226.7 jit_solution(1422918149720768709)
XLA Ops:
  2.6 3.0 %collective-permute-start.3 = (bf16[512,1024]{1,0:T(8,128)(2,1)S(1)}, bf16[512,1024]{1,0:T(8,128)(2,1)S(1)}, u32[]{:S(2)}, u32[]{:S(2)}) collective-permute-start(bf16[512,1024]{1,0:T(8,128)(2,1)S(1)} %fusion.1.refs_0_), channel_id=1, source_target_pairs={{0,8},{4,12},{8,0},{12,4},{16,24},{20,28},{24,16},{28,20},{1,9},{5... | collective-permute-start | bytes 3145736 | tf_op jit(solution)/shard_map/ppermute | solution.py:306
  7.2 21.6 %collective-permute-done.3.refs_2_ = bf16[512,1024]{1,0:T(8,128)(2,1)S(1)} collective-permute-done((bf16[512,1024]{1,0:T(8,128)(2,1)S(1)}, bf16[512,1024]{1,0:T(8,128)(2,1)S(1)}, u32[]{:S(2)}, u32[]{:S(2)}) %collective-permute-start.3) | collective-permute-done | bytes 1048608 | tf_op jit(solution)/shard_map/ppermute | solution.py:306
  28.8 1.8 collective-permute-start.7
  30.7 1.6 collective-permute-start
  32.4 2.5 %collective-permute-start.1 = (bf16[528,1024]{1,0:T(8,128)(2,1)S(1)}, bf16[528,1024]{1,0:T(8,128)(2,1)}, u32[]{:S(2)}, u32[]{:S(2)}) collective-permute-start(bf16[528,1024]{1,0:T(8,128)(2,1)S(1)} %fusion.2.own), channel_id=1, source_target_pairs={{0,3},{1,2},{2,1},{3,0},{4,7},{5,6},{6,5},{7,4},{8,11},{9,10},{10,... | collective-permute-start | bytes 3244040 | tf_op jit(solution)/shard_map/ppermute | solution.py:355
  36.3 17.0 %collective-permute-done.7.refs_6_ = bf16[512,1024]{1,0:T(8,128)(2,1)} collective-permute-done((bf16[512,1024]{1,0:T(8,128)(2,1)S(1)}, bf16[512,1024]{1,0:T(8,128)(2,1)}, u32[]{:S(2)}, u32[]{:S(2)}) %collective-permute-start.7) | collective-permute-done | bytes 1048608 | tf_op jit(solution)/shard_map/ppermute | solution.py:306
  53.4 3.2 %collective-permute-done.pair = bf16[528,1024]{1,0:T(8,128)(2,1)} collective-permute-done((bf16[528,1024]{1,0:T(8,128)(2,1)S(1)}, bf16[528,1024]{1,0:T(8,128)(2,1)}, u32[]{:S(2)}, u32[]{:S(2)}) %collective-permute-start) | collective-permute-done | bytes 1081376 | tf_op jit(solution)/shard_map/ppermute | solution.py:354
  56.6 24.1 %collective-permute-done.1.cross = bf16[528,1024]{1,0:T(8,128)(2,1)} collective-permute-done((bf16[528,1024]{1,0:T(8,128)(2,1)S(1)}, bf16[528,1024]{1,0:T(8,128)(2,1)}, u32[]{:S(2)}, u32[]{:S(2)}) %collective-permute-start.1) | collective-permute-done | bytes 1081376 | tf_op jit(solution)/shard_map/ppermute | solution.py:355
  82.0 10.6 %shard_map.41 = (f32[512,1024]{1,0:T(8,128)S(1)}, bf16[3,528,1024]{2,1,0:T(8,128)(2,1)}, bf16[8,512,1024]{2,1,0:T(8,128)(2,1)S(1)}, bf16[2,512,1024]{2,1,0:T(8,128)(2,1)S(1)}) custom-call(s32[2]{0:T(128)S(1)} %pad_add_fusion.where, bf16[528,1024]{1,0:T(8,128)(2,1)S(1)} %fusion.2.own, bf16[528,1024]{1,0:T(8,128)(2,1)} %collective-permute-done.pair, ...), custom_call_target="tpu_custom_call" | custom-call | flops 3221225472 | bytes 25165824 | tf_op jit(solution)/shard_map/pallas_call | solution.py:294
  92.6 3.3 %copy-done = bf16[8,512,1024]{2,1,0:T(8,128)(2,1)} copy-done((bf16[8,512,1024]{2,1,0:T(8,128)(2,1)}, bf16[8,512,1024]{2,1,0:T(8,128)(2,1)S(1)}, u32[]{:S(2)}) %copy-start) | copy-done | bytes 8388632
  97.9 26.3 %collective-permute-done.10.outer2 = bf16[528,1024]{1,0:T(8,128)(2,1)S(1)} collective-permute-done((bf16[528,1024]{1,0:T(8,128)(2,1)}, bf16[528,1024]{1,0:T(8,128)(2,1)S(1)}, u32[]{:S(2)}, u32[]{:S(2)}) %collective-permute-start.10) | collective-permute-done | bytes 1081376 | tf_op jit(solution)/shard_map/ppermute | solution.py:357
  124.3 3.2 %shard_map.42 = (bf16[512,1024]{1,0:T(8,128)(2,1)S(1)}, f32[8,128]{1,0:T(8,128)S(1)}, bf16[528,1024]{1,0:T(8,128)(2,1)}) custom-call(s32[2]{0:T(128)S(1)} %pad_add_fusion.where, bf16[528,1024]{1,0:T(8,128)(2,1)S(1)} %fusion.2.own, f32[512,1024]{1,0:T(8,128)S(1)} %get-tuple-element.11.acc_in, bf16[2,512,1024]{2,1,0:T(8,128)(2,1)S(1)} %get-tuple-element.12.right, ...), custom_call_target="tpu_custom_call" | custom-call | flops 1073741824 | bytes 8388608 | tf_op jit(solution)/shard_map/pallas_call | solution.py:294
  127.6 2.8 %shard_map.45 = (bf16[512,512]{1,0:T(8,128)(2,1)}, bf16[512,512]{1,0:T(8,128)(2,1)}) custom-call(s32[2]{0:T(128)S(1)} %pad_add_fusion.where, bf16[512,1024]{1,0:T(8,128)(2,1)S(1)} %get-tuple-element.13.squared), custom_call_target="tpu_custom_call" | custom-call | bytes 2097152 | tf_op jit(solution)/shard_map/pallas_call | solution.py:294
  137.6 2.2 collective-permute-done.23
  140.5 4.0 %collective-permute-start.24 = (f32[]{:T(128)}, f32[]{:T(128)}, u32[]{:S(2)}, u32[]{:S(2)}) collective-permute-start(f32[]{:T(128)} %add.18), channel_id=1, source_target_pairs={{0,8},{4,12},{8,0},{12,4},{16,24},{20,28},{24,16},{28,20},{1,9},{5... | collective-permute-start | bytes 20 | tf_op jit(solution)/shard_map/ppermute | solution.py:306
  144.4 13.6 %collective-permute-done.24 = f32[]{:T(128)} collective-permute-done((f32[]{:T(128)}, f32[]{:T(128)}, u32[]{:S(2)}, u32[]{:S(2)}) %collective-permute-start.24) | collective-permute-done | bytes 36 | tf_op jit(solution)/shard_map/ppermute | solution.py:306
  160.0 3.1 %collective-permute-done.25 = f32[]{:T(128)} collective-permute-done((f32[]{:T(128)}, f32[]{:T(128)}, u32[]{:S(2)}, u32[]{:S(2)}) %collective-permute-start.25) | collective-permute-done | bytes 36 | tf_op jit(solution)/shard_map/ppermute | solution.py:425
  163.7 4.9 %collective-permute-start.26 = (f32[]{:T(128)}, f32[]{:T(128)}, u32[]{:S(2)}, u32[]{:S(2)}) collective-permute-start(f32[]{:T(128)} %add.20), channel_id=1, source_target_pairs={{0,1},{1,0},{2,3},{3,2},{4,5},{5,4},{6,7},{7,6},{8,9},{9,8},{10,11... | collective-permute-start | bytes 20 | tf_op jit(solution)/shard_map/ppermute | solution.py:425
  174.8 7.9 %collective-permute-done.16.refs_2_ = bf16[512,512]{1,0:T(8,128)(2,1)S(1)} collective-permute-done((bf16[512,512]{1,0:T(8,128)(2,1)}, bf16[512,512]{1,0:T(8,128)(2,1)S(1)}, u32[]{:S(2)}, u32[]{:S(2)}) %collective-permute-start.16) | collective-permute-done | bytes 524320 | tf_op jit(solution)/shard_map/ppermute | solution.py:335
  188.7 8.0 %shard_map.43.local_square = bf16[512,1024]{1,0:T(8,128)(2,1)S(1)} custom-call(s32[2]{0:T(128)S(1)} %pad_add_fusion.where, bf16[3,528,1024]{2,1,0:T(8,128)(2,1)} %get-tuple-element.14.panel, bf16[3,528,1024]{2,1,0:T(8,128)(2,1)} %collective-permute-done.11.other, bf16[528,1024]{1,0:T(8,128)(2,1)} %get-tuple-element.15.far, ...), custom_call_target="tpu_custom_call" | custom-call | flops 4294967296 | bytes 9437184 | tf_op jit(solution)/shard_map/pallas_call | solution.py:294
  196.8 4.0 %shard_map.44.acc_in = f32[512,1024]{1,0:T(8,128)S(1)} custom-call(s32[2]{0:T(128)S(1)} %pad_add_fusion.where, bf16[512,1024]{1,0:T(8,128)(2,1)S(1)} %get-tuple-element.13.squared, bf16[512,1024]{1,0:T(8,128)(2,1)S(1)} %shard_map.43.local_square, bf16[8,512,1024]{2,1,0:T(8,128)(2,1)} %copy-done), custom_call_target="tpu_custom_call" | custom-call | flops 2147483648 | bytes 8388608 | tf_op jit(solution)/shard_map/pallas_call | solution.py:294
  202.0 9.1 %collective-permute-done.17.refs_3_ = bf16[512,512]{1,0:T(8,128)(2,1)S(1)} collective-permute-done((bf16[512,512]{1,0:T(8,128)(2,1)}, bf16[512,512]{1,0:T(8,128)(2,1)S(1)}, u32[]{:S(2)}, u32[]{:S(2)}) %collective-permute-start.17) | collective-permute-done | bytes 524320 | tf_op jit(solution)/shard_map/ppermute | solution.py:335
  211.2 7.1 %shard_map.46.acc = f32[512,1024]{1,0:T(8,128)S(1)} custom-call(s32[2]{0:T(128)S(1)} %pad_add_fusion.where, f32[512,1024]{1,0:T(8,128)} %copy-done.2, bf16[512,1024]{1,0:T(8,128)(2,1)} %collective-permute-done.13.turn, bf16[512,512]{1,0:T(8,128)(2,1)S(1)} %copy-done.4, bf16[512,512]{1,0:T(8,128)(2,1)S(1)} %copy-done.6, bf16[512,512]{1,0:T(8,128)(2,1)S(1)} %copy-done.8, ...), custom_call_target="tpu_custom_call" | custom-call | flops 2147483648 | bytes 10485760 | tf_op jit(solution)/shard_map/pallas_call | solution.py:294
  219.7 5.9 %shard_map.47 = f32[512,1024]{1,0:T(8,128)} custom-call(s32[2]{0:T(128)S(1)} %pad_add_fusion.where, bf16[528,1024]{1,0:T(8,128)(2,1)S(1)} %fusion.2.own, bf16[512,1024]{1,0:T(8,128)(2,1)S(1)} %get-tuple-element.13.squared, f32[512,1024]{1,0:T(8,128)} %copy-done.1, bf16[512,1024]{1,0:T(8,128)(2,1)S(1)} %collective-permute-done.18.turn, ...), custom_call_target="tpu_custom_call" | custom-call | flops 1073741824 | bytes 9437184 | tf_op jit(solution)/shard_map/pallas_call | solution.py:294
  (69 shorter events, 30.2 us)
Async XLA Ops:
  2.6 26.2 %collective-permute-start.3 = (bf16[512,1024]{1,0:T(8,128)(2,1)S(1)}, bf16[512,1024]{1,0:T(8,128)(2,1)S(1)}, u32[]{:S(2)}, u32[]{:S(2)}) collective-permute-start(bf16[512,1024]{1,0:T(8,128)(2,1)S(1)} %fusion.1.refs_0_), channel_id=1, source_target_pairs={{0,8},{4,12},{8,0},{12,4},{16,24},{20,28},{24,16},{28,20},{1,9},{5... | collective-permute-start | bytes 3145736 | tf_op jit(solution)/shard_map/ppermute | solution.py:306
  5.6 29.2 %collective-permute-start.5 = (bf16[512,1024]{1,0:T(8,128)(2,1)S(1)}, bf16[512,1024]{1,0:T(8,128)(2,1)}, u32[]{:S(2)}, u32[]{:S(2)}) collective-permute-start(bf16[512,1024]{1,0:T(8,128)(2,1)S(1)} %fusion.1.refs_0_), channel_id=1, source_target_pairs={{0,16},{4,20},{8,24},{12,28},{16,0},{20,4},{24,8},{28,12},{1,17},{... | collective-permute-start | bytes 3145736 | tf_op jit(solution)/shard_map/ppermute | solution.py:306
  7.2 27.7 %collective-permute-start.2 = (bf16[512,1024]{1,0:T(8,128)(2,1)S(1)}, bf16[512,1024]{1,0:T(8,128)(2,1)S(1)}, u32[]{:S(2)}, u32[]{:S(2)}) collective-permute-start(bf16[512,1024]{1,0:T(8,128)(2,1)S(1)} %fusion.1.refs_0_), channel_id=1, source_target_pairs={{0,4},{4,0},{8,12},{12,8},{16,20},{20,16},{24,28},{28,24},{1,5},{5... | collective-permute-start | bytes 3145736 | tf_op jit(solution)/shard_map/ppermute | solution.py:306
  28.8 24.5 %collective-permute-start.7 = (bf16[512,1024]{1,0:T(8,128)(2,1)S(1)}, bf16[512,1024]{1,0:T(8,128)(2,1)}, u32[]{:S(2)}, u32[]{:S(2)}) collective-permute-start(bf16[512,1024]{1,0:T(8,128)(2,1)S(1)} %collective-permute-done.3.refs_2_), channel_id=1, source_target_pairs={{0,16},{4,20},{8,24},{12,28},{16,0},{20,4},{24,8},{28,12},{1,17},{... | collective-permute-start | bytes 3145736 | tf_op jit(solution)/shard_map/ppermute | solution.py:306
  30.7 25.9 %collective-permute-start = (bf16[528,1024]{1,0:T(8,128)(2,1)S(1)}, bf16[528,1024]{1,0:T(8,128)(2,1)}, u32[]{:S(2)}, u32[]{:S(2)}) collective-permute-start(bf16[528,1024]{1,0:T(8,128)(2,1)S(1)} %fusion.2.own), channel_id=1, source_target_pairs={{0,1},{1,0},{2,3},{3,2},{4,5},{5,4},{6,7},{7,6},{8,9},{9,8},{10,11... | collective-permute-start | bytes 3244040 | tf_op jit(solution)/shard_map/ppermute | solution.py:354
  32.4 48.4 %collective-permute-start.1 = (bf16[528,1024]{1,0:T(8,128)(2,1)S(1)}, bf16[528,1024]{1,0:T(8,128)(2,1)}, u32[]{:S(2)}, u32[]{:S(2)}) collective-permute-start(bf16[528,1024]{1,0:T(8,128)(2,1)S(1)} %fusion.2.own), channel_id=1, source_target_pairs={{0,3},{1,2},{2,1},{3,0},{4,7},{5,6},{6,5},{7,4},{8,11},{9,10},{10,... | collective-permute-start | bytes 3244040 | tf_op jit(solution)/shard_map/ppermute | solution.py:355
  34.9 45.9 %collective-permute-start.4 = (bf16[512,1024]{1,0:T(8,128)(2,1)S(1)}, bf16[512,1024]{1,0:T(8,128)(2,1)}, u32[]{:S(2)}, u32[]{:S(2)}) collective-permute-start(bf16[512,1024]{1,0:T(8,128)(2,1)S(1)} %collective-permute-done.3.refs_2_), channel_id=1, source_target_pairs={{0,4},{4,0},{8,12},{12,8},{16,20},{20,16},{24,28},{28,24},{1,5},{5... | collective-permute-start | bytes 3145736 | tf_op jit(solution)/shard_map/ppermute | solution.py:306
  35.8 44.9 %collective-permute-start.6 = (bf16[512,1024]{1,0:T(8,128)(2,1)}, bf16[512,1024]{1,0:T(8,128)(2,1)}, u32[]{:S(2)}, u32[]{:S(2)}) collective-permute-start(bf16[512,1024]{1,0:T(8,128)(2,1)} %collective-permute-done.5.refs_4_), channel_id=1, source_target_pairs={{0,4},{4,0},{8,12},{12,8},{16,20},{20,16},{24,28},{28,24},{1,5},{5... | collective-permute-start | bytes 3145736 | tf_op jit(solution)/shard_map/ppermute | solution.py:306
  53.3 27.5 %collective-permute-start.8 = (bf16[512,1024]{1,0:T(8,128)(2,1)}, bf16[512,1024]{1,0:T(8,128)(2,1)}, u32[]{:S(2)}, u32[]{:S(2)}) collective-permute-start(bf16[512,1024]{1,0:T(8,128)(2,1)} %collective-permute-done.7.refs_6_), channel_id=1, source_target_pairs={{0,4},{4,0},{8,12},{12,8},{16,20},{20,16},{24,28},{28,24},{1,5},{5... | collective-permute-start | bytes 3145736 | tf_op jit(solution)/shard_map/ppermute | solution.py:306
  95.9 91.5 %collective-permute-start.11 = (bf16[3,528,1024]{2,1,0:T(8,128)(2,1)}, bf16[3,528,1024]{2,1,0:T(8,128)(2,1)}, u32[]{:S(2)}, u32[]{:S(2)}) collective-permute-start(bf16[3,528,1024]{2,1,0:T(8,128)(2,1)} %get-tuple-element.14.panel), channel_id=1, source_target_pairs={{0,4},{4,0},{8,12},{12,8},{16,20},{20,16},{24,28},{28,24},{1,5},{5... | collective-permute-start | bytes 9732104 | tf_op jit(solution)/shard_map/ppermute | solution.py:306
  95.9 28.4 %collective-permute-start.10 = (bf16[528,1024]{1,0:T(8,128)(2,1)}, bf16[528,1024]{1,0:T(8,128)(2,1)S(1)}, u32[]{:S(2)}, u32[]{:S(2)}) collective-permute-start(bf16[528,1024]{1,0:T(8,128)(2,1)} %collective-permute-done.1.cross), channel_id=1, source_target_pairs={{2,3},{1,0},{6,7},{5,4},{10,11},{9,8},{14,15},{13,12},{18,19},{17,... | collective-permute-start | bytes 3244040 | tf_op jit(solution)/shard_map/ppermute | solution.py:357
  97.2 27.1 %collective-permute-start.9 = (bf16[528,1024]{1,0:T(8,128)(2,1)}, bf16[528,1024]{1,0:T(8,128)(2,1)S(1)}, u32[]{:S(2)}, u32[]{:S(2)}) collective-permute-start(bf16[528,1024]{1,0:T(8,128)(2,1)} %collective-permute-done.pair), channel_id=1, source_target_pairs={{1,2},{2,1},{5,6},{6,5},{9,10},{10,9},{13,14},{14,13},{17,18},{18,... | collective-permute-start | bytes 3244040 | tf_op jit(solution)/shard_map/ppermute | solution.py:356
  127.5 58.6 %collective-permute-start.12 = (bf16[528,1024]{1,0:T(8,128)(2,1)}, bf16[528,1024]{1,0:T(8,128)(2,1)}, u32[]{:S(2)}, u32[]{:S(2)}) collective-permute-start(bf16[528,1024]{1,0:T(8,128)(2,1)} %get-tuple-element.15.far), channel_id=1, source_target_pairs={{0,4},{4,0},{8,12},{12,8},{16,20},{20,16},{24,28},{28,24},{1,5},{5... | collective-permute-start | bytes 3244040 | tf_op jit(solution)/shard_map/ppermute | solution.py:306
  130.4 39.7 %collective-permute-start.14 = (bf16[512,512]{1,0:T(8,128)(2,1)}, bf16[512,512]{1,0:T(8,128)(2,1)S(1)}, u32[]{:S(2)}, u32[]{:S(2)}) collective-permute-start(bf16[512,512]{1,0:T(8,128)(2,1)} %get-tuple-element.17), channel_id=1, source_target_pairs={{8,0},{12,4},{1,9},{5,13},{26,18},{30,22},{19,27},{23,31}} | collective-permute-start | bytes 1572872 | tf_op jit(solution)/shard_map/ppermute | solution.py:335
  131.7 40.7 %collective-permute-start.15 = (bf16[512,512]{1,0:T(8,128)(2,1)}, bf16[512,512]{1,0:T(8,128)(2,1)S(1)}, u32[]{:S(2)}, u32[]{:S(2)}) collective-permute-start(bf16[512,512]{1,0:T(8,128)(2,1)} %get-tuple-element.18), channel_id=1, source_target_pairs={{8,4},{12,0},{1,13},{5,9},{26,22},{30,18},{19,31},{23,27}} | collective-permute-start | bytes 1572872 | tf_op jit(solution)/shard_map/ppermute | solution.py:335
  140.5 17.5 %collective-permute-start.24 = (f32[]{:T(128)}, f32[]{:T(128)}, u32[]{:S(2)}, u32[]{:S(2)}) collective-permute-start(f32[]{:T(128)} %add.18), channel_id=1, source_target_pairs={{0,8},{4,12},{8,0},{12,4},{16,24},{20,28},{24,16},{28,20},{1,9},{5... | collective-permute-start | bytes 20 | tf_op jit(solution)/shard_map/ppermute | solution.py:306
  163.7 5.1 %collective-permute-start.26 = (f32[]{:T(128)}, f32[]{:T(128)}, u32[]{:S(2)}, u32[]{:S(2)}) collective-permute-start(f32[]{:T(128)} %add.20), channel_id=1, source_target_pairs={{0,1},{1,0},{2,3},{3,2},{4,5},{5,4},{6,7},{7,6},{8,9},{9,8},{10,11... | collective-permute-start | bytes 20 | tf_op jit(solution)/shard_map/ppermute | solution.py:425
  168.8 13.8 %collective-permute-start.16 = (bf16[512,512]{1,0:T(8,128)(2,1)}, bf16[512,512]{1,0:T(8,128)(2,1)S(1)}, u32[]{:S(2)}, u32[]{:S(2)}) collective-permute-start(bf16[512,512]{1,0:T(8,128)(2,1)} %get-tuple-element.17), channel_id=1, source_target_pairs={{16,0},{20,4},{25,9},{29,13},{2,18},{6,22},{11,27},{15,31}} | collective-permute-start | bytes 1572872 | tf_op jit(solution)/shard_map/ppermute | solution.py:335
  170.9 14.0 %collective-permute-start.20 = (bf16[512,512]{1,0:T(8,128)(2,1)}, bf16[512,512]{1,0:T(8,128)(2,1)}, u32[]{:S(2)}, u32[]{:S(2)}) collective-permute-start(bf16[512,512]{1,0:T(8,128)(2,1)} %get-tuple-element.18), channel_id=1, source_target_pairs={{24,8},{28,12},{17,1},{21,5},{10,26},{14,30},{3,19},{7,23}} | collective-permute-start | bytes 1572872 | tf_op jit(solution)/shard_map/ppermute | solution.py:335
  173.1 38.0 %collective-permute-start.13 = (bf16[512,1024]{1,0:T(8,128)(2,1)S(1)}, bf16[512,1024]{1,0:T(8,128)(2,1)}, u32[]{:S(2)}, u32[]{:S(2)}) collective-permute-start(bf16[512,1024]{1,0:T(8,128)(2,1)S(1)} %get-tuple-element.13.squared), channel_id=1, source_target_pairs={{1,2},{2,3},{3,1},{5,6},{6,7},{7,5},{8,10},{10,11},{11,8},{12,14},... | collective-permute-start | bytes 3145736 | tf_op jit(solution)/shard_map/ppermute | solution.py:325
  183.4 36.3 %collective-permute-start.18 = (bf16[512,1024]{1,0:T(8,128)(2,1)S(1)}, bf16[512,1024]{1,0:T(8,128)(2,1)S(1)}, u32[]{:S(2)}, u32[]{:S(2)}) collective-permute-start(bf16[512,1024]{1,0:T(8,128)(2,1)S(1)} %get-tuple-element.13.squared), channel_id=1, source_target_pairs={{1,3},{2,1},{3,2},{5,7},{6,5},{7,6},{8,11},{10,8},{11,10},{12,15},... | collective-permute-start | bytes 3145736 | tf_op jit(solution)/shard_map/ppermute | solution.py:325
  184.8 26.3 %collective-permute-start.17 = (bf16[512,512]{1,0:T(8,128)(2,1)}, bf16[512,512]{1,0:T(8,128)(2,1)S(1)}, u32[]{:S(2)}, u32[]{:S(2)}) collective-permute-start(bf16[512,512]{1,0:T(8,128)(2,1)} %get-tuple-element.18), channel_id=1, source_target_pairs={{16,4},{20,0},{25,13},{29,9},{2,22},{6,18},{11,31},{15,27}} | collective-permute-start | bytes 1572872 | tf_op jit(solution)/shard_map/ppermute | solution.py:335
  186.1 33.5 %collective-permute-start.19 = (bf16[512,512]{1,0:T(8,128)(2,1)}, bf16[512,512]{1,0:T(8,128)(2,1)S(1)}, u32[]{:S(2)}, u32[]{:S(2)}) collective-permute-start(bf16[512,512]{1,0:T(8,128)(2,1)} %get-tuple-element.17), channel_id=1, source_target_pairs={{24,0},{28,4},{17,9},{21,13},{10,18},{14,22},{3,27},{7,31}} | collective-permute-start | bytes 1572872 | tf_op jit(solution)/shard_map/ppermute | solution.py:335
  187.4 32.2 %collective-permute-start.21 = (bf16[512,512]{1,0:T(8,128)(2,1)}, bf16[512,512]{1,0:T(8,128)(2,1)S(1)}, u32[]{:S(2)}, u32[]{:S(2)}) collective-permute-start(bf16[512,512]{1,0:T(8,128)(2,1)} %collective-permute-done.20), channel_id=1, source_target_pairs={{8,4},{12,0},{1,13},{5,9},{26,22},{30,18},{19,31},{23,27}} | collective-permute-start | bytes 1572872 | tf_op jit(solution)/shard_map/ppermute | solution.py:335
  (15 other events, 64.6 us)

commit v4 on v2

--- a/solution.py
+++ b/solution.py
@@ -43,23 +43,21 @@
 
 NEAR = (0, 1, 3)
 LAST = 2
-TILE = 256
 EXTRA = 16
 
 
+def piece(left, right):
+    rows = right.shape[1]
+    return jnp.dot(left[:rows, :rows], right[0], preferred_element_type=jnp.float32) + jnp.dot(
+        left[:rows, rows:], right[1], preferred_element_type=jnp.float32
+    )
+
+
 def multiply(acc, left, right, fresh):
-    rows, columns = acc.shape
-
-    @pl.loop(0, columns // TILE)
-    def _(n):
-        lanes = pl.ds(pl.multiple_of(n * TILE, TILE), TILE)
-        part = jnp.dot(
-            left[:rows, :rows], right[0, :, lanes], preferred_element_type=jnp.float32
-        ) + jnp.dot(left[:rows, rows:], right[1, :, lanes], preferred_element_type=jnp.float32)
-        if fresh:
-            acc[:, lanes] = part
-        else:
-            acc[:, lanes] += part
+    if fresh:
+        acc[...] = piece(left, right)
+    else:
+        acc[...] += piece(left, right)
 
 
 def blocks(rows, columns, body):
@@ -76,7 +74,7 @@
 
 def square_early_kernel(where, own, pair, cross, *refs):
     rights = refs[:8]
-    acc, panel, right, ahead, left_sem, right_sem, ahead_sem = refs[8:]
+    acc, panel, right, left_sem, right_sem = refs[8:]
     row, col = where[0], where[1]
     for i, ref in enumerate((own, pair, cross)):
         pltpu.make_async_copy(ref, panel.at[i], left_sem.at[i]).start()
@@ -84,12 +82,6 @@
     for k in range(8):
         slot = row ^ k
         pltpu.make_async_copy(rights[k], right.at[slot], right_sem.at[slot]).start()
-    slot = 2 * (col ^ LAST)
-    for t in range(2):
-        there = right.at[slot + t]
-        pltpu.make_async_copy(there, there, right_sem.at[slot + t]).wait()
-    hand_over = pltpu.make_async_copy(right.at[pl.ds(slot, 2)], ahead, ahead_sem)
-    hand_over.start()
     for i, d in enumerate(NEAR):
         slot = 2 * (col ^ d)
         pltpu.make_async_copy(panel.at[i], panel.at[i], left_sem.at[i]).wait()
@@ -97,14 +89,10 @@
             there = right.at[slot + t]
             pltpu.make_async_copy(there, there, right_sem.at[slot + t]).wait()
         multiply(acc, panel.at[i], right.at[pl.ds(slot, 2)], i == 0)
-    hand_over.wait()
-
-
-def piece(left, right, lanes):
-    rows = right.shape[1]
-    return jnp.dot(
-        left[:rows, :rows], right[0, :, lanes], preferred_element_type=jnp.float32
-    ) + jnp.dot(left[:rows, rows:], right[1, :, lanes], preferred_element_type=jnp.float32)
+    slot = 2 * (col ^ LAST)
+    for t in range(2):
+        there = right.at[slot + t]
+        pltpu.make_async_copy(there, there, right_sem.at[slot + t]).wait()
 
 
 def square_late_kernel(where, own, acc_in, right, middle2, outer2, *refs):
@@ -122,19 +110,17 @@
         pltpu.make_async_copy(outer2, far, left_sem).start()
 
     pltpu.make_async_copy(far, far, left_sem).wait()
-    sums = jnp.zeros((8, TILE), jnp.float32)
-    for n in range(columns // TILE):
-        lanes = slice(n * TILE, (n + 1) * TILE)
-        total = acc_in[:, lanes] + piece(far, right, lanes)
-        kept = own[rows : rows + EXTRA, lanes].astype(jnp.float32)
-        for a in range(rows // B):
-            part = slice(a * B, (a + 1) * B)
-            squared = (total[part] * kept[a : a + 1]).astype(jnp.bfloat16)
-            squared_ref[part, lanes] = squared
-            term = squared.astype(jnp.float32) * own[part, lanes].astype(jnp.float32)
-            sums -= 2.0 * jnp.sum(term.reshape(B // 8, 8, TILE), axis=0)
+    total = acc_in[...] + piece(far, right.at[pl.ds(2 * (col ^ LAST), 2)])
+    kept = own[rows : rows + EXTRA, :].astype(jnp.float32)
+    sums = jnp.zeros((8, columns), jnp.float32)
+    for a in range(rows // B):
+        part = slice(a * B, (a + 1) * B)
+        squared = (total[part] * kept[a : a + 1]).astype(jnp.bfloat16)
+        squared_ref[part, :] = squared
+        term = squared.astype(jnp.float32) * own[part, :].astype(jnp.float32)
+        sums -= 2.0 * jnp.sum(term.reshape(B // 8, 8, columns), axis=0)
     sum_ref[...] = sums[:, :B]
-    for n in range(1, TILE // B):
+    for n in range(1, columns // B):
         sum_ref[...] += sums[:, n * B : (n + 1) * B]
 
     @pl.when(row // 2 == col)
@@ -147,6 +133,12 @@
             squared = squared_ref[a * B : (a + 1) * B, lanes].astype(jnp.float32)
             term = jnp.where(same, 3.0 * squared, 0.0)
             sum_ref[...] += jnp.sum(term.reshape(B // 8, 8, B), axis=0)
+
+    sum_ref[...] = jnp.broadcast_to(jnp.sum(sum_ref[...], keepdims=True), sum_ref.shape)
+
+
+def add_kernel(left, right, out):
+    out[...] = left[...] + right[...]
 
 
 def turn_kernel(where, squared, same_ref, cross_ref):
@@ -196,76 +188,58 @@
     return sources
 
 
-def cubic_early_kernel(where, squared, local_square, right_all, acc, right, sem):
+def cubic_early_kernel(where, squared, local_square, right, acc):
     row, col = where[0], where[1]
     chip = row // 2
-    first = pltpu.make_async_copy(right_all.at[pl.ds(2 * col, 2)], right.at[0], sem.at[0])
-    second = pltpu.make_async_copy(right_all.at[pl.ds(2 * chip, 2)], right.at[1], sem.at[1])
-    first.start()
-    second.start()
-    first.wait()
-    multiply(acc, squared, right.at[0], True)
-    second.wait()
+    multiply(acc, squared, right.at[pl.ds(2 * col, 2)], True)
 
     @pl.when(chip != col)
     def _():
-        multiply(acc, local_square, right.at[1], False)
-
-
-def cubic_late_kernel(where, own, squared, acc_in, turn1, turn2, *refs):
+        multiply(acc, local_square, right.at[pl.ds(2 * chip, 2)], False)
+
+
+def cubic_late_kernel(where, own, squared, acc_in, turn1, turn2, right_all, *refs):
     sides = refs[:6]
-    right_all, purified_ref, left, right, acc, sem, right_sem = refs[6:]
+    purified_ref, left, acc, sem = refs[6:]
     row, col = where[0], where[1]
     core, chip = row % 2, row // 2
-    rows, columns = squared.shape
+    rows, _ = squared.shape
     corner = chip == col
-    fetches = [
-        pltpu.make_async_copy(right_all.at[pl.ds(2 * source, 2)], right.at[i], right_sem.at[i])
-        for i, source in enumerate(late_sources(row, col))
-    ]
-    fetches[0].start()
-    fetches[1].start()
+    rights = [right_all.at[pl.ds(2 * source, 2)] for source in late_sources(row, col)]
 
     def finish(last):
-        for n in range(columns // TILE):
-            lanes = slice(n * TILE, (n + 1) * TILE)
-            total = acc_in[:, lanes] + acc[:, lanes] + piece(last, right.at[1], lanes)
-            kept = own[rows : rows + EXTRA, lanes].astype(jnp.float32)
-            for a in range(rows // B):
-                part = slice(a * B, (a + 1) * B)
-                wide = squared[part, lanes].astype(jnp.float32)
-                purified_ref[part, lanes] = 3.0 * wide - 2.0 * (total[part] * kept[a : a + 1])
+        total = acc_in[...] + acc[...] + piece(last, rights[1])
+        kept = own[rows : rows + EXTRA, :].astype(jnp.float32)
+        for a in range(rows // B):
+            part = slice(a * B, (a + 1) * B)
+            wide = squared[part, :].astype(jnp.float32)
+            purified_ref[part, :] = 3.0 * wide - 2.0 * (total[part] * kept[a : a + 1])
 
     @pl.when(jnp.logical_not(corner))
     def _():
-        fetches[0].wait()
-        multiply(acc, turn1, right.at[0], True)
-        fetches[1].wait()
+        multiply(acc, turn1, rights[0], True)
         finish(turn2)
 
     @pl.when(corner)
     def _():
-        fetches[2].start()
         for i in range(3):
             for u in range(2):
                 lanes = pl.ds(pl.multiple_of((core ^ u) * rows, rows), rows)
                 pltpu.make_async_copy(sides[2 * i + u], left.at[i, :, lanes], sem.at[i]).start()
         for i in (0, 2, 1):
             pltpu.make_async_copy(left.at[i], left.at[i], sem.at[i]).wait()
-            fetches[i].wait()
             if i != 1:
-                multiply(acc, left.at[i], right.at[i], i == 0)
+                multiply(acc, left.at[i], rights[i], i == 0)
         finish(left.at[1])
 
 
 ANYWHERE = pl.BlockSpec(memory_space=pl.ANY)
-AWAY = pl.BlockSpec(memory_space=pltpu.HBM)
 SCALARS = pl.BlockSpec(memory_space=pltpu.SMEM)
 WHOLE = pl.BlockSpec(memory_space=pltpu.VMEM)
 DMA = pltpu.SemaphoreType.DMA
 
 
-def call(kernel, specs, args, outs, scratch, flops, moved, grant=24):
+def call(kernel, specs, args, outs, scratch, flops, moved, grant=16):
     return pl.pallas_call(
         kernel,
         out_shape=outs,
@@ -338,7 +312,7 @@
     wide = jax.ShapeDtypeStruct((rows, columns), jnp.float32)
     extended = jax.ShapeDtypeStruct((rows + EXTRA, columns), jnp.bfloat16)
     acc = pltpu.VMEM((rows, columns), jnp.float32)
-    partial, panel, right, ahead = call(
+    partial, panel, right = call(
         square_early_kernel,
         [SCALARS] + [ANYWHERE] * 11,
         (where, own, pair, cross, *rights),
@@ -346,9 +320,8 @@
             wide,
             jax.ShapeDtypeStruct((3, rows + EXTRA, columns), jnp.bfloat16),
             jax.ShapeDtypeStruct((8, rows, columns), jnp.bfloat16),
-            jax.ShapeDtypeStruct((2, rows, columns), jnp.bfloat16),
         ),
-        [DMA((3,)), DMA((8,)), DMA(())],
+        [DMA((3,)), DMA((8,))],
         3 * flops,
         24 * size,
     )
@@ -356,16 +329,29 @@
     squared, sums, far = call(
         square_late_kernel,
         [SCALARS, WHOLE, WHOLE, WHOLE] + [ANYWHERE] * 2,
-        (where, own, partial, ahead, middle2, outer2),
+        (where, own, partial, right, middle2, outer2),
         (tile, jax.ShapeDtypeStruct((8, B), jnp.float32), extended),
         [DMA(())],
         flops,
         8 * size,
     )
     turns = [rotate(squared, 1), rotate(squared, 2)]
-    total = jnp.sum(sums)
+    total = sums
+
+    def add(left, right):
+        return call(
+            add_kernel,
+            [WHOLE] * 2,
+            (left, right),
+            jax.ShapeDtypeStruct(left.shape, left.dtype),
+            [],
+            left.size,
+            12 * left.size,
+            1,
+        )
+
     for k in (1, 4, 2):
-        total = total + swap(total, k)
+        total = add(total, swap(total, k))
     quarter = jax.ShapeDtypeStruct((rows, rows), jnp.bfloat16)
     turned = call(
         turn_kernel,
@@ -385,37 +371,35 @@
         [],
         4 * flops,
         9 * size,
-        48,
+        16,
     )
     cubic = call(
         cubic_early_kernel,
-        [SCALARS, WHOLE, WHOLE, AWAY],
+        [SCALARS] + [WHOLE] * 3,
         (where, squared, local_square, right),
         wide,
-        [pltpu.VMEM((2, 2, rows, columns), jnp.bfloat16), DMA((2,))],
+        [],
         2 * flops,
         8 * size,
-        48,
+        16,
     )
     for k in (2, 1):
-        total = total + lax.ppermute(total, "col", [(i, i ^ k) for i in range(4)])
+        total = add(total, lax.ppermute(total, "col", [(i, i ^ k) for i in range(4)]))
     purified = call(
         cubic_late_kernel,
-        [SCALARS] + [WHOLE] * 5 + [ANYWHERE] * 6 + [AWAY],
-        (where, own, squared, cubic, *turns, *sides, right),
+        [SCALARS] + [WHOLE] * 6 + [ANYWHERE] * 6,
+        (where, own, squared, cubic, *turns, right, *sides),
         wide,
         [
             pltpu.VMEM((3, rows, columns), jnp.bfloat16),
-            pltpu.VMEM((3, 2, rows, columns), jnp.bfloat16),
             acc,
-            DMA((3,)),
             DMA((3,)),
         ],
         3 * flops,
         16 * size,
-        48,
-    )
-    return (purified, total / (rows * lax.axis_size("row")))
+        16,
+    )
+    return (purified, total[0, 0] / (rows * lax.axis_size("row")))
 
 
 def solution(mesh):

time: 226 us -> 212 us (0.938)
  the two profiles are of different devices: /device:TPU:3 before, /device:TPU:2 now
where the time goes in v4:
time: 212 us; the launch traced here: 211 us
  waiting for transfers between devices  146 us (69%)
  starting transfers between devices  34.3 us (16%)
  Pallas kernels  23.3 us (11%)
  local copies, waits for them, and re-layouts  3.23 us (2%)
  between operations  2.69 us (1%)
    ppermute x12, waiting for transfers between devices, swap(): return lax.ppermute(x, 'row', [(i, i ^ k) for i in range(8)])  55.6 us
    ppermute x1, waiting for transfers between devices, local(): outer2 = lax.ppermute(cross, 'col', [(2, 3), (1, 0)])  26.3 us
    ppermute x1, waiting for transfers between devices, local(): cross = lax.ppermute(own, 'col', [(i, i ^ 3) for i in range(4)])  24 us
    pallas_call x11, Pallas kernels, call(): pl.pallas_call(kernel, out_shape=outs, in_specs=specs, out_specs=jax.tree...  23.3 us
    ppermute x2, waiting for transfers between devices, rotate(): return lax.ppermute(x, ('row', 'col'), pairs)  19.4 us
    ppermute x7, waiting for transfers between devices, in_plane(): return lax.ppermute(x, ('row', 'col'), pairs)  15.7 us
    ppermute x7, starting transfers between devices, in_plane(): return lax.ppermute(x, ('row', 'col'), pairs)  12.5 us
    ppermute x12, starting transfers between devices, swap(): return lax.ppermute(x, 'row', [(i, i ^ k) for i in range(8)])  7.37 us
  transfers between devices with their start and end apart: 27, of which 13 were waited for; matrix products, arithmetic and copies ran while one was open for 0% of the time, Pallas kernels for 6%

profile of v4, /device:TPU:2, one launch (start us, length us, event | category | flops | bytes accessed | tf_op | source)
XLA Modules:
  0.0 211.4 jit_solution(4261878339532414429)
XLA Ops:
  2.7 2.0 collective-permute-start.5
  4.7 22.9 %collective-permute-done.3.refs_2_ = bf16[512,1024]{1,0:T(8,128)(2,1)} collective-permute-done((bf16[512,1024]{1,0:T(8,128)(2,1)S(1)}, bf16[512,1024]{1,0:T(8,128)(2,1)}, u32[]{:S(2)}, u32[]{:S(2)}) %collective-permute-start.3) | collective-permute-done | bytes 1048608 | tf_op jit(solution)/shard_map/ppermute | solution.py:255
  31.0 2.5 %collective-permute-start.1 = (bf16[528,1024]{1,0:T(8,128)(2,1)S(1)}, bf16[528,1024]{1,0:T(8,128)(2,1)}, u32[]{:S(2)}, u32[]{:S(2)}) collective-permute-start(bf16[528,1024]{1,0:T(8,128)(2,1)S(1)} %fusion.2.own), channel_id=1, source_target_pairs={{0,3},{1,2},{2,1},{3,0},{4,7},{5,6},{6,5},{7,4},{8,11},{9,10},{10,... | collective-permute-start | bytes 3244040 | tf_op jit(solution)/shard_map/ppermute | solution.py:304
  35.0 17.1 %collective-permute-done.7.refs_6_ = bf16[512,1024]{1,0:T(8,128)(2,1)} collective-permute-done((bf16[512,1024]{1,0:T(8,128)(2,1)}, bf16[512,1024]{1,0:T(8,128)(2,1)}, u32[]{:S(2)}, u32[]{:S(2)}) %collective-permute-start.7) | collective-permute-done | bytes 1048608 | tf_op jit(solution)/shard_map/ppermute | solution.py:255
  52.1 3.1 %collective-permute-done.pair = bf16[528,1024]{1,0:T(8,128)(2,1)S(1)} collective-permute-done((bf16[528,1024]{1,0:T(8,128)(2,1)S(1)}, bf16[528,1024]{1,0:T(8,128)(2,1)S(1)}, u32[]{:S(2)}, u32[]{:S(2)}) %collective-permute-start) | collective-permute-done | bytes 1081376 | tf_op jit(solution)/shard_map/ppermute | solution.py:303
  55.3 24.0 %collective-permute-done.1.cross = bf16[528,1024]{1,0:T(8,128)(2,1)} collective-permute-done((bf16[528,1024]{1,0:T(8,128)(2,1)S(1)}, bf16[528,1024]{1,0:T(8,128)(2,1)}, u32[]{:S(2)}, u32[]{:S(2)}) %collective-permute-start.1) | collective-permute-done | bytes 1081376 | tf_op jit(solution)/shard_map/ppermute | solution.py:304
  80.5 6.3 %shard_map.41 = (f32[512,1024]{1,0:T(8,128)S(1)}, bf16[3,528,1024]{2,1,0:T(8,128)(2,1)S(1)}, bf16[8,512,1024]{2,1,0:T(8,128)(2,1)S(1)}) custom-call(s32[2]{0:T(128)S(1)} %pad_add_fusion.where, bf16[528,1024]{1,0:T(8,128)(2,1)S(1)} %fusion.2.own, bf16[528,1024]{1,0:T(8,128)(2,1)S(1)} %collective-permute-done.pair, ...), custom_call_target="tpu_custom_call" | custom-call | flops 3221225472 | bytes 25165824 | tf_op jit(solution)/shard_map/pallas_call | solution.py:243
  89.0 26.3 %collective-permute-done.10.outer2 = bf16[528,1024]{1,0:T(8,128)(2,1)S(1)} collective-permute-done((bf16[528,1024]{1,0:T(8,128)(2,1)}, bf16[528,1024]{1,0:T(8,128)(2,1)S(1)}, u32[]{:S(2)}, u32[]{:S(2)}) %collective-permute-start.10) | collective-permute-done | bytes 1081376 | tf_op jit(solution)/shard_map/ppermute | solution.py:306
  115.3 2.3 %shard_map.42 = (bf16[512,1024]{1,0:T(8,128)(2,1)S(1)}, f32[8,128]{1,0:T(8,128)S(1)}, bf16[528,1024]{1,0:T(8,128)(2,1)S(1)}) custom-call(s32[2]{0:T(128)S(1)} %pad_add_fusion.where, bf16[528,1024]{1,0:T(8,128)(2,1)S(1)} %fusion.2.own, f32[512,1024]{1,0:T(8,128)S(1)} %get-tuple-element.10.acc_in, bf16[8,512,1024]{2,1,0:T(8,128)(2,1)S(1)} %get-tuple-element.11.right.right_all, ...), custom_call_target="tpu_custom_call" | custom-call | flops 1073741824 | bytes 8388608 | tf_op jit(solution)/shard_map/pallas_call | solution.py:243
  122.2 2.5 %collective-permute-start.23 = (f32[8,128]{1,0:T(8,128)S(1)}, f32[8,128]{1,0:T(8,128)S(1)}, u32[]{:S(2)}, u32[]{:S(2)}) collective-permute-start(f32[8,128]{1,0:T(8,128)S(1)} %shard_map.47.left), channel_id=1, source_target_pairs={{0,16},{4,20},{8,24},{12,28},{16,0},{20,4},{24,8},{28,12},{1,17},{... | collective-permute-start | bytes 12296 | tf_op jit(solution)/shard_map/ppermute | solution.py:255
  124.7 11.1 %collective-permute-done.23.right = f32[8,128]{1,0:T(8,128)S(1)} collective-permute-done((f32[8,128]{1,0:T(8,128)S(1)}, f32[8,128]{1,0:T(8,128)S(1)}, u32[]{:S(2)}, u32[]{:S(2)}) %collective-permute-start.23) | collective-permute-done | bytes 4128 | tf_op jit(solution)/shard_map/ppermute | solution.py:255
  135.8 3.6 %collective-permute-done.24.right = f32[8,128]{1,0:T(8,128)S(1)} collective-permute-done((f32[8,128]{1,0:T(8,128)S(1)}, f32[8,128]{1,0:T(8,128)S(1)}, u32[]{:S(2)}, u32[]{:S(2)}) %collective-permute-start.24) | collective-permute-done | bytes 4128 | tf_op jit(solution)/shard_map/ppermute | solution.py:255
  139.4 2.5 %collective-permute-start.25 = (f32[8,128]{1,0:T(8,128)S(1)}, f32[8,128]{1,0:T(8,128)S(1)}, u32[]{:S(2)}, u32[]{:S(2)}) collective-permute-start(f32[8,128]{1,0:T(8,128)S(1)} %shard_map.49.left), channel_id=1, source_target_pairs={{0,2},{1,3},{2,0},{3,1},{4,6},{5,7},{6,4},{7,5},{8,10},{9,11},{10,... | collective-permute-start | bytes 12296 | tf_op jit(solution)/shard_map/ppermute | solution.py:387
  141.9 2.0 collective-permute-done.25.right
  143.9 2.0 collective-permute-start.26
  146.0 3.9 %collective-permute-start.15 = (bf16[512,512]{1,0:T(8,128)(2,1)S(1)}, bf16[512,512]{1,0:T(8,128)(2,1)S(1)}, u32[]{:S(2)}, u32[]{:S(2)}) collective-permute-start(bf16[512,512]{1,0:T(8,128)(2,1)S(1)} %get-tuple-element.15), channel_id=1, source_target_pairs={{8,0},{12,4},{1,9},{5,13},{26,18},{30,22},{19,27},{23,31}} | collective-permute-start | bytes 1572872 | tf_op jit(solution)/shard_map/ppermute | solution.py:284
  152.0 10.2 %collective-permute-done.15.refs_0_ = bf16[512,512]{1,0:T(8,128)(2,1)S(1)} collective-permute-done((bf16[512,512]{1,0:T(8,128)(2,1)S(1)}, bf16[512,512]{1,0:T(8,128)(2,1)S(1)}, u32[]{:S(2)}, u32[]{:S(2)}) %collective-permute-start.15) | collective-permute-done | bytes 524320 | tf_op jit(solution)/shard_map/ppermute | solution.py:284
  164.1 5.4 %collective-permute-done.16.refs_1_ = bf16[512,512]{1,0:T(8,128)(2,1)S(1)} collective-permute-done((bf16[512,512]{1,0:T(8,128)(2,1)S(1)}, bf16[512,512]{1,0:T(8,128)(2,1)S(1)}, u32[]{:S(2)}, u32[]{:S(2)}) %collective-permute-start.16) | collective-permute-done | bytes 524320 | tf_op jit(solution)/shard_map/ppermute | solution.py:284
  174.0 3.8 %collective-permute-start.21 = (bf16[512,512]{1,0:T(8,128)(2,1)S(1)}, bf16[512,512]{1,0:T(8,128)(2,1)S(1)}, u32[]{:S(2)}, u32[]{:S(2)}) collective-permute-start(bf16[512,512]{1,0:T(8,128)(2,1)S(1)} %collective-permute-done.20), channel_id=1, source_target_pairs={{8,4},{12,0},{1,13},{5,9},{26,22},{30,18},{19,31},{23,27}} | collective-permute-start | bytes 1572872 | tf_op jit(solution)/shard_map/ppermute | solution.py:284
  177.9 5.1 %shard_map.43.local_square = bf16[512,1024]{1,0:T(8,128)(2,1)S(1)} custom-call(s32[2]{0:T(128)S(1)} %pad_add_fusion.where, bf16[3,528,1024]{2,1,0:T(8,128)(2,1)S(1)} %get-tuple-element.13.panel, bf16[3,528,1024]{2,1,0:T(8,128)(2,1)S(1)} %collective-permute-done.11.other, bf16[528,1024]{1,0:T(8,128)(2,1)S(1)} %get-tuple-element.14.far, ...), custom_call_target="tpu_custom_call" | custom-call | flops 4294967296 | bytes 9437184 | tf_op jit(solution)/shard_map/pallas_call | solution.py:243
  183.0 3.2 %shard_map.44.acc_in = f32[512,1024]{1,0:T(8,128)S(1)} custom-call(s32[2]{0:T(128)S(1)} %pad_add_fusion.where, bf16[512,1024]{1,0:T(8,128)(2,1)S(1)} %get-tuple-element.12.squared, bf16[512,1024]{1,0:T(8,128)(2,1)S(1)} %shard_map.43.local_square, bf16[8,512,1024]{2,1,0:T(8,128)(2,1)S(1)} %get-tuple-element.11.right.right_all), custom_call_target="tpu_custom_call" | custom-call | flops 2147483648 | bytes 8388608 | tf_op jit(solution)/shard_map/pallas_call | solution.py:243
  186.3 5.7 %collective-permute-done.13.turn1 = bf16[512,1024]{1,0:T(8,128)(2,1)S(1)} collective-permute-done((bf16[512,1024]{1,0:T(8,128)(2,1)S(1)}, bf16[512,1024]{1,0:T(8,128)(2,1)S(1)}, u32[]{:S(2)}, u32[]{:S(2)}) %collective-permute-start.13) | collective-permute-done | bytes 1048608 | tf_op jit(solution)/shard_map/ppermute | solution.py:274
  191.9 13.8 %collective-permute-done.14.turn2 = bf16[512,1024]{1,0:T(8,128)(2,1)S(1)} collective-permute-done((bf16[512,1024]{1,0:T(8,128)(2,1)S(1)}, bf16[512,1024]{1,0:T(8,128)(2,1)S(1)}, u32[]{:S(2)}, u32[]{:S(2)}) %collective-permute-start.14) | collective-permute-done | bytes 1048608 | tf_op jit(solution)/shard_map/ppermute | solution.py:274
  205.7 4.6 %shard_map.46 = f32[512,1024]{1,0:T(8,128)} custom-call(s32[2]{0:T(128)S(1)} %pad_add_fusion.where, bf16[528,1024]{1,0:T(8,128)(2,1)S(1)} %fusion.2.own, bf16[512,1024]{1,0:T(8,128)(2,1)S(1)} %get-tuple-element.12.squared, f32[512,1024]{1,0:T(8,128)S(1)} %shard_map.44.acc_in, bf16[512,1024]{1,0:T(8,128)(2,1)S(1)} %collective-permute-done.13.turn1, ...), custom_call_target="tpu_custom_call" | custom-call | flops 3221225472 | bytes 16777216 | tf_op jit(solution)/shard_map/pallas_call | solution.py:243
  (55 shorter events, 22.6 us)
Async XLA Ops:
  2.6 25.1 %collective-permute-start.3 = (bf16[512,1024]{1,0:T(8,128)(2,1)S(1)}, bf16[512,1024]{1,0:T(8,128)(2,1)}, u32[]{:S(2)}, u32[]{:S(2)}) collective-permute-start(bf16[512,1024]{1,0:T(8,128)(2,1)S(1)} %fusion.1.refs_0_), channel_id=1, source_target_pairs={{0,8},{4,12},{8,0},{12,4},{16,24},{20,28},{24,16},{28,20},{1,9},{5... | collective-permute-start | bytes 3145736 | tf_op jit(solution)/shard_map/ppermute | solution.py:255
  2.7 30.8 %collective-permute-start.5 = (bf16[512,1024]{1,0:T(8,128)(2,1)S(1)}, bf16[512,1024]{1,0:T(8,128)(2,1)}, u32[]{:S(2)}, u32[]{:S(2)}) collective-permute-start(bf16[512,1024]{1,0:T(8,128)(2,1)S(1)} %fusion.1.refs_0_), channel_id=1, source_target_pairs={{0,16},{4,20},{8,24},{12,28},{16,0},{20,4},{24,8},{28,12},{1,17},{... | collective-permute-start | bytes 3145736 | tf_op jit(solution)/shard_map/ppermute | solution.py:255
  4.7 28.8 %collective-permute-start.2 = (bf16[512,1024]{1,0:T(8,128)(2,1)S(1)}, bf16[512,1024]{1,0:T(8,128)(2,1)S(1)}, u32[]{:S(2)}, u32[]{:S(2)}) collective-permute-start(bf16[512,1024]{1,0:T(8,128)(2,1)S(1)} %fusion.1.refs_0_), channel_id=1, source_target_pairs={{0,4},{4,0},{8,12},{12,8},{16,20},{20,16},{24,28},{28,24},{1,5},{5... | collective-permute-start | bytes 3145736 | tf_op jit(solution)/shard_map/ppermute | solution.py:255
  27.7 24.4 %collective-permute-start.7 = (bf16[512,1024]{1,0:T(8,128)(2,1)}, bf16[512,1024]{1,0:T(8,128)(2,1)}, u32[]{:S(2)}, u32[]{:S(2)}) collective-permute-start(bf16[512,1024]{1,0:T(8,128)(2,1)} %collective-permute-done.3.refs_2_), channel_id=1, source_target_pairs={{0,16},{4,20},{8,24},{12,28},{16,0},{20,4},{24,8},{28,12},{1,17},{... | collective-permute-start | bytes 3145736 | tf_op jit(solution)/shard_map/ppermute | solution.py:255
  29.4 25.9 %collective-permute-start = (bf16[528,1024]{1,0:T(8,128)(2,1)S(1)}, bf16[528,1024]{1,0:T(8,128)(2,1)S(1)}, u32[]{:S(2)}, u32[]{:S(2)}) collective-permute-start(bf16[528,1024]{1,0:T(8,128)(2,1)S(1)} %fusion.2.own), channel_id=1, source_target_pairs={{0,1},{1,0},{2,3},{3,2},{4,5},{5,4},{6,7},{7,6},{8,9},{9,8},{10,11... | collective-permute-start | bytes 3244040 | tf_op jit(solution)/shard_map/ppermute | solution.py:303
  31.0 48.3 %collective-permute-start.1 = (bf16[528,1024]{1,0:T(8,128)(2,1)S(1)}, bf16[528,1024]{1,0:T(8,128)(2,1)}, u32[]{:S(2)}, u32[]{:S(2)}) collective-permute-start(bf16[528,1024]{1,0:T(8,128)(2,1)S(1)} %fusion.2.own), channel_id=1, source_target_pairs={{0,3},{1,2},{2,1},{3,0},{4,7},{5,6},{6,5},{7,4},{8,11},{9,10},{10,... | collective-permute-start | bytes 3244040 | tf_op jit(solution)/shard_map/ppermute | solution.py:304
  33.5 45.8 %collective-permute-start.4 = (bf16[512,1024]{1,0:T(8,128)(2,1)}, bf16[512,1024]{1,0:T(8,128)(2,1)}, u32[]{:S(2)}, u32[]{:S(2)}) collective-permute-start(bf16[512,1024]{1,0:T(8,128)(2,1)} %collective-permute-done.3.refs_2_), channel_id=1, source_target_pairs={{0,4},{4,0},{8,12},{12,8},{16,20},{20,16},{24,28},{28,24},{1,5},{5... | collective-permute-start | bytes 3145736 | tf_op jit(solution)/shard_map/ppermute | solution.py:255
  34.5 44.8 %collective-permute-start.6 = (bf16[512,1024]{1,0:T(8,128)(2,1)}, bf16[512,1024]{1,0:T(8,128)(2,1)}, u32[]{:S(2)}, u32[]{:S(2)}) collective-permute-start(bf16[512,1024]{1,0:T(8,128)(2,1)} %collective-permute-done.5.refs_4_), channel_id=1, source_target_pairs={{0,4},{4,0},{8,12},{12,8},{16,20},{20,16},{24,28},{28,24},{1,5},{5... | collective-permute-start | bytes 3145736 | tf_op jit(solution)/shard_map/ppermute | solution.py:255
  52.0 27.3 %collective-permute-start.8 = (bf16[512,1024]{1,0:T(8,128)(2,1)}, bf16[512,1024]{1,0:T(8,128)(2,1)}, u32[]{:S(2)}, u32[]{:S(2)}) collective-permute-start(bf16[512,1024]{1,0:T(8,128)(2,1)} %collective-permute-done.7.refs_6_), channel_id=1, source_target_pairs={{0,4},{4,0},{8,12},{12,8},{16,20},{20,16},{24,28},{28,24},{1,5},{5... | collective-permute-start | bytes 3145736 | tf_op jit(solution)/shard_map/ppermute | solution.py:255
  86.9 87.2 %collective-permute-start.11 = (bf16[3,528,1024]{2,1,0:T(8,128)(2,1)S(1)}, bf16[3,528,1024]{2,1,0:T(8,128)(2,1)S(1)}, u32[]{:S(2)}, u32[]{:S(2)}) collective-permute-start(bf16[3,528,1024]{2,1,0:T(8,128)(2,1)S(1)} %get-tuple-element.13.panel), channel_id=1, source_target_pairs={{0,4},{4,0},{8,12},{12,8},{16,20},{20,16},{24,28},{28,24},{1,5},{5... | collective-permute-start | bytes 9732104 | tf_op jit(solution)/shard_map/ppermute | solution.py:255
  86.9 28.4 %collective-permute-start.10 = (bf16[528,1024]{1,0:T(8,128)(2,1)}, bf16[528,1024]{1,0:T(8,128)(2,1)S(1)}, u32[]{:S(2)}, u32[]{:S(2)}) collective-permute-start(bf16[528,1024]{1,0:T(8,128)(2,1)} %collective-permute-done.1.cross), channel_id=1, source_target_pairs={{2,3},{1,0},{6,7},{5,4},{10,11},{9,8},{14,15},{13,12},{18,19},{17,... | collective-permute-start | bytes 3244040 | tf_op jit(solution)/shard_map/ppermute | solution.py:306
  88.2 27.1 %collective-permute-start.9 = (bf16[528,1024]{1,0:T(8,128)(2,1)S(1)}, bf16[528,1024]{1,0:T(8,128)(2,1)S(1)}, u32[]{:S(2)}, u32[]{:S(2)}) collective-permute-start(bf16[528,1024]{1,0:T(8,128)(2,1)S(1)} %collective-permute-done.pair), channel_id=1, source_target_pairs={{1,2},{2,1},{5,6},{6,5},{9,10},{10,9},{13,14},{14,13},{17,18},{18,... | collective-permute-start | bytes 3244040 | tf_op jit(solution)/shard_map/ppermute | solution.py:305
  117.6 55.7 %collective-permute-start.12 = (bf16[528,1024]{1,0:T(8,128)(2,1)S(1)}, bf16[528,1024]{1,0:T(8,128)(2,1)S(1)}, u32[]{:S(2)}, u32[]{:S(2)}) collective-permute-start(bf16[528,1024]{1,0:T(8,128)(2,1)S(1)} %get-tuple-element.14.far), channel_id=1, source_target_pairs={{0,4},{4,0},{8,12},{12,8},{16,20},{20,16},{24,28},{28,24},{1,5},{5... | collective-permute-start | bytes 3244040 | tf_op jit(solution)/shard_map/ppermute | solution.py:255
  119.5 31.8 %collective-permute-start.20 = (bf16[512,512]{1,0:T(8,128)(2,1)S(1)}, bf16[512,512]{1,0:T(8,128)(2,1)S(1)}, u32[]{:S(2)}, u32[]{:S(2)}) collective-permute-start(bf16[512,512]{1,0:T(8,128)(2,1)S(1)} %get-tuple-element.16), channel_id=1, source_target_pairs={{24,8},{28,12},{17,1},{21,5},{10,26},{14,30},{3,19},{7,23}} | collective-permute-start | bytes 1572872 | tf_op jit(solution)/shard_map/ppermute | solution.py:284
  122.2 13.6 %collective-permute-start.23 = (f32[8,128]{1,0:T(8,128)S(1)}, f32[8,128]{1,0:T(8,128)S(1)}, u32[]{:S(2)}, u32[]{:S(2)}) collective-permute-start(f32[8,128]{1,0:T(8,128)S(1)} %shard_map.47.left), channel_id=1, source_target_pairs={{0,16},{4,20},{8,24},{12,28},{16,0},{20,4},{24,8},{28,12},{1,17},{... | collective-permute-start | bytes 12296 | tf_op jit(solution)/shard_map/ppermute | solution.py:255
  143.9 6.0 %collective-permute-start.26 = (f32[8,128]{1,0:T(8,128)S(1)}, f32[8,128]{1,0:T(8,128)S(1)}, u32[]{:S(2)}, u32[]{:S(2)}) collective-permute-start(f32[8,128]{1,0:T(8,128)S(1)} %shard_map.50.left), channel_id=1, source_target_pairs={{0,1},{1,0},{2,3},{3,2},{4,5},{5,4},{6,7},{7,6},{8,9},{9,8},{10,11... | collective-permute-start | bytes 12296 | tf_op jit(solution)/shard_map/ppermute | solution.py:387
  146.0 16.2 %collective-permute-start.15 = (bf16[512,512]{1,0:T(8,128)(2,1)S(1)}, bf16[512,512]{1,0:T(8,128)(2,1)S(1)}, u32[]{:S(2)}, u32[]{:S(2)}) collective-permute-start(bf16[512,512]{1,0:T(8,128)(2,1)S(1)} %get-tuple-element.15), channel_id=1, source_target_pairs={{8,0},{12,4},{1,9},{5,13},{26,18},{30,22},{19,27},{23,31}} | collective-permute-start | bytes 1572872 | tf_op jit(solution)/shard_map/ppermute | solution.py:284
  149.9 19.6 %collective-permute-start.16 = (bf16[512,512]{1,0:T(8,128)(2,1)S(1)}, bf16[512,512]{1,0:T(8,128)(2,1)S(1)}, u32[]{:S(2)}, u32[]{:S(2)}) collective-permute-start(bf16[512,512]{1,0:T(8,128)(2,1)S(1)} %get-tuple-element.16), channel_id=1, source_target_pairs={{8,4},{12,0},{1,13},{5,9},{26,22},{30,18},{19,31},{23,27}} | collective-permute-start | bytes 1572872 | tf_op jit(solution)/shard_map/ppermute | solution.py:284
  151.3 21.3 %collective-permute-start.17 = (bf16[512,512]{1,0:T(8,128)(2,1)S(1)}, bf16[512,512]{1,0:T(8,128)(2,1)S(1)}, u32[]{:S(2)}, u32[]{:S(2)}) collective-permute-start(bf16[512,512]{1,0:T(8,128)(2,1)S(1)} %get-tuple-element.15), channel_id=1, source_target_pairs={{16,0},{20,4},{25,9},{29,13},{2,18},{6,22},{11,27},{15,31}} | collective-permute-start | bytes 1572872 | tf_op jit(solution)/shard_map/ppermute | solution.py:284
  162.2 29.8 %collective-permute-start.13 = (bf16[512,1024]{1,0:T(8,128)(2,1)S(1)}, bf16[512,1024]{1,0:T(8,128)(2,1)S(1)}, u32[]{:S(2)}, u32[]{:S(2)}) collective-permute-start(bf16[512,1024]{1,0:T(8,128)(2,1)S(1)} %get-tuple-element.12.squared), channel_id=1, source_target_pairs={{1,2},{2,3},{3,1},{5,6},{6,7},{7,5},{8,10},{10,11},{11,8},{12,14},... | collective-permute-start | bytes 3145736 | tf_op jit(solution)/shard_map/ppermute | solution.py:274
  169.5 36.2 %collective-permute-start.14 = (bf16[512,1024]{1,0:T(8,128)(2,1)S(1)}, bf16[512,1024]{1,0:T(8,128)(2,1)S(1)}, u32[]{:S(2)}, u32[]{:S(2)}) collective-permute-start(bf16[512,1024]{1,0:T(8,128)(2,1)S(1)} %get-tuple-element.12.squared), channel_id=1, source_target_pairs={{1,3},{2,1},{3,2},{5,7},{6,5},{7,6},{8,11},{10,8},{11,10},{12,15},... | collective-permute-start | bytes 3145736 | tf_op jit(solution)/shard_map/ppermute | solution.py:274
  172.6 13.6 %collective-permute-start.18 = (bf16[512,512]{1,0:T(8,128)(2,1)S(1)}, bf16[512,512]{1,0:T(8,128)(2,1)S(1)}, u32[]{:S(2)}, u32[]{:S(2)}) collective-permute-start(bf16[512,512]{1,0:T(8,128)(2,1)S(1)} %get-tuple-element.16), channel_id=1, source_target_pairs={{16,4},{20,0},{25,13},{29,9},{2,22},{6,18},{11,31},{15,27}} | collective-permute-start | bytes 1572872 | tf_op jit(solution)/shard_map/ppermute | solution.py:284
  173.3 12.9 %collective-permute-start.19 = (bf16[512,512]{1,0:T(8,128)(2,1)S(1)}, bf16[512,512]{1,0:T(8,128)(2,1)S(1)}, u32[]{:S(2)}, u32[]{:S(2)}) collective-permute-start(bf16[512,512]{1,0:T(8,128)(2,1)S(1)} %get-tuple-element.15), channel_id=1, source_target_pairs={{24,0},{28,4},{17,9},{21,13},{10,18},{14,22},{3,27},{7,31}} | collective-permute-start | bytes 1572872 | tf_op jit(solution)/shard_map/ppermute | solution.py:284
  174.0 12.2 %collective-permute-start.21 = (bf16[512,512]{1,0:T(8,128)(2,1)S(1)}, bf16[512,512]{1,0:T(8,128)(2,1)S(1)}, u32[]{:S(2)}, u32[]{:S(2)}) collective-permute-start(bf16[512,512]{1,0:T(8,128)(2,1)S(1)} %collective-permute-done.20), channel_id=1, source_target_pairs={{8,4},{12,0},{1,13},{5,9},{26,22},{30,18},{19,31},{23,27}} | collective-permute-start | bytes 1572872 | tf_op jit(solution)/shard_map/ppermute | solution.py:284
  (6 other events, 13.0 us)

commit v5 on v4

--- a/solution.py
+++ b/solution.py
@@ -95,21 +95,9 @@
         pltpu.make_async_copy(there, there, right_sem.at[slot + t]).wait()
 
 
-def square_late_kernel(where, own, acc_in, right, middle2, outer2, *refs):
-    squared_ref, sum_ref, far, left_sem = refs
+def square_late_kernel(where, own, acc_in, right, far, squared_ref, sum_ref):
     row, col = where[0], where[1]
     rows, columns = squared_ref.shape
-    inner = (col == 1) | (col == 2)
-
-    @pl.when(inner)
-    def _():
-        pltpu.make_async_copy(middle2, far, left_sem).start()
-
-    @pl.when(jnp.logical_not(inner))
-    def _():
-        pltpu.make_async_copy(outer2, far, left_sem).start()
-
-    pltpu.make_async_copy(far, far, left_sem).wait()
     total = acc_in[...] + piece(far, right.at[pl.ds(2 * (col ^ LAST), 2)])
     kept = own[rows : rows + EXTRA, :].astype(jnp.float32)
     sums = jnp.zeros((8, columns), jnp.float32)
@@ -198,39 +186,54 @@
         multiply(acc, local_square, right.at[pl.ds(2 * chip, 2)], False)
 
 
-def cubic_late_kernel(where, own, squared, acc_in, turn1, turn2, right_all, *refs):
-    sides = refs[:6]
-    purified_ref, left, acc, sem = refs[6:]
+def side_piece(sides, right_all, source, core):
+    return sum(
+        jnp.dot(ref[...], right_all[2 * source + (core ^ u)], preferred_element_type=jnp.float32)
+        for u, ref in enumerate(sides)
+    )
+
+
+def cubic_middle_kernel(where, acc_in, right_all, same, cross, acc):
+    row, col = where[0], where[1]
+
+    @pl.when(row // 2 == col)
+    def _():
+        acc[...] = acc_in[...] + side_piece((same, cross), right_all, col ^ 2, row % 2)
+
+    @pl.when(row // 2 != col)
+    def _():
+        acc[...] = acc_in[...]
+
+
+def cubic_late_kernel(where, own, squared, acc, turn1, turn2, right_all, *refs):
+    sides, purified_ref, scratch = refs[:4], refs[4], refs[5]
     row, col = where[0], where[1]
     core, chip = row % 2, row // 2
     rows, _ = squared.shape
-    corner = chip == col
-    rights = [right_all.at[pl.ds(2 * source, 2)] for source in late_sources(row, col)]
-
-    def finish(last):
-        total = acc_in[...] + acc[...] + piece(last, rights[1])
+    sources = late_sources(row, col)
+
+    def finish(first, second):
+        scratch[...] = acc[...] + first
+        total = scratch[...] + second()
         kept = own[rows : rows + EXTRA, :].astype(jnp.float32)
         for a in range(rows // B):
             part = slice(a * B, (a + 1) * B)
             wide = squared[part, :].astype(jnp.float32)
             purified_ref[part, :] = 3.0 * wide - 2.0 * (total[part] * kept[a : a + 1])
 
-    @pl.when(jnp.logical_not(corner))
-    def _():
-        multiply(acc, turn1, rights[0], True)
-        finish(turn2)
-
-    @pl.when(corner)
-    def _():
-        for i in range(3):
-            for u in range(2):
-                lanes = pl.ds(pl.multiple_of((core ^ u) * rows, rows), rows)
-                pltpu.make_async_copy(sides[2 * i + u], left.at[i, :, lanes], sem.at[i]).start()
-        for i in (0, 2, 1):
-            pltpu.make_async_copy(left.at[i], left.at[i], sem.at[i]).wait()
-            if i != 1:
-                multiply(acc, left.at[i], rights[i], i == 0)
-        finish(left.at[1])
+    @pl.when(chip != col)
+    def _():
+        finish(
+            piece(turn1, right_all.at[pl.ds(2 * sources[0], 2)]),
+            lambda: piece(turn2, right_all.at[pl.ds(2 * sources[1], 2)]),
+        )
+
+    @pl.when(chip == col)
+    def _():
+        finish(
+            side_piece(sides[:2], right_all, col ^ 1, core),
+            lambda: side_piece(sides[2:], right_all, col ^ 3, core),
+        )
 
 
 ANYWHERE = pl.BlockSpec(memory_space=pl.ANY)
@@ -300,18 +303,15 @@
     kept = jnp.repeat(pattern.astype(jnp.bfloat16), B, axis=1)
     kept = jnp.pad(kept, ((0, EXTRA - kept.shape[0]), (0, 0)))
     own = jnp.concatenate([masked, kept], axis=0)
+    cross = lax.ppermute(own, "col", [(i, i ^ 3) for i in range(4)])
     pair = lax.ppermute(own, "col", [(i, i ^ 1) for i in range(4)])
-    cross = lax.ppermute(own, "col", [(i, i ^ 3) for i in range(4)])
-    middle2 = lax.ppermute(pair, "col", [(1, 2), (2, 1)])
-    outer2 = lax.ppermute(cross, "col", [(2, 3), (1, 0)])
+    far = lax.ppermute(cross, "col", [(i, i ^ 1) for i in range(4)])
     rights = column_gather(masked)
 
     flops = 2 * 2 * rows * rows * columns
     size = 2 * rows * columns
     tile = jax.ShapeDtypeStruct((rows, columns), jnp.bfloat16)
     wide = jax.ShapeDtypeStruct((rows, columns), jnp.float32)
-    extended = jax.ShapeDtypeStruct((rows + EXTRA, columns), jnp.bfloat16)
-    acc = pltpu.VMEM((rows, columns), jnp.float32)
     partial, panel, right = call(
         square_early_kernel,
         [SCALARS] + [ANYWHERE] * 11,
@@ -326,12 +326,12 @@
         24 * size,
     )
     other = swap(panel, 1)
-    squared, sums, far = call(
+    squared, sums = call(
         square_late_kernel,
-        [SCALARS, WHOLE, WHOLE, WHOLE] + [ANYWHERE] * 2,
-        (where, own, partial, right, middle2, outer2),
-        (tile, jax.ShapeDtypeStruct((8, B), jnp.float32), extended),
-        [DMA(())],
+        [SCALARS] + [WHOLE] * 4,
+        (where, own, partial, right, far),
+        (tile, jax.ShapeDtypeStruct((8, B), jnp.float32)),
+        [],
         flops,
         8 * size,
     )
@@ -350,7 +350,7 @@
             1,
         )
 
-    for k in (1, 4, 2):
+    for k in (1, 2, 4):
         total = add(total, swap(total, k))
     quarter = jax.ShapeDtypeStruct((rows, rows), jnp.bfloat16)
     turned = call(
@@ -383,21 +383,25 @@
         8 * size,
         16,
     )
+    cubic = call(
+        cubic_middle_kernel,
+        [SCALARS] + [WHOLE] * 4,
+        (where, cubic, right, *sides[2:4]),
+        wide,
+        [],
+        flops,
+        9 * size,
+    )
     for k in (2, 1):
         total = add(total, lax.ppermute(total, "col", [(i, i ^ k) for i in range(4)]))
     purified = call(
         cubic_late_kernel,
-        [SCALARS] + [WHOLE] * 6 + [ANYWHERE] * 6,
-        (where, own, squared, cubic, *turns, right, *sides),
+        [SCALARS] + [WHOLE] * 10,
+        (where, own, squared, cubic, *turns, right, *sides[:2], *sides[4:]),
         wide,
-        [
-            pltpu.VMEM((3, rows, columns), jnp.bfloat16),
-            acc,
-            DMA((3,)),
-        ],
-        3 * flops,
+        [pltpu.VMEM((rows, columns), jnp.float32)],
+        2 * flops,
         16 * size,
-        16,
     )
     return (purified, total[0, 0] / (rows * lax.axis_size("row")))
 

time: 212 us -> 210 us (level)
  the two profiles are of different devices: /device:TPU:2 before, /device:TPU:3 now
where the time goes in v5:
time: 210 us
  waiting for transfers between devices  119 us (57%)
  starting transfers between devices  59.8 us (28%)
  Pallas kernels  23.6 us (11%)
  local copies, waits for them, and re-layouts  3.24 us (2%)
  between operations  2.66 us (1%)
    ppermute x12, waiting for transfers between devices, swap(): return lax.ppermute(x, 'row', [(i, i ^ k) for i in range(8)])  40.2 us
    ppermute x1, waiting for transfers between devices, local(): pair = lax.ppermute(own, 'col', [(i, i ^ 1) for i in range(4)])  25.4 us
    ppermute x1, waiting for transfers between devices, local(): far = lax.ppermute(cross, 'col', [(i, i ^ 1) for i in range(4)])  25 us
    pallas_call x12, Pallas kernels, call(): pl.pallas_call(kernel, out_shape=outs, in_specs=specs, out_specs=jax.tree...  23.6 us
    ppermute x2, waiting for transfers between devices, rotate(): return lax.ppermute(x, ('row', 'col'), pairs)  19.8 us
    ppermute x2, starting transfers between devices, local(): lax.ppermute(total, 'col', [(i, i ^ k) for i in range(4)])  19.7 us
    ppermute x7, starting transfers between devices, in_plane(): return lax.ppermute(x, ('row', 'col'), pairs)  15.6 us
    ppermute x12, starting transfers between devices, swap(): return lax.ppermute(x, 'row', [(i, i ^ k) for i in range(8)])  13.6 us
  transfers between devices with their start and end apart: 26, of which 13 were waited for; matrix products, arithmetic and copies ran while one was open for 0% of the time, Pallas kernels for 6%

profile of v5, /device:TPU:3, one launch (start us, length us, event | category | flops | bytes accessed | tf_op | source)
XLA Modules:
  0.0 209.7 jit_solution(7099313358140208164)
XLA Ops:
  2.7 1.5 collective-permute-start.5
  5.4 21.4 %collective-permute-done.3.refs_2_ = bf16[512,1024]{1,0:T(8,128)(2,1)} collective-permute-done((bf16[512,1024]{1,0:T(8,128)(2,1)S(1)}, bf16[512,1024]{1,0:T(8,128)(2,1)}, u32[]{:S(2)}, u32[]{:S(2)}) %collective-permute-start.3) | collective-permute-done | bytes 1048608 | tf_op jit(solution)/shard_map/ppermute | solution.py:258
  28.2 3.4 %collective-permute-start.1 = (bf16[528,1024]{1,0:T(8,128)(2,1)S(1)}, bf16[528,1024]{1,0:T(8,128)(2,1)S(1)}, u32[]{:S(2)}, u32[]{:S(2)}) collective-permute-start(bf16[528,1024]{1,0:T(8,128)(2,1)S(1)} %fusion.2.own), channel_id=1, source_target_pairs={{0,3},{1,2},{2,1},{3,0},{4,7},{5,6},{6,5},{7,4},{8,11},{9,10},{10,... | collective-permute-start | bytes 3244040 | tf_op jit(solution)/shard_map/ppermute | solution.py:306
  31.6 2.1 collective-permute-start.4
  34.7 15.6 %collective-permute-done.7.refs_6_ = bf16[512,1024]{1,0:T(8,128)(2,1)} collective-permute-done((bf16[512,1024]{1,0:T(8,128)(2,1)}, bf16[512,1024]{1,0:T(8,128)(2,1)}, u32[]{:S(2)}, u32[]{:S(2)}) %collective-permute-start.7) | collective-permute-done | bytes 1048608 | tf_op jit(solution)/shard_map/ppermute | solution.py:258
  50.3 2.4 %collective-permute-start.8 = (bf16[512,1024]{1,0:T(8,128)(2,1)}, bf16[512,1024]{1,0:T(8,128)(2,1)}, u32[]{:S(2)}, u32[]{:S(2)}) collective-permute-start(bf16[512,1024]{1,0:T(8,128)(2,1)} %collective-permute-done.7.refs_6_), channel_id=1, source_target_pairs={{0,4},{4,0},{8,12},{12,8},{16,20},{20,16},{24,28},{28,24},{1,5},{5... | collective-permute-start | bytes 3145736 | tf_op jit(solution)/shard_map/ppermute | solution.py:258
  54.0 25.4 %collective-permute-done.pair = bf16[528,1024]{1,0:T(8,128)(2,1)} collective-permute-done((bf16[528,1024]{1,0:T(8,128)(2,1)S(1)}, bf16[528,1024]{1,0:T(8,128)(2,1)}, u32[]{:S(2)}, u32[]{:S(2)}) %collective-permute-start) | collective-permute-done | bytes 1081376 | tf_op jit(solution)/shard_map/ppermute | solution.py:307
  80.6 6.2 %shard_map.41 = (f32[512,1024]{1,0:T(8,128)S(1)}, bf16[3,528,1024]{2,1,0:T(8,128)(2,1)S(1)}, bf16[8,512,1024]{2,1,0:T(8,128)(2,1)S(1)}) custom-call(s32[2]{0:T(128)S(1)} %pad_add_fusion.where, bf16[528,1024]{1,0:T(8,128)(2,1)S(1)} %fusion.2.own, bf16[528,1024]{1,0:T(8,128)(2,1)} %collective-permute-done.pair, ...), custom_call_target="tpu_custom_call" | custom-call | flops 3221225472 | bytes 25165824 | tf_op jit(solution)/shard_map/pallas_call | solution.py:246
  87.7 25.0 %collective-permute-done.9.far = bf16[528,1024]{1,0:T(8,128)(2,1)S(1)} collective-permute-done((bf16[528,1024]{1,0:T(8,128)(2,1)S(1)}, bf16[528,1024]{1,0:T(8,128)(2,1)S(1)}, u32[]{:S(2)}, u32[]{:S(2)}) %collective-permute-start.9) | collective-permute-done | bytes 1081376 | tf_op jit(solution)/shard_map/ppermute | solution.py:308
  113.6 2.2 %shard_map.42 = (bf16[512,1024]{1,0:T(8,128)(2,1)S(1)}, f32[8,128]{1,0:T(8,128)S(1)}) custom-call(s32[2]{0:T(128)S(1)} %pad_add_fusion.where, bf16[528,1024]{1,0:T(8,128)(2,1)S(1)} %fusion.2.own, f32[512,1024]{1,0:T(8,128)S(1)} %get-tuple-element.9.acc_in, bf16[8,512,1024]{2,1,0:T(8,128)(2,1)S(1)} %get-tuple-element.10.right.right_all, ...), custom_call_target="tpu_custom_call" | custom-call | flops 1073741824 | bytes 8388608 | tf_op jit(solution)/shard_map/pallas_call | solution.py:246
  115.8 1.8 shard_map.45
  120.3 1.4 collective-permute-start.22
  122.8 2.1 %collective-permute-start.23 = (f32[8,128]{1,0:T(8,128)S(1)}, f32[8,128]{1,0:T(8,128)S(1)}, u32[]{:S(2)}, u32[]{:S(2)}) collective-permute-start(f32[8,128]{1,0:T(8,128)S(1)} %shard_map.49.left), channel_id=1, source_target_pairs={{0,16},{4,20},{8,24},{12,28},{16,0},{20,4},{24,8},{28,12},{1,17},{... | collective-permute-start | bytes 12296 | tf_op jit(solution)/shard_map/ppermute | solution.py:258
  126.8 2.5 %collective-permute-done.24.right = f32[8,128]{1,0:T(8,128)S(1)} collective-permute-done((f32[8,128]{1,0:T(8,128)S(1)}, f32[8,128]{1,0:T(8,128)S(1)}, u32[]{:S(2)}, u32[]{:S(2)}) %collective-permute-start.24) | collective-permute-done | bytes 4128 | tf_op jit(solution)/shard_map/ppermute | solution.py:396
  129.2 18.8 %collective-permute-start.25 = (f32[8,128]{1,0:T(8,128)S(1)}, f32[8,128]{1,0:T(8,128)S(1)}, u32[]{:S(2)}, u32[]{:S(2)}) collective-permute-start(f32[8,128]{1,0:T(8,128)S(1)} %shard_map.51.left), channel_id=1, source_target_pairs={{0,1},{1,0},{2,3},{3,2},{4,5},{5,4},{6,7},{7,6},{8,9},{9,8},{10,11... | collective-permute-start | bytes 12296 | tf_op jit(solution)/shard_map/ppermute | solution.py:396
  150.3 2.6 %collective-permute-start.16 = (bf16[512,512]{1,0:T(8,128)(2,1)S(1)}, bf16[512,512]{1,0:T(8,128)(2,1)S(1)}, u32[]{:S(2)}, u32[]{:S(2)}) collective-permute-start(bf16[512,512]{1,0:T(8,128)(2,1)S(1)} %get-tuple-element.13), channel_id=1, source_target_pairs={{8,0},{12,4},{1,9},{5,13},{26,18},{30,22},{19,27},{23,31}} | collective-permute-start | bytes 1572872 | tf_op jit(solution)/shard_map/ppermute | solution.py:287
  153.0 2.2 %collective-permute-start.14 = (bf16[512,1024]{1,0:T(8,128)(2,1)S(1)}, bf16[512,1024]{1,0:T(8,128)(2,1)S(1)}, u32[]{:S(2)}, u32[]{:S(2)}) collective-permute-start(bf16[512,1024]{1,0:T(8,128)(2,1)S(1)} %get-tuple-element.11.squared), channel_id=1, source_target_pairs={{1,2},{2,3},{3,1},{5,6},{6,7},{7,5},{8,10},{10,11},{11,8},{12,14},... | collective-permute-start | bytes 3145736 | tf_op jit(solution)/shard_map/ppermute | solution.py:277
  155.2 4.8 %collective-permute-start.15 = (bf16[512,1024]{1,0:T(8,128)(2,1)S(1)}, bf16[512,1024]{1,0:T(8,128)(2,1)S(1)}, u32[]{:S(2)}, u32[]{:S(2)}) collective-permute-start(bf16[512,1024]{1,0:T(8,128)(2,1)S(1)} %get-tuple-element.11.squared), channel_id=1, source_target_pairs={{1,3},{2,1},{3,2},{5,7},{6,5},{7,6},{8,11},{10,8},{11,10},{12,15},... | collective-permute-start | bytes 3145736 | tf_op jit(solution)/shard_map/ppermute | solution.py:277
  163.5 8.3 %collective-permute-start.20 = (bf16[512,512]{1,0:T(8,128)(2,1)S(1)}, bf16[512,512]{1,0:T(8,128)(2,1)S(1)}, u32[]{:S(2)}, u32[]{:S(2)}) collective-permute-start(bf16[512,512]{1,0:T(8,128)(2,1)S(1)} %collective-permute-done.19), channel_id=1, source_target_pairs={{8,4},{12,0},{1,13},{5,9},{26,22},{30,18},{19,31},{23,27}} | collective-permute-start | bytes 1572872 | tf_op jit(solution)/shard_map/ppermute | solution.py:287
  171.8 5.1 %shard_map.43.local_square = bf16[512,1024]{1,0:T(8,128)(2,1)S(1)} custom-call(s32[2]{0:T(128)S(1)} %pad_add_fusion.where, bf16[3,528,1024]{2,1,0:T(8,128)(2,1)S(1)} %get-tuple-element.12.panel, bf16[3,528,1024]{2,1,0:T(8,128)(2,1)S(1)} %collective-permute-done.10.other, bf16[528,1024]{1,0:T(8,128)(2,1)S(1)} %collective-permute-done.9.far, ...), custom_call_target="tpu_custom_call" | custom-call | flops 4294967296 | bytes 9437184 | tf_op jit(solution)/shard_map/pallas_call | solution.py:246
  176.9 3.2 %shard_map.44.acc_in = f32[512,1024]{1,0:T(8,128)S(1)} custom-call(s32[2]{0:T(128)S(1)} %pad_add_fusion.where, bf16[512,1024]{1,0:T(8,128)(2,1)S(1)} %get-tuple-element.11.squared, bf16[512,1024]{1,0:T(8,128)(2,1)S(1)} %shard_map.43.local_square, bf16[8,512,1024]{2,1,0:T(8,128)(2,1)S(1)} %get-tuple-element.10.right.right_all), custom_call_target="tpu_custom_call" | custom-call | flops 2147483648 | bytes 8388608 | tf_op jit(solution)/shard_map/pallas_call | solution.py:246
  180.8 3.6 %collective-permute-done.20.refs_3_ = bf16[512,512]{1,0:T(8,128)(2,1)S(1)} collective-permute-done((bf16[512,512]{1,0:T(8,128)(2,1)S(1)}, bf16[512,512]{1,0:T(8,128)(2,1)S(1)}, u32[]{:S(2)}, u32[]{:S(2)}) %collective-permute-start.20) | collective-permute-done | bytes 524320 | tf_op jit(solution)/shard_map/ppermute | solution.py:287
  184.5 19.8 %collective-permute-done.15.turn2 = bf16[512,1024]{1,0:T(8,128)(2,1)S(1)} collective-permute-done((bf16[512,1024]{1,0:T(8,128)(2,1)S(1)}, bf16[512,1024]{1,0:T(8,128)(2,1)S(1)}, u32[]{:S(2)}, u32[]{:S(2)}) %collective-permute-start.15) | collective-permute-done | bytes 1048608 | tf_op jit(solution)/shard_map/ppermute | solution.py:277
  204.2 4.3 %shard_map.47 = f32[512,1024]{1,0:T(8,128)} custom-call(s32[2]{0:T(128)S(1)} %pad_add_fusion.where, bf16[528,1024]{1,0:T(8,128)(2,1)S(1)} %fusion.2.own, bf16[512,1024]{1,0:T(8,128)(2,1)S(1)} %get-tuple-element.11.squared, f32[512,1024]{1,0:T(8,128)S(1)} %shard_map.46.acc, bf16[512,1024]{1,0:T(8,128)(2,1)S(1)} %collective-permute-done.14.turn1, ...), custom_call_target="tpu_custom_call" | custom-call | flops 2147483648 | bytes 16777216 | tf_op jit(solution)/shard_map/pallas_call | solution.py:246
  (54 shorter events, 21.2 us)
Async XLA Ops:
  2.6 24.2 %collective-permute-start.3 = (bf16[512,1024]{1,0:T(8,128)(2,1)S(1)}, bf16[512,1024]{1,0:T(8,128)(2,1)}, u32[]{:S(2)}, u32[]{:S(2)}) collective-permute-start(bf16[512,1024]{1,0:T(8,128)(2,1)S(1)} %fusion.1.refs_0_), channel_id=1, source_target_pairs={{0,8},{4,12},{8,0},{12,4},{16,24},{20,28},{24,16},{28,20},{1,9},{5... | collective-permute-start | bytes 3145736 | tf_op jit(solution)/shard_map/ppermute | solution.py:258
  2.7 28.9 %collective-permute-start.5 = (bf16[512,1024]{1,0:T(8,128)(2,1)S(1)}, bf16[512,1024]{1,0:T(8,128)(2,1)}, u32[]{:S(2)}, u32[]{:S(2)}) collective-permute-start(bf16[512,1024]{1,0:T(8,128)(2,1)S(1)} %fusion.1.refs_0_), channel_id=1, source_target_pairs={{0,16},{4,20},{8,24},{12,28},{16,0},{20,4},{24,8},{28,12},{1,17},{... | collective-permute-start | bytes 3145736 | tf_op jit(solution)/shard_map/ppermute | solution.py:258
  4.2 29.6 %collective-permute-start.2 = (bf16[512,1024]{1,0:T(8,128)(2,1)S(1)}, bf16[512,1024]{1,0:T(8,128)(2,1)S(1)}, u32[]{:S(2)}, u32[]{:S(2)}) collective-permute-start(bf16[512,1024]{1,0:T(8,128)(2,1)S(1)} %fusion.1.refs_0_), channel_id=1, source_target_pairs={{0,4},{4,0},{8,12},{12,8},{16,20},{20,16},{24,28},{28,24},{1,5},{5... | collective-permute-start | bytes 3145736 | tf_op jit(solution)/shard_map/ppermute | solution.py:258
  26.8 23.5 %collective-permute-start.7 = (bf16[512,1024]{1,0:T(8,128)(2,1)}, bf16[512,1024]{1,0:T(8,128)(2,1)}, u32[]{:S(2)}, u32[]{:S(2)}) collective-permute-start(bf16[512,1024]{1,0:T(8,128)(2,1)} %collective-permute-done.3.refs_2_), channel_id=1, source_target_pairs={{0,16},{4,20},{8,24},{12,28},{16,0},{20,4},{24,8},{28,12},{1,17},{... | collective-permute-start | bytes 3145736 | tf_op jit(solution)/shard_map/ppermute | solution.py:258
  28.2 25.7 %collective-permute-start.1 = (bf16[528,1024]{1,0:T(8,128)(2,1)S(1)}, bf16[528,1024]{1,0:T(8,128)(2,1)S(1)}, u32[]{:S(2)}, u32[]{:S(2)}) collective-permute-start(bf16[528,1024]{1,0:T(8,128)(2,1)S(1)} %fusion.2.own), channel_id=1, source_target_pairs={{0,3},{1,2},{2,1},{3,0},{4,7},{5,6},{6,5},{7,4},{8,11},{9,10},{10,... | collective-permute-start | bytes 3244040 | tf_op jit(solution)/shard_map/ppermute | solution.py:306
  31.6 47.7 %collective-permute-start = (bf16[528,1024]{1,0:T(8,128)(2,1)S(1)}, bf16[528,1024]{1,0:T(8,128)(2,1)}, u32[]{:S(2)}, u32[]{:S(2)}) collective-permute-start(bf16[528,1024]{1,0:T(8,128)(2,1)S(1)} %fusion.2.own), channel_id=1, source_target_pairs={{0,1},{1,0},{2,3},{3,2},{4,5},{5,4},{6,7},{7,6},{8,9},{9,8},{10,11... | collective-permute-start | bytes 3244040 | tf_op jit(solution)/shard_map/ppermute | solution.py:307
  31.6 47.7 %collective-permute-start.4 = (bf16[512,1024]{1,0:T(8,128)(2,1)}, bf16[512,1024]{1,0:T(8,128)(2,1)}, u32[]{:S(2)}, u32[]{:S(2)}) collective-permute-start(bf16[512,1024]{1,0:T(8,128)(2,1)} %collective-permute-done.3.refs_2_), channel_id=1, source_target_pairs={{0,4},{4,0},{8,12},{12,8},{16,20},{20,16},{24,28},{28,24},{1,5},{5... | collective-permute-start | bytes 3145736 | tf_op jit(solution)/shard_map/ppermute | solution.py:258
  34.7 44.6 %collective-permute-start.6 = (bf16[512,1024]{1,0:T(8,128)(2,1)}, bf16[512,1024]{1,0:T(8,128)(2,1)}, u32[]{:S(2)}, u32[]{:S(2)}) collective-permute-start(bf16[512,1024]{1,0:T(8,128)(2,1)} %collective-permute-done.5.refs_4_), channel_id=1, source_target_pairs={{0,4},{4,0},{8,12},{12,8},{16,20},{20,16},{24,28},{28,24},{1,5},{5... | collective-permute-start | bytes 3145736 | tf_op jit(solution)/shard_map/ppermute | solution.py:258
  50.3 29.0 %collective-permute-start.8 = (bf16[512,1024]{1,0:T(8,128)(2,1)}, bf16[512,1024]{1,0:T(8,128)(2,1)}, u32[]{:S(2)}, u32[]{:S(2)}) collective-permute-start(bf16[512,1024]{1,0:T(8,128)(2,1)} %collective-permute-done.7.refs_6_), channel_id=1, source_target_pairs={{0,4},{4,0},{8,12},{12,8},{16,20},{20,16},{24,28},{28,24},{1,5},{5... | collective-permute-start | bytes 3145736 | tf_op jit(solution)/shard_map/ppermute | solution.py:258
  86.8 76.7 %collective-permute-start.10 = (bf16[3,528,1024]{2,1,0:T(8,128)(2,1)S(1)}, bf16[3,528,1024]{2,1,0:T(8,128)(2,1)S(1)}, u32[]{:S(2)}, u32[]{:S(2)}) collective-permute-start(bf16[3,528,1024]{2,1,0:T(8,128)(2,1)S(1)} %get-tuple-element.12.panel), channel_id=1, source_target_pairs={{0,4},{4,0},{8,12},{12,8},{16,20},{20,16},{24,28},{28,24},{1,5},{5... | collective-permute-start | bytes 9732104 | tf_op jit(solution)/shard_map/ppermute | solution.py:258
  87.4 25.3 %collective-permute-start.9 = (bf16[528,1024]{1,0:T(8,128)(2,1)S(1)}, bf16[528,1024]{1,0:T(8,128)(2,1)S(1)}, u32[]{:S(2)}, u32[]{:S(2)}) collective-permute-start(bf16[528,1024]{1,0:T(8,128)(2,1)S(1)} %collective-permute-done.1.cross), channel_id=1, source_target_pairs={{0,1},{1,0},{2,3},{3,2},{4,5},{5,4},{6,7},{7,6},{8,9},{9,8},{10,11... | collective-permute-start | bytes 3244040 | tf_op jit(solution)/shard_map/ppermute | solution.py:308
  112.7 37.6 %collective-permute-start.11 = (bf16[528,1024]{1,0:T(8,128)(2,1)S(1)}, bf16[528,1024]{1,0:T(8,128)(2,1)S(1)}, u32[]{:S(2)}, u32[]{:S(2)}) collective-permute-start(bf16[528,1024]{1,0:T(8,128)(2,1)S(1)} %collective-permute-done.9.far), channel_id=1, source_target_pairs={{0,4},{4,0},{8,12},{12,8},{16,20},{20,16},{24,28},{28,24},{1,5},{5... | collective-permute-start | bytes 3244040 | tf_op jit(solution)/shard_map/ppermute | solution.py:258
  117.7 35.3 %collective-permute-start.12 = (bf16[512,512]{1,0:T(8,128)(2,1)S(1)}, bf16[512,512]{1,0:T(8,128)(2,1)S(1)}, u32[]{:S(2)}, u32[]{:S(2)}) collective-permute-start(bf16[512,512]{1,0:T(8,128)(2,1)S(1)} %get-tuple-element.13), channel_id=1, source_target_pairs={{16,0},{20,4},{25,9},{29,13},{2,18},{6,22},{11,27},{15,31}} | collective-permute-start | bytes 1572872 | tf_op jit(solution)/shard_map/ppermute | solution.py:287
  118.4 36.9 %collective-permute-start.13 = (bf16[512,512]{1,0:T(8,128)(2,1)S(1)}, bf16[512,512]{1,0:T(8,128)(2,1)S(1)}, u32[]{:S(2)}, u32[]{:S(2)}) collective-permute-start(bf16[512,512]{1,0:T(8,128)(2,1)S(1)} %get-tuple-element.14), channel_id=1, source_target_pairs={{16,4},{20,0},{25,13},{29,9},{2,22},{6,18},{11,31},{15,27}} | collective-permute-start | bytes 1572872 | tf_op jit(solution)/shard_map/ppermute | solution.py:287
  122.8 3.1 %collective-permute-start.23 = (f32[8,128]{1,0:T(8,128)S(1)}, f32[8,128]{1,0:T(8,128)S(1)}, u32[]{:S(2)}, u32[]{:S(2)}) collective-permute-start(f32[8,128]{1,0:T(8,128)S(1)} %shard_map.49.left), channel_id=1, source_target_pairs={{0,16},{4,20},{8,24},{12,28},{16,0},{20,4},{24,8},{28,12},{1,17},{... | collective-permute-start | bytes 12296 | tf_op jit(solution)/shard_map/ppermute | solution.py:258
  125.9 3.4 %collective-permute-start.24 = (f32[8,128]{1,0:T(8,128)S(1)}, f32[8,128]{1,0:T(8,128)S(1)}, u32[]{:S(2)}, u32[]{:S(2)}) collective-permute-start(f32[8,128]{1,0:T(8,128)S(1)} %shard_map.50.left), channel_id=1, source_target_pairs={{0,2},{1,3},{2,0},{3,1},{4,6},{5,7},{6,4},{7,5},{8,10},{9,11},{10,... | collective-permute-start | bytes 12296 | tf_op jit(solution)/shard_map/ppermute | solution.py:396
  129.2 19.8 %collective-permute-start.25 = (f32[8,128]{1,0:T(8,128)S(1)}, f32[8,128]{1,0:T(8,128)S(1)}, u32[]{:S(2)}, u32[]{:S(2)}) collective-permute-start(f32[8,128]{1,0:T(8,128)S(1)} %shard_map.51.left), channel_id=1, source_target_pairs={{0,1},{1,0},{2,3},{3,2},{4,5},{5,4},{6,7},{7,6},{8,9},{9,8},{10,11... | collective-permute-start | bytes 12296 | tf_op jit(solution)/shard_map/ppermute | solution.py:396
  149.0 12.4 %collective-permute-start.19 = (bf16[512,512]{1,0:T(8,128)(2,1)S(1)}, bf16[512,512]{1,0:T(8,128)(2,1)S(1)}, u32[]{:S(2)}, u32[]{:S(2)}) collective-permute-start(bf16[512,512]{1,0:T(8,128)(2,1)S(1)} %get-tuple-element.14), channel_id=1, source_target_pairs={{24,8},{28,12},{17,1},{21,5},{10,26},{14,30},{3,19},{7,23}} | collective-permute-start | bytes 1572872 | tf_op jit(solution)/shard_map/ppermute | solution.py:287
  150.3 12.4 %collective-permute-start.16 = (bf16[512,512]{1,0:T(8,128)(2,1)S(1)}, bf16[512,512]{1,0:T(8,128)(2,1)S(1)}, u32[]{:S(2)}, u32[]{:S(2)}) collective-permute-start(bf16[512,512]{1,0:T(8,128)(2,1)S(1)} %get-tuple-element.13), channel_id=1, source_target_pairs={{8,0},{12,4},{1,9},{5,13},{26,18},{30,22},{19,27},{23,31}} | collective-permute-start | bytes 1572872 | tf_op jit(solution)/shard_map/ppermute | solution.py:287
  153.0 31.5 %collective-permute-start.14 = (bf16[512,1024]{1,0:T(8,128)(2,1)S(1)}, bf16[512,1024]{1,0:T(8,128)(2,1)S(1)}, u32[]{:S(2)}, u32[]{:S(2)}) collective-permute-start(bf16[512,1024]{1,0:T(8,128)(2,1)S(1)} %get-tuple-element.11.squared), channel_id=1, source_target_pairs={{1,2},{2,3},{3,1},{5,6},{6,7},{7,5},{8,10},{10,11},{11,8},{12,14},... | collective-permute-start | bytes 3145736 | tf_op jit(solution)/shard_map/ppermute | solution.py:277
  155.2 49.0 %collective-permute-start.15 = (bf16[512,1024]{1,0:T(8,128)(2,1)S(1)}, bf16[512,1024]{1,0:T(8,128)(2,1)S(1)}, u32[]{:S(2)}, u32[]{:S(2)}) collective-permute-start(bf16[512,1024]{1,0:T(8,128)(2,1)S(1)} %get-tuple-element.11.squared), channel_id=1, source_target_pairs={{1,3},{2,1},{3,2},{5,7},{6,5},{7,6},{8,11},{10,8},{11,10},{12,15},... | collective-permute-start | bytes 3145736 | tf_op jit(solution)/shard_map/ppermute | solution.py:277
  161.4 19.4 %collective-permute-start.17 = (bf16[512,512]{1,0:T(8,128)(2,1)S(1)}, bf16[512,512]{1,0:T(8,128)(2,1)S(1)}, u32[]{:S(2)}, u32[]{:S(2)}) collective-permute-start(bf16[512,512]{1,0:T(8,128)(2,1)S(1)} %get-tuple-element.14), channel_id=1, source_target_pairs={{8,4},{12,0},{1,13},{5,9},{26,22},{30,18},{19,31},{23,27}} | collective-permute-start | bytes 1572872 | tf_op jit(solution)/shard_map/ppermute | solution.py:287
  162.8 18.1 %collective-permute-start.18 = (bf16[512,512]{1,0:T(8,128)(2,1)S(1)}, bf16[512,512]{1,0:T(8,128)(2,1)S(1)}, u32[]{:S(2)}, u32[]{:S(2)}) collective-permute-start(bf16[512,512]{1,0:T(8,128)(2,1)S(1)} %get-tuple-element.13), channel_id=1, source_target_pairs={{24,0},{28,4},{17,9},{21,13},{10,18},{14,22},{3,27},{7,31}} | collective-permute-start | bytes 1572872 | tf_op jit(solution)/shard_map/ppermute | solution.py:287
  163.5 21.0 %collective-permute-start.20 = (bf16[512,512]{1,0:T(8,128)(2,1)S(1)}, bf16[512,512]{1,0:T(8,128)(2,1)S(1)}, u32[]{:S(2)}, u32[]{:S(2)}) collective-permute-start(bf16[512,512]{1,0:T(8,128)(2,1)S(1)} %collective-permute-done.19), channel_id=1, source_target_pairs={{8,4},{12,0},{1,13},{5,9},{26,22},{30,18},{19,31},{23,27}} | collective-permute-start | bytes 1572872 | tf_op jit(solution)/shard_map/ppermute | solution.py:287
  (5 other events, 7.1 us)

commit v6 on v5

--- a/solution.py
+++ b/solution.py
@@ -127,6 +127,10 @@
 
 def add_kernel(left, right, out):
     out[...] = left[...] + right[...]
+
+
+def add_planes_kernel(own, first, second, third, out):
+    out[...] = (own[...] + first[...]) + (second[...] + third[...])
 
 
 def turn_kernel(where, squared, same_ref, cross_ref):
@@ -198,7 +202,7 @@
 
     @pl.when(row // 2 == col)
     def _():
-        acc[...] = acc_in[...] + side_piece((same, cross), right_all, col ^ 2, row % 2)
+        acc[...] = acc_in[...] + side_piece((same, cross), right_all, col ^ 1, row % 2)
 
     @pl.when(row // 2 != col)
     def _():
@@ -231,7 +235,7 @@
     @pl.when(chip == col)
     def _():
         finish(
-            side_piece(sides[:2], right_all, col ^ 1, core),
+            side_piece(sides[:2], right_all, col ^ 2, core),
             lambda: side_piece(sides[2:], right_all, col ^ 3, core),
         )
 
@@ -386,18 +390,27 @@
     cubic = call(
         cubic_middle_kernel,
         [SCALARS] + [WHOLE] * 4,
-        (where, cubic, right, *sides[2:4]),
+        (where, cubic, right, *sides[:2]),
         wide,
         [],
         flops,
         9 * size,
     )
-    for k in (2, 1):
-        total = add(total, lax.ppermute(total, "col", [(i, i ^ k) for i in range(4)]))
+    planes = [lax.ppermute(total, "col", [(i, i ^ k) for i in range(4)]) for k in (1, 2, 3)]
+    total = call(
+        add_planes_kernel,
+        [WHOLE] * 4,
+        (total, *planes),
+        jax.ShapeDtypeStruct(total.shape, total.dtype),
+        [],
+        3 * total.size,
+        20 * total.size,
+        1,
+    )
     purified = call(
         cubic_late_kernel,
         [SCALARS] + [WHOLE] * 10,
-        (where, own, squared, cubic, *turns, right, *sides[:2], *sides[4:]),
+        (where, own, squared, cubic, *turns, right, *sides[2:]),
         wide,
         [pltpu.VMEM((rows, columns), jnp.float32)],
         2 * flops,

time: 210 us -> 217 us (1.033)
  the two profiles are of different devices: /device:TPU:3 before, /device:TPU:5 now
where the time goes in v6:
time: 217 us; the launch traced here: 216 us
  waiting for transfers between devices  132 us (61%)
  starting transfers between devices  53 us (24%)
  Pallas kernels  24.2 us (11%)
  local copies, waits for them, and re-layouts  3.24 us (1%)
  between operations  2.65 us (1%)
    ppermute x12, waiting for transfers between devices, swap(): return lax.ppermute(x, 'row', [(i, i ^ k) for i in range(8)])  41.5 us
    ppermute x12, starting transfers between devices, swap(): return lax.ppermute(x, 'row', [(i, i ^ k) for i in range(8)])  31.6 us
    ppermute x1, waiting for transfers between devices, local(): pair = lax.ppermute(own, 'col', [(i, i ^ 1) for i in range(4)])  25.1 us
    pallas_call x11, Pallas kernels, call(): pl.pallas_call(kernel, out_shape=outs, in_specs=specs, out_specs=jax.tree...  24.2 us
    ppermute x1, waiting for transfers between devices, local(): far = lax.ppermute(cross, 'col', [(i, i ^ 1) for i in range(4)])  24.2 us
    ppermute x2, waiting for transfers between devices, rotate(): return lax.ppermute(x, ('row', 'col'), pairs)  18.7 us
    ppermute x7, waiting for transfers between devices, in_plane(): return lax.ppermute(x, ('row', 'col'), pairs)  12.5 us
    ppermute x3, waiting for transfers between devices, local(): lax.ppermute(total, 'col', [(i, i ^ k) for i in range(4)])  9.27 us
  transfers between devices with their start and end apart: 27, of which 13 were waited for; matrix products, arithmetic and copies ran while one was open for 0% of the time, Pallas kernels for 6%

profile of v6, /device:TPU:5, one launch (start us, length us, event | category | flops | bytes accessed | tf_op | source)
XLA Modules:
  0.0 216.4 jit_solution(6251595937401438191)
XLA Ops:
  5.4 21.5 %collective-permute-done.3.refs_2_ = bf16[512,1024]{1,0:T(8,128)(2,1)} collective-permute-done((bf16[512,1024]{1,0:T(8,128)(2,1)S(1)}, bf16[512,1024]{1,0:T(8,128)(2,1)}, u32[]{:S(2)}, u32[]{:S(2)}) %collective-permute-start.3) | collective-permute-done | bytes 1048608 | tf_op jit(solution)/shard_map/ppermute | solution.py:262
  27.3 3.4 %collective-permute-start.1 = (bf16[528,1024]{1,0:T(8,128)(2,1)S(1)}, bf16[528,1024]{1,0:T(8,128)(2,1)S(1)}, u32[]{:S(2)}, u32[]{:S(2)}) collective-permute-start(bf16[528,1024]{1,0:T(8,128)(2,1)S(1)} %fusion.2.own), channel_id=1, source_target_pairs={{0,3},{1,2},{2,1},{3,0},{4,7},{5,6},{6,5},{7,4},{8,11},{9,10},{10,... | collective-permute-start | bytes 3244040 | tf_op jit(solution)/shard_map/ppermute | solution.py:310
  30.6 2.1 collective-permute-start.4
  33.7 16.6 %collective-permute-done.7.refs_6_ = bf16[512,1024]{1,0:T(8,128)(2,1)} collective-permute-done((bf16[512,1024]{1,0:T(8,128)(2,1)}, bf16[512,1024]{1,0:T(8,128)(2,1)}, u32[]{:S(2)}, u32[]{:S(2)}) %collective-permute-start.7) | collective-permute-done | bytes 1048608 | tf_op jit(solution)/shard_map/ppermute | solution.py:262
  50.3 2.4 %collective-permute-start.8 = (bf16[512,1024]{1,0:T(8,128)(2,1)}, bf16[512,1024]{1,0:T(8,128)(2,1)}, u32[]{:S(2)}, u32[]{:S(2)}) collective-permute-start(bf16[512,1024]{1,0:T(8,128)(2,1)} %collective-permute-done.7.refs_6_), channel_id=1, source_target_pairs={{0,4},{4,0},{8,12},{12,8},{16,20},{20,16},{24,28},{28,24},{1,5},{5... | collective-permute-start | bytes 3145736 | tf_op jit(solution)/shard_map/ppermute | solution.py:262
  53.2 25.1 %collective-permute-done.pair = bf16[528,1024]{1,0:T(8,128)(2,1)} collective-permute-done((bf16[528,1024]{1,0:T(8,128)(2,1)S(1)}, bf16[528,1024]{1,0:T(8,128)(2,1)}, u32[]{:S(2)}, u32[]{:S(2)}) %collective-permute-start) | collective-permute-done | bytes 1081376 | tf_op jit(solution)/shard_map/ppermute | solution.py:311
  79.6 6.9 %shard_map.41 = (f32[512,1024]{1,0:T(8,128)S(1)}, bf16[3,528,1024]{2,1,0:T(8,128)(2,1)S(1)}, bf16[8,512,1024]{2,1,0:T(8,128)(2,1)S(1)}) custom-call(s32[2]{0:T(128)S(1)} %pad_add_fusion.where, bf16[528,1024]{1,0:T(8,128)(2,1)S(1)} %fusion.2.own, bf16[528,1024]{1,0:T(8,128)(2,1)} %collective-permute-done.pair, ...), custom_call_target="tpu_custom_call" | custom-call | flops 3221225472 | bytes 25165824 | tf_op jit(solution)/shard_map/pallas_call | solution.py:250
  87.0 2.0 collective-permute-start.9
  89.0 24.2 %collective-permute-done.9.far = bf16[528,1024]{1,0:T(8,128)(2,1)S(1)} collective-permute-done((bf16[528,1024]{1,0:T(8,128)(2,1)S(1)}, bf16[528,1024]{1,0:T(8,128)(2,1)S(1)}, u32[]{:S(2)}, u32[]{:S(2)}) %collective-permute-start.9) | collective-permute-done | bytes 1081376 | tf_op jit(solution)/shard_map/ppermute | solution.py:312
  113.8 2.2 %shard_map.42 = (bf16[512,1024]{1,0:T(8,128)(2,1)S(1)}, f32[8,128]{1,0:T(8,128)S(1)}) custom-call(s32[2]{0:T(128)S(1)} %pad_add_fusion.where, bf16[528,1024]{1,0:T(8,128)(2,1)S(1)} %fusion.2.own, f32[512,1024]{1,0:T(8,128)S(1)} %get-tuple-element.9.acc_in, bf16[8,512,1024]{2,1,0:T(8,128)(2,1)S(1)} %get-tuple-element.10.right.right_all, ...), custom_call_target="tpu_custom_call" | custom-call | flops 1073741824 | bytes 8388608 | tf_op jit(solution)/shard_map/pallas_call | solution.py:250
  116.0 1.8 shard_map.45
  122.9 21.5 %collective-permute-start.23 = (f32[8,128]{1,0:T(8,128)S(1)}, f32[8,128]{1,0:T(8,128)S(1)}, u32[]{:S(2)}, u32[]{:S(2)}) collective-permute-start(f32[8,128]{1,0:T(8,128)S(1)} %shard_map.49.left), channel_id=1, source_target_pairs={{0,16},{4,20},{8,24},{12,28},{16,0},{20,4},{24,8},{28,12},{1,17},{... | collective-permute-start | bytes 12296 | tf_op jit(solution)/shard_map/ppermute | solution.py:262
  145.5 2.5 %collective-permute-done.24.first = f32[8,128]{1,0:T(8,128)S(1)} collective-permute-done((f32[8,128]{1,0:T(8,128)S(1)}, f32[8,128]{1,0:T(8,128)S(1)}, u32[]{:S(2)}, u32[]{:S(2)}) %collective-permute-start.24) | collective-permute-done | bytes 4128 | tf_op jit(solution)/shard_map/ppermute | solution.py:399
  148.5 2.8 %collective-permute-done.25.second = f32[8,128]{1,0:T(8,128)S(1)} collective-permute-done((f32[8,128]{1,0:T(8,128)S(1)}, f32[8,128]{1,0:T(8,128)S(1)}, u32[]{:S(2)}, u32[]{:S(2)}) %collective-permute-start.25) | collective-permute-done | bytes 4128 | tf_op jit(solution)/shard_map/ppermute | solution.py:399
  151.5 4.0 %collective-permute-done.26.third = f32[8,128]{1,0:T(8,128)S(1)} collective-permute-done((f32[8,128]{1,0:T(8,128)S(1)}, f32[8,128]{1,0:T(8,128)S(1)}, u32[]{:S(2)}, u32[]{:S(2)}) %collective-permute-start.26) | collective-permute-done | bytes 4128 | tf_op jit(solution)/shard_map/ppermute | solution.py:399
  156.2 3.4 %collective-permute-start.16 = (bf16[512,512]{1,0:T(8,128)(2,1)S(1)}, bf16[512,512]{1,0:T(8,128)(2,1)S(1)}, u32[]{:S(2)}, u32[]{:S(2)}) collective-permute-start(bf16[512,512]{1,0:T(8,128)(2,1)S(1)} %get-tuple-element.13), channel_id=1, source_target_pairs={{16,0},{20,4},{25,9},{29,13},{2,18},{6,22},{11,27},{15,31}} | collective-permute-start | bytes 1572872 | tf_op jit(solution)/shard_map/ppermute | solution.py:291
  159.7 1.9 collective-permute-start.14
  161.6 5.2 %collective-permute-start.15 = (bf16[512,1024]{1,0:T(8,128)(2,1)S(1)}, bf16[512,1024]{1,0:T(8,128)(2,1)S(1)}, u32[]{:S(2)}, u32[]{:S(2)}) collective-permute-start(bf16[512,1024]{1,0:T(8,128)(2,1)S(1)} %get-tuple-element.11.squared), channel_id=1, source_target_pairs={{1,3},{2,1},{3,2},{5,7},{6,5},{7,6},{8,11},{10,8},{11,10},{12,15},... | collective-permute-start | bytes 3145736 | tf_op jit(solution)/shard_map/ppermute | solution.py:281
  168.0 1.3 collective-permute-start.17
  170.7 5.1 %shard_map.43.local_square = bf16[512,1024]{1,0:T(8,128)(2,1)S(1)} custom-call(s32[2]{0:T(128)S(1)} %pad_add_fusion.where, bf16[3,528,1024]{2,1,0:T(8,128)(2,1)S(1)} %get-tuple-element.12.panel, bf16[3,528,1024]{2,1,0:T(8,128)(2,1)S(1)} %collective-permute-done.10.other, bf16[528,1024]{1,0:T(8,128)(2,1)S(1)} %collective-permute-done.9.far, ...), custom_call_target="tpu_custom_call" | custom-call | flops 4294967296 | bytes 9437184 | tf_op jit(solution)/shard_map/pallas_call | solution.py:250
  175.8 3.2 %shard_map.44.acc_in = f32[512,1024]{1,0:T(8,128)S(1)} custom-call(s32[2]{0:T(128)S(1)} %pad_add_fusion.where, bf16[512,1024]{1,0:T(8,128)(2,1)S(1)} %get-tuple-element.11.squared, bf16[512,1024]{1,0:T(8,128)(2,1)S(1)} %shard_map.43.local_square, bf16[8,512,1024]{2,1,0:T(8,128)(2,1)S(1)} %get-tuple-element.10.right.right_all), custom_call_target="tpu_custom_call" | custom-call | flops 2147483648 | bytes 8388608 | tf_op jit(solution)/shard_map/pallas_call | solution.py:250
  179.7 12.5 %collective-permute-done.17.refs_1_ = bf16[512,512]{1,0:T(8,128)(2,1)S(1)} collective-permute-done((bf16[512,512]{1,0:T(8,128)(2,1)S(1)}, bf16[512,512]{1,0:T(8,128)(2,1)S(1)}, u32[]{:S(2)}, u32[]{:S(2)}) %collective-permute-start.17) | collective-permute-done | bytes 524320 | tf_op jit(solution)/shard_map/ppermute | solution.py:291
  192.2 18.7 %collective-permute-done.15.turn2 = bf16[512,1024]{1,0:T(8,128)(2,1)S(1)} collective-permute-done((bf16[512,1024]{1,0:T(8,128)(2,1)S(1)}, bf16[512,1024]{1,0:T(8,128)(2,1)S(1)}, u32[]{:S(2)}, u32[]{:S(2)}) %collective-permute-start.15) | collective-permute-done | bytes 1048608 | tf_op jit(solution)/shard_map/ppermute | solution.py:281
  210.9 4.3 %shard_map.47 = f32[512,1024]{1,0:T(8,128)} custom-call(s32[2]{0:T(128)S(1)} %pad_add_fusion.where, bf16[528,1024]{1,0:T(8,128)(2,1)S(1)} %fusion.2.own, bf16[512,1024]{1,0:T(8,128)(2,1)S(1)} %get-tuple-element.11.squared, f32[512,1024]{1,0:T(8,128)S(1)} %shard_map.46.acc, bf16[512,1024]{1,0:T(8,128)(2,1)S(1)} %collective-permute-done.14.turn1, ...), custom_call_target="tpu_custom_call" | custom-call | flops 2147483648 | bytes 16777216 | tf_op jit(solution)/shard_map/pallas_call | solution.py:250
  (55 shorter events, 19.2 us)
Async XLA Ops:
  2.6 24.2 %collective-permute-start.3 = (bf16[512,1024]{1,0:T(8,128)(2,1)S(1)}, bf16[512,1024]{1,0:T(8,128)(2,1)}, u32[]{:S(2)}, u32[]{:S(2)}) collective-permute-start(bf16[512,1024]{1,0:T(8,128)(2,1)S(1)} %fusion.1.refs_0_), channel_id=1, source_target_pairs={{0,8},{4,12},{8,0},{12,4},{16,24},{20,28},{24,16},{28,20},{1,9},{5... | collective-permute-start | bytes 3145736 | tf_op jit(solution)/shard_map/ppermute | solution.py:262
  3.9 26.7 %collective-permute-start.5 = (bf16[512,1024]{1,0:T(8,128)(2,1)S(1)}, bf16[512,1024]{1,0:T(8,128)(2,1)}, u32[]{:S(2)}, u32[]{:S(2)}) collective-permute-start(bf16[512,1024]{1,0:T(8,128)(2,1)S(1)} %fusion.1.refs_0_), channel_id=1, source_target_pairs={{0,16},{4,20},{8,24},{12,28},{16,0},{20,4},{24,8},{28,12},{1,17},{... | collective-permute-start | bytes 3145736 | tf_op jit(solution)/shard_map/ppermute | solution.py:262
  4.1 28.6 %collective-permute-start.2 = (bf16[512,1024]{1,0:T(8,128)(2,1)S(1)}, bf16[512,1024]{1,0:T(8,128)(2,1)S(1)}, u32[]{:S(2)}, u32[]{:S(2)}) collective-permute-start(bf16[512,1024]{1,0:T(8,128)(2,1)S(1)} %fusion.1.refs_0_), channel_id=1, source_target_pairs={{0,4},{4,0},{8,12},{12,8},{16,20},{20,16},{24,28},{28,24},{1,5},{5... | collective-permute-start | bytes 3145736 | tf_op jit(solution)/shard_map/ppermute | solution.py:262
  26.8 23.5 %collective-permute-start.7 = (bf16[512,1024]{1,0:T(8,128)(2,1)}, bf16[512,1024]{1,0:T(8,128)(2,1)}, u32[]{:S(2)}, u32[]{:S(2)}) collective-permute-start(bf16[512,1024]{1,0:T(8,128)(2,1)} %collective-permute-done.3.refs_2_), channel_id=1, source_target_pairs={{0,16},{4,20},{8,24},{12,28},{16,0},{20,4},{24,8},{28,12},{1,17},{... | collective-permute-start | bytes 3145736 | tf_op jit(solution)/shard_map/ppermute | solution.py:262
  27.3 25.9 %collective-permute-start.1 = (bf16[528,1024]{1,0:T(8,128)(2,1)S(1)}, bf16[528,1024]{1,0:T(8,128)(2,1)S(1)}, u32[]{:S(2)}, u32[]{:S(2)}) collective-permute-start(bf16[528,1024]{1,0:T(8,128)(2,1)S(1)} %fusion.2.own), channel_id=1, source_target_pairs={{0,3},{1,2},{2,1},{3,0},{4,7},{5,6},{6,5},{7,4},{8,11},{9,10},{10,... | collective-permute-start | bytes 3244040 | tf_op jit(solution)/shard_map/ppermute | solution.py:310
  30.6 47.7 %collective-permute-start = (bf16[528,1024]{1,0:T(8,128)(2,1)S(1)}, bf16[528,1024]{1,0:T(8,128)(2,1)}, u32[]{:S(2)}, u32[]{:S(2)}) collective-permute-start(bf16[528,1024]{1,0:T(8,128)(2,1)S(1)} %fusion.2.own), channel_id=1, source_target_pairs={{0,1},{1,0},{2,3},{3,2},{4,5},{5,4},{6,7},{7,6},{8,9},{9,8},{10,11... | collective-permute-start | bytes 3244040 | tf_op jit(solution)/shard_map/ppermute | solution.py:311
  30.6 47.7 %collective-permute-start.4 = (bf16[512,1024]{1,0:T(8,128)(2,1)}, bf16[512,1024]{1,0:T(8,128)(2,1)}, u32[]{:S(2)}, u32[]{:S(2)}) collective-permute-start(bf16[512,1024]{1,0:T(8,128)(2,1)} %collective-permute-done.3.refs_2_), channel_id=1, source_target_pairs={{0,4},{4,0},{8,12},{12,8},{16,20},{20,16},{24,28},{28,24},{1,5},{5... | collective-permute-start | bytes 3145736 | tf_op jit(solution)/shard_map/ppermute | solution.py:262
  33.7 44.6 %collective-permute-start.6 = (bf16[512,1024]{1,0:T(8,128)(2,1)}, bf16[512,1024]{1,0:T(8,128)(2,1)}, u32[]{:S(2)}, u32[]{:S(2)}) collective-permute-start(bf16[512,1024]{1,0:T(8,128)(2,1)} %collective-permute-done.5.refs_4_), channel_id=1, source_target_pairs={{0,4},{4,0},{8,12},{12,8},{16,20},{20,16},{24,28},{28,24},{1,5},{5... | collective-permute-start | bytes 3145736 | tf_op jit(solution)/shard_map/ppermute | solution.py:262
  50.3 28.0 %collective-permute-start.8 = (bf16[512,1024]{1,0:T(8,128)(2,1)}, bf16[512,1024]{1,0:T(8,128)(2,1)}, u32[]{:S(2)}, u32[]{:S(2)}) collective-permute-start(bf16[512,1024]{1,0:T(8,128)(2,1)} %collective-permute-done.7.refs_6_), channel_id=1, source_target_pairs={{0,4},{4,0},{8,12},{12,8},{16,20},{20,16},{24,28},{28,24},{1,5},{5... | collective-permute-start | bytes 3145736 | tf_op jit(solution)/shard_map/ppermute | solution.py:262
  86.4 83.6 %collective-permute-start.10 = (bf16[3,528,1024]{2,1,0:T(8,128)(2,1)S(1)}, bf16[3,528,1024]{2,1,0:T(8,128)(2,1)S(1)}, u32[]{:S(2)}, u32[]{:S(2)}) collective-permute-start(bf16[3,528,1024]{2,1,0:T(8,128)(2,1)S(1)} %get-tuple-element.12.panel), channel_id=1, source_target_pairs={{0,4},{4,0},{8,12},{12,8},{16,20},{20,16},{24,28},{28,24},{1,5},{5... | collective-permute-start | bytes 9732104 | tf_op jit(solution)/shard_map/ppermute | solution.py:262
  87.0 26.2 %collective-permute-start.9 = (bf16[528,1024]{1,0:T(8,128)(2,1)S(1)}, bf16[528,1024]{1,0:T(8,128)(2,1)S(1)}, u32[]{:S(2)}, u32[]{:S(2)}) collective-permute-start(bf16[528,1024]{1,0:T(8,128)(2,1)S(1)} %collective-permute-done.1.cross), channel_id=1, source_target_pairs={{0,1},{1,0},{2,3},{3,2},{4,5},{5,4},{6,7},{7,6},{8,9},{9,8},{10,11... | collective-permute-start | bytes 3244040 | tf_op jit(solution)/shard_map/ppermute | solution.py:312
  113.2 43.1 %collective-permute-start.11 = (bf16[528,1024]{1,0:T(8,128)(2,1)S(1)}, bf16[528,1024]{1,0:T(8,128)(2,1)S(1)}, u32[]{:S(2)}, u32[]{:S(2)}) collective-permute-start(bf16[528,1024]{1,0:T(8,128)(2,1)S(1)} %collective-permute-done.9.far), channel_id=1, source_target_pairs={{0,4},{4,0},{8,12},{12,8},{16,20},{20,16},{24,28},{28,24},{1,5},{5... | collective-permute-start | bytes 3244040 | tf_op jit(solution)/shard_map/ppermute | solution.py:262
  117.8 41.8 %collective-permute-start.12 = (bf16[512,512]{1,0:T(8,128)(2,1)S(1)}, bf16[512,512]{1,0:T(8,128)(2,1)S(1)}, u32[]{:S(2)}, u32[]{:S(2)}) collective-permute-start(bf16[512,512]{1,0:T(8,128)(2,1)S(1)} %get-tuple-element.13), channel_id=1, source_target_pairs={{8,0},{12,4},{1,9},{5,13},{26,18},{30,22},{19,27},{23,31}} | collective-permute-start | bytes 1572872 | tf_op jit(solution)/shard_map/ppermute | solution.py:291
  118.5 43.1 %collective-permute-start.13 = (bf16[512,512]{1,0:T(8,128)(2,1)S(1)}, bf16[512,512]{1,0:T(8,128)(2,1)S(1)}, u32[]{:S(2)}, u32[]{:S(2)}) collective-permute-start(bf16[512,512]{1,0:T(8,128)(2,1)S(1)} %get-tuple-element.14), channel_id=1, source_target_pairs={{8,4},{12,0},{1,13},{5,9},{26,22},{30,18},{19,31},{23,27}} | collective-permute-start | bytes 1572872 | tf_op jit(solution)/shard_map/ppermute | solution.py:291
  122.9 22.5 %collective-permute-start.23 = (f32[8,128]{1,0:T(8,128)S(1)}, f32[8,128]{1,0:T(8,128)S(1)}, u32[]{:S(2)}, u32[]{:S(2)}) collective-permute-start(f32[8,128]{1,0:T(8,128)S(1)} %shard_map.49.left), channel_id=1, source_target_pairs={{0,16},{4,20},{8,24},{12,28},{16,0},{20,4},{24,8},{28,12},{1,17},{... | collective-permute-start | bytes 12296 | tf_op jit(solution)/shard_map/ppermute | solution.py:262
  147.9 3.4 %collective-permute-start.25 = (f32[8,128]{1,0:T(8,128)S(1)}, f32[8,128]{1,0:T(8,128)S(1)}, u32[]{:S(2)}, u32[]{:S(2)}) collective-permute-start(f32[8,128]{1,0:T(8,128)S(1)} %shard_map.50.own), channel_id=1, source_target_pairs={{0,2},{1,3},{2,0},{3,1},{4,6},{5,7},{6,4},{7,5},{8,10},{9,11},{10,... | collective-permute-start | bytes 12296 | tf_op jit(solution)/shard_map/ppermute | solution.py:399
  151.3 4.3 %collective-permute-start.26 = (f32[8,128]{1,0:T(8,128)S(1)}, f32[8,128]{1,0:T(8,128)S(1)}, u32[]{:S(2)}, u32[]{:S(2)}) collective-permute-start(f32[8,128]{1,0:T(8,128)S(1)} %shard_map.50.own), channel_id=1, source_target_pairs={{0,3},{1,2},{2,1},{3,0},{4,7},{5,6},{6,5},{7,4},{8,11},{9,10},{10,... | collective-permute-start | bytes 12296 | tf_op jit(solution)/shard_map/ppermute | solution.py:399
  155.5 12.4 %collective-permute-start.19 = (bf16[512,512]{1,0:T(8,128)(2,1)S(1)}, bf16[512,512]{1,0:T(8,128)(2,1)S(1)}, u32[]{:S(2)}, u32[]{:S(2)}) collective-permute-start(bf16[512,512]{1,0:T(8,128)(2,1)S(1)} %get-tuple-element.14), channel_id=1, source_target_pairs={{24,8},{28,12},{17,1},{21,5},{10,26},{14,30},{3,19},{7,23}} | collective-permute-start | bytes 1572872 | tf_op jit(solution)/shard_map/ppermute | solution.py:291
  156.2 13.0 %collective-permute-start.16 = (bf16[512,512]{1,0:T(8,128)(2,1)S(1)}, bf16[512,512]{1,0:T(8,128)(2,1)S(1)}, u32[]{:S(2)}, u32[]{:S(2)}) collective-permute-start(bf16[512,512]{1,0:T(8,128)(2,1)S(1)} %get-tuple-element.13), channel_id=1, source_target_pairs={{16,0},{20,4},{25,9},{29,13},{2,18},{6,22},{11,27},{15,31}} | collective-permute-start | bytes 1572872 | tf_op jit(solution)/shard_map/ppermute | solution.py:291
  159.7 32.6 %collective-permute-start.14 = (bf16[512,1024]{1,0:T(8,128)(2,1)S(1)}, bf16[512,1024]{1,0:T(8,128)(2,1)S(1)}, u32[]{:S(2)}, u32[]{:S(2)}) collective-permute-start(bf16[512,1024]{1,0:T(8,128)(2,1)S(1)} %get-tuple-element.11.squared), channel_id=1, source_target_pairs={{1,2},{2,3},{3,1},{5,6},{6,7},{7,5},{8,10},{10,11},{11,8},{12,14},... | collective-permute-start | bytes 3145736 | tf_op jit(solution)/shard_map/ppermute | solution.py:281
  161.6 49.3 %collective-permute-start.15 = (bf16[512,1024]{1,0:T(8,128)(2,1)S(1)}, bf16[512,1024]{1,0:T(8,128)(2,1)S(1)}, u32[]{:S(2)}, u32[]{:S(2)}) collective-permute-start(bf16[512,1024]{1,0:T(8,128)(2,1)S(1)} %get-tuple-element.11.squared), channel_id=1, source_target_pairs={{1,3},{2,1},{3,2},{5,7},{6,5},{7,6},{8,11},{10,8},{11,10},{12,15},... | collective-permute-start | bytes 3145736 | tf_op jit(solution)/shard_map/ppermute | solution.py:281
  168.0 24.3 %collective-permute-start.17 = (bf16[512,512]{1,0:T(8,128)(2,1)S(1)}, bf16[512,512]{1,0:T(8,128)(2,1)S(1)}, u32[]{:S(2)}, u32[]{:S(2)}) collective-permute-start(bf16[512,512]{1,0:T(8,128)(2,1)S(1)} %get-tuple-element.14), channel_id=1, source_target_pairs={{16,4},{20,0},{25,13},{29,9},{2,22},{6,18},{11,31},{15,27}} | collective-permute-start | bytes 1572872 | tf_op jit(solution)/shard_map/ppermute | solution.py:291
  169.3 22.9 %collective-permute-start.18 = (bf16[512,512]{1,0:T(8,128)(2,1)S(1)}, bf16[512,512]{1,0:T(8,128)(2,1)S(1)}, u32[]{:S(2)}, u32[]{:S(2)}) collective-permute-start(bf16[512,512]{1,0:T(8,128)(2,1)S(1)} %get-tuple-element.13), channel_id=1, source_target_pairs={{24,0},{28,4},{17,9},{21,13},{10,18},{14,22},{3,27},{7,31}} | collective-permute-start | bytes 1572872 | tf_op jit(solution)/shard_map/ppermute | solution.py:291
  170.0 22.2 %collective-permute-start.20 = (bf16[512,512]{1,0:T(8,128)(2,1)S(1)}, bf16[512,512]{1,0:T(8,128)(2,1)S(1)}, u32[]{:S(2)}, u32[]{:S(2)}) collective-permute-start(bf16[512,512]{1,0:T(8,128)(2,1)S(1)} %collective-permute-done.19), channel_id=1, source_target_pairs={{8,4},{12,0},{1,13},{5,9},{26,22},{30,18},{19,31},{23,27}} | collective-permute-start | bytes 1572872 | tf_op jit(solution)/shard_map/ppermute | solution.py:291
  (6 other events, 9.6 us)

commit v7 on v6

--- a/solution.py
+++ b/solution.py
@@ -48,8 +48,8 @@
 
 def piece(left, right):
     rows = right.shape[1]
-    return jnp.dot(left[:rows, :rows], right[0], preferred_element_type=jnp.float32) + jnp.dot(
-        left[:rows, rows:], right[1], preferred_element_type=jnp.float32
+    return jnp.dot(left[:, :rows], right[0], preferred_element_type=jnp.float32) + jnp.dot(
+        left[:, rows:], right[1], preferred_element_type=jnp.float32
     )
 
 
@@ -72,12 +72,15 @@
         )
 
 
-def square_early_kernel(where, own, pair, cross, *refs):
+def square_early_kernel(where, own, pair, cross_a, cross_b, *refs):
     rights = refs[:8]
     acc, panel, right, left_sem, right_sem = refs[8:]
     row, col = where[0], where[1]
-    for i, ref in enumerate((own, pair, cross)):
-        pltpu.make_async_copy(ref, panel.at[i], left_sem.at[i]).start()
+    half = cross_a.shape[0]
+    pltpu.make_async_copy(own, panel.at[0], left_sem.at[0]).start()
+    pltpu.make_async_copy(pair, panel.at[1], left_sem.at[1]).start()
+    pltpu.make_async_copy(cross_a, panel.at[2, :half], left_sem.at[2]).start()
+    pltpu.make_async_copy(cross_b, panel.at[2, half:], left_sem.at[2]).start()
 
     for k in range(8):
         slot = row ^ k
@@ -88,24 +91,29 @@
         for t in range(2):
             there = right.at[slot + t]
             pltpu.make_async_copy(there, there, right_sem.at[slot + t]).wait()
-        multiply(acc, panel.at[i], right.at[pl.ds(slot, 2)], i == 0)
+        multiply(acc, panel.at[i, : acc.shape[0]], right.at[pl.ds(slot, 2)], i == 0)
     slot = 2 * (col ^ LAST)
     for t in range(2):
         there = right.at[slot + t]
         pltpu.make_async_copy(there, there, right_sem.at[slot + t]).wait()
 
 
-def square_late_kernel(where, own, acc_in, right, far, squared_ref, sum_ref):
-    row, col = where[0], where[1]
-    rows, columns = squared_ref.shape
-    total = acc_in[...] + piece(far, right.at[pl.ds(2 * (col ^ LAST), 2)])
+def square_late_kernel(first, where, own, acc_in, right, far, sums_in, squared_ref, sum_ref):
+    row, col = where[0], where[1]
+    rows, columns = acc_in.shape
+    count = squared_ref.shape[0]
+    total = acc_in[first : first + count] + piece(
+        far.at[:count], right.at[pl.ds(2 * (col ^ LAST), 2)]
+    )
     kept = own[rows : rows + EXTRA, :].astype(jnp.float32)
     sums = jnp.zeros((8, columns), jnp.float32)
-    for a in range(rows // B):
+    for a in range(count // B):
         part = slice(a * B, (a + 1) * B)
-        squared = (total[part] * kept[a : a + 1]).astype(jnp.bfloat16)
+        whole = slice(first + a * B, first + (a + 1) * B)
+        line = first // B + a
+        squared = (total[part] * kept[line : line + 1]).astype(jnp.bfloat16)
         squared_ref[part, :] = squared
-        term = squared.astype(jnp.float32) * own[part, :].astype(jnp.float32)
+        term = squared.astype(jnp.float32) * own[whole, :].astype(jnp.float32)
         sums -= 2.0 * jnp.sum(term.reshape(B // 8, 8, columns), axis=0)
     sum_ref[...] = sums[:, :B]
     for n in range(1, columns // B):
@@ -116,36 +124,61 @@
         same = lax.broadcasted_iota(jnp.int32, (B, B), 0) == lax.broadcasted_iota(
             jnp.int32, (B, B), 1
         )
-        for a in range(rows // B):
-            lanes = pl.ds(pl.multiple_of(row * rows - col * columns + a * B, B), B)
+        for a in range(count // B):
+            start = row * rows - col * columns + first + a * B
+            lanes = pl.ds(pl.multiple_of(start, B), B)
             squared = squared_ref[a * B : (a + 1) * B, lanes].astype(jnp.float32)
             term = jnp.where(same, 3.0 * squared, 0.0)
             sum_ref[...] += jnp.sum(term.reshape(B // 8, 8, B), axis=0)
 
-    sum_ref[...] = jnp.broadcast_to(jnp.sum(sum_ref[...], keepdims=True), sum_ref.shape)
+    total_sum = jnp.sum(sum_ref[...], keepdims=True)
+    sum_ref[...] = jnp.broadcast_to(total_sum, sum_ref.shape)
+    if first:
+        sum_ref[...] += sums_in[...]
+
+
+def square_a_kernel(where, own, acc_in, right, far, squared_ref, sum_ref):
+    square_late_kernel(0, where, own, acc_in, right, far, None, squared_ref, sum_ref)
+
+
+def square_b_kernel(where, own, acc_in, right, far, sums_in, squared_ref, sum_ref):
+    first = squared_ref.shape[0]
+    square_late_kernel(first, where, own, acc_in, right, far, sums_in, squared_ref, sum_ref)
 
 
 def add_kernel(left, right, out):
     out[...] = left[...] + right[...]
 
 
+def tick_kernel(left, out):
+    out[...] = left[...]
+
+
 def add_planes_kernel(own, first, second, third, out):
     out[...] = (own[...] + first[...]) + (second[...] + third[...])
 
 
-def turn_kernel(where, squared, same_ref, cross_ref):
+def turn_kernel(where, squared_a, squared_b, same_ref, cross_ref):
     core = where[0] % 2
     half = same_ref.shape[0]
-
-    def body(a, b, part):
-        for out, h in ((same_ref, core), (cross_ref, 1 - core)):
-            lanes = pl.ds(pl.multiple_of(h * half + b * B, B), B)
-            out[part[1], part[0]] = squared[part[0], lanes].T
-
-    blocks(half, half, body)
-
-
-def own_square_kernel(where, panel, other, far, far_other, out):
+    count = squared_a.shape[0]
+    for i, squared in enumerate((squared_a, squared_b)):
+
+        def body(a, b, part):
+            for out, h in ((same_ref, core), (cross_ref, 1 - core)):
+                lanes = pl.ds(pl.multiple_of(h * half + b * B, B), B)
+                there = pl.ds(pl.multiple_of(i * count + a * B, B), B)
+                out[part[1], there] = squared[part[0], lanes].T
+
+        blocks(count, half, body)
+
+
+def own_square_kernel(where, panel, other, far_a, far_b, far_other_a, far_other_b, *refs):
+    out, far, far_other = refs
+    half = far_a.shape[0]
+    for whole, a_half, b_half in ((far, far_a, far_b), (far_other, far_other_a, far_other_b)):
+        whole[:half] = a_half[...]
+        whole[half:] = b_half[...]
     row, col = where[0], where[1]
     core, chip = row % 2, row // 2
     rows = out.shape[0]
@@ -180,10 +213,13 @@
     return sources
 
 
-def cubic_early_kernel(where, squared, local_square, right, acc):
+def cubic_early_kernel(where, squared_a, squared_b, local_square, right, acc):
     row, col = where[0], where[1]
     chip = row // 2
-    multiply(acc, squared, right.at[pl.ds(2 * col, 2)], True)
+    half = squared_a.shape[0]
+    own_right = right.at[pl.ds(2 * col, 2)]
+    acc[:half] = piece(squared_a, own_right)
+    acc[half:] = piece(squared_b, own_right)
 
     @pl.when(chip != col)
     def _():
@@ -197,8 +233,10 @@
     )
 
 
-def cubic_middle_kernel(where, acc_in, right_all, same, cross, acc):
-    row, col = where[0], where[1]
+def cubic_middle_kernel(where, acc_in, turn1, turn2, right_all, same, cross, acc):
+    row, col = where[0], where[1]
+    half = turn1.shape[0]
+    sources = late_sources(row, col)
 
     @pl.when(row // 2 == col)
     def _():
@@ -206,38 +244,47 @@
 
     @pl.when(row // 2 != col)
     def _():
-        acc[...] = acc_in[...]
-
-
-def cubic_late_kernel(where, own, squared, acc, turn1, turn2, right_all, *refs):
+        acc[:half] = (
+            acc_in[:half]
+            + piece(turn1, right_all.at[pl.ds(2 * sources[0], 2)])
+            + piece(turn2, right_all.at[pl.ds(2 * sources[1], 2)])
+        )
+        acc[half:] = acc_in[half:]
+
+
+def cubic_late_kernel(where, own, squared_a, squared_b, acc, turn1, turn2, right_all, *refs):
     sides, purified_ref, scratch = refs[:4], refs[4], refs[5]
     row, col = where[0], where[1]
     core, chip = row % 2, row // 2
-    rows, _ = squared.shape
+    rows, _ = acc.shape
+    half = squared_a.shape[0]
     sources = late_sources(row, col)
 
-    def finish(first, second):
-        scratch[...] = acc[...] + first
-        total = scratch[...] + second()
+    def finish(total, first):
         kept = own[rows : rows + EXTRA, :].astype(jnp.float32)
-        for a in range(rows // B):
+        squared = squared_b if first else squared_a
+        for a in range(half // B):
             part = slice(a * B, (a + 1) * B)
+            whole = slice(first + a * B, first + (a + 1) * B)
+            line = first // B + a
             wide = squared[part, :].astype(jnp.float32)
-            purified_ref[part, :] = 3.0 * wide - 2.0 * (total[part] * kept[a : a + 1])
+            purified_ref[whole, :] = 3.0 * wide - 2.0 * (total[part] * kept[line : line + 1])
 
     @pl.when(chip != col)
     def _():
+        scratch[half:] = acc[half:] + piece(turn1, right_all.at[pl.ds(2 * sources[0], 2)])
+        finish(acc, 0)
         finish(
-            piece(turn1, right_all.at[pl.ds(2 * sources[0], 2)]),
-            lambda: piece(turn2, right_all.at[pl.ds(2 * sources[1], 2)]),
+            scratch[half:] + piece(turn2, right_all.at[pl.ds(2 * sources[1], 2)]),
+            half,
         )
 
     @pl.when(chip == col)
     def _():
-        finish(
-            side_piece(sides[:2], right_all, col ^ 2, core),
-            lambda: side_piece(sides[2:], right_all, col ^ 3, core),
-        )
+        scratch[...] = acc[...] + side_piece(sides[:2], right_all, col ^ 2, core)
+        total = scratch[...] + side_piece(sides[2:], right_all, col ^ 3, core)
+        finish(total[:half], 0)
+        finish(total[half:], half)
 
 
 ANYWHERE = pl.BlockSpec(memory_space=pl.ANY)
@@ -307,9 +354,13 @@
     kept = jnp.repeat(pattern.astype(jnp.bfloat16), B, axis=1)
     kept = jnp.pad(kept, ((0, EXTRA - kept.shape[0]), (0, 0)))
     own = jnp.concatenate([masked, kept], axis=0)
-    cross = lax.ppermute(own, "col", [(i, i ^ 3) for i in range(4)])
-    pair = lax.ppermute(own, "col", [(i, i ^ 1) for i in range(4)])
-    far = lax.ppermute(cross, "col", [(i, i ^ 1) for i in range(4)])
+    half = rows // 2
+    near, flip = [(i, i ^ 1) for i in range(4)], [(i, i ^ 3) for i in range(4)]
+    cross_a = lax.ppermute(own[:half], "col", flip)
+    cross_b = lax.ppermute(own[half:], "col", flip)
+    pair = lax.ppermute(own, "col", near)
+    far_a = lax.ppermute(cross_a, "col", near)
+    far_b = lax.ppermute(cross_b, "col", near)
     rights = column_gather(masked)
 
     flops = 2 * 2 * rows * rows * columns
@@ -318,8 +369,8 @@
     wide = jax.ShapeDtypeStruct((rows, columns), jnp.float32)
     partial, panel, right = call(
         square_early_kernel,
-        [SCALARS] + [ANYWHERE] * 11,
-        (where, own, pair, cross, *rights),
+        [SCALARS] + [ANYWHERE] * 12,
+        (where, own, pair, cross_a, cross_b, *rights),
         (
             wide,
             jax.ShapeDtypeStruct((3, rows + EXTRA, columns), jnp.bfloat16),
@@ -330,16 +381,29 @@
         24 * size,
     )
     other = swap(panel, 1)
-    squared, sums = call(
-        square_late_kernel,
+    half_tile = jax.ShapeDtypeStruct((half, columns), jnp.bfloat16)
+    sums_shape = jax.ShapeDtypeStruct((8, B), jnp.float32)
+    squared_a, sums = call(
+        square_a_kernel,
         [SCALARS] + [WHOLE] * 4,
-        (where, own, partial, right, far),
-        (tile, jax.ShapeDtypeStruct((8, B), jnp.float32)),
-        [],
-        flops,
-        8 * size,
-    )
-    turns = [rotate(squared, 1), rotate(squared, 2)]
+        (where, own, partial, right, far_a),
+        (half_tile, sums_shape),
+        [],
+        flops // 2,
+        6 * size,
+    )
+    turns_a = [rotate(squared_a, i) for i in (1, 2)]
+    sums = call(tick_kernel, [WHOLE], (sums,), sums_shape, [], 0, 8 * sums.size, 1)
+    squared_b, sums = call(
+        square_b_kernel,
+        [SCALARS] + [WHOLE] * 5,
+        (where, own, partial, right, far_b, sums),
+        (half_tile, sums_shape),
+        [],
+        flops // 2,
+        6 * size,
+    )
+    turns_b = [rotate(squared_b, i) for i in (1, 2)]
     total = sums
 
     def add(left, right):
@@ -359,8 +423,8 @@
     quarter = jax.ShapeDtypeStruct((rows, rows), jnp.bfloat16)
     turned = call(
         turn_kernel,
-        [SCALARS, WHOLE],
-        (where, squared),
+        [SCALARS, WHOLE, WHOLE],
+        (where, squared_a, squared_b),
         (quarter, quarter),
         [],
         0,
@@ -369,18 +433,18 @@
     sides = to_corner(*turned)
     local_square = call(
         own_square_kernel,
-        [SCALARS] + [WHOLE] * 4,
-        (where, panel, other, far, swap(far, 1)),
+        [SCALARS] + [WHOLE] * 6,
+        (where, panel, other, far_a, far_b, swap(far_a, 1), swap(far_b, 1)),
         tile,
-        [],
+        [pltpu.VMEM((rows + EXTRA, columns), jnp.bfloat16)] * 2,
         4 * flops,
         9 * size,
         16,
     )
     cubic = call(
         cubic_early_kernel,
-        [SCALARS] + [WHOLE] * 3,
-        (where, squared, local_square, right),
+        [SCALARS] + [WHOLE] * 4,
+        (where, squared_a, squared_b, local_square, right),
         wide,
         [],
         2 * flops,
@@ -389,8 +453,8 @@
     )
     cubic = call(
         cubic_middle_kernel,
-        [SCALARS] + [WHOLE] * 4,
-        (where, cubic, right, *sides[:2]),
+        [SCALARS] + [WHOLE] * 6,
+        (where, cubic, *turns_a, right, *sides[:2]),
         wide,
         [],
         flops,
@@ -409,8 +473,8 @@
     )
     purified = call(
         cubic_late_kernel,
-        [SCALARS] + [WHOLE] * 10,
-        (where, own, squared, cubic, *turns, right, *sides[2:]),
+        [SCALARS] + [WHOLE] * 11,
+        (where, own, squared_a, squared_b, cubic, *turns_b, right, *sides[2:]),
         wide,
         [pltpu.VMEM((rows, columns), jnp.float32)],
         2 * flops,

time: 217 us -> 208 us (0.959)
  the two profiles are of different devices: /device:TPU:5 before, /device:TPU:0 now
where the time goes in v7:
time: 208 us
  waiting for transfers between devices  136 us (65%)
  starting transfers between devices  38.6 us (19%)
  Pallas kernels  23.6 us (11%)
  local copies, waits for them, and re-layouts  4.85 us (2%)
  between operations  2.71 us (1%)
    ppermute x7, waiting for transfers between devices, in_plane(): return lax.ppermute(x, ('row', 'col'), pairs)  38.2 us
    ppermute x13, waiting for transfers between devices, swap(): return lax.ppermute(x, 'row', [(i, i ^ k) for i in range(8)])  26.1 us
    ppermute x1, waiting for transfers between devices, local(): cross_a = lax.ppermute(own[:half], 'col', flip)  24.6 us
    pallas_call x13, Pallas kernels, call(): pl.pallas_call(kernel, out_shape=outs, in_specs=specs, out_specs=jax.tree...  23.6 us
    ppermute x1, waiting for transfers between devices, local(): pair = lax.ppermute(own, 'col', near)  17.4 us
    ppermute x1, waiting for transfers between devices, local(): far_b = lax.ppermute(cross_b, 'col', near)  13.4 us
    ppermute x1, waiting for transfers between devices, local(): far_a = lax.ppermute(cross_a, 'col', near)  10.9 us
    ppermute x13, starting transfers between devices, swap(): return lax.ppermute(x, 'row', [(i, i ^ k) for i in range(8)])  10.5 us
  transfers between devices with their start and end apart: 32, of which 16 were waited for; matrix products, arithmetic and copies ran while one was open for 0% of the time, Pallas kernels for 6%

profile of v7, /device:TPU:0, one launch (start us, length us, event | category | flops | bytes accessed | tf_op | source)
XLA Modules:
  0.0 207.6 jit_solution(17046504912901971543)
XLA Ops:
  2.6 3.0 %collective-permute-start.4 = (bf16[512,1024]{1,0:T(8,128)(2,1)S(1)}, bf16[512,1024]{1,0:T(8,128)(2,1)}, u32[]{:S(2)}, u32[]{:S(2)}) collective-permute-start(bf16[512,1024]{1,0:T(8,128)(2,1)S(1)} %fusion.1.refs_0_), channel_id=1, source_target_pairs={{0,8},{4,12},{8,0},{12,4},{16,24},{20,28},{24,16},{28,20},{1,9},{5... | collective-permute-start | bytes 3145736 | tf_op jit(solution)/shard_map/ppermute | solution.py:309
  7.2 21.7 %collective-permute-done.4.refs_2_ = bf16[512,1024]{1,0:T(8,128)(2,1)} collective-permute-done((bf16[512,1024]{1,0:T(8,128)(2,1)S(1)}, bf16[512,1024]{1,0:T(8,128)(2,1)}, u32[]{:S(2)}, u32[]{:S(2)}) %collective-permute-start.4) | collective-permute-done | bytes 1048608 | tf_op jit(solution)/shard_map/ppermute | solution.py:309
  28.9 1.8 collective-permute-start.8
  30.9 3.7 %collective-permute-start.2 = (bf16[272,1024]{1,0:T(8,128)(2,1)S(1)}, bf16[272,1024]{1,0:T(8,128)(2,1)S(1)}, u32[]{:S(2)}, u32[]{:S(2)}) collective-permute-start(bf16[272,1024]{1,0:T(8,128)(2,1)S(1)} %slice.13), channel_id=1, source_target_pairs={{0,3},{1,2},{2,1},{3,0},{4,7},{5,6},{6,5},{7,4},{8,11},{9,10},{10,... | collective-permute-start | bytes 1671176 | tf_op jit(solution)/shard_map/ppermute | solution.py:360
  34.9 24.6 %collective-permute-done.1.cross_a = bf16[256,1024]{1,0:T(8,128)(2,1)S(1)} collective-permute-done((bf16[256,1024]{1,0:T(8,128)(2,1)S(1)}, bf16[256,1024]{1,0:T(8,128)(2,1)S(1)}, u32[]{:S(2)}, u32[]{:S(2)}) %collective-permute-start.1) | collective-permute-done | bytes 524320 | tf_op jit(solution)/shard_map/ppermute | solution.py:359
  63.2 17.4 %collective-permute-done.pair = bf16[528,1024]{1,0:T(8,128)(2,1)S(1)} collective-permute-done((bf16[528,1024]{1,0:T(8,128)(2,1)S(1)}, bf16[528,1024]{1,0:T(8,128)(2,1)S(1)}, u32[]{:S(2)}, u32[]{:S(2)}) %collective-permute-start) | collective-permute-done | bytes 1081376 | tf_op jit(solution)/shard_map/ppermute | solution.py:361
  82.7 5.8 %shard_map.41 = (f32[512,1024]{1,0:T(8,128)S(1)}, bf16[3,528,1024]{2,1,0:T(8,128)(2,1)S(1)}, bf16[8,512,1024]{2,1,0:T(8,128)(2,1)S(1)}) custom-call(s32[2]{0:T(128)S(1)} %pad_add_fusion.where, bf16[528,1024]{1,0:T(8,128)(2,1)S(1)} %fusion.2.own, bf16[528,1024]{1,0:T(8,128)(2,1)S(1)} %collective-permute-done.pair, bf16[256,1024]{1,0:T(8,128)(2,1)S(1)} %copy-done.3, ...), custom_call_target="tpu_custom_call" | custom-call | flops 3221225472 | bytes 25165824 | tf_op jit(solution)/shard_map/pallas_call | solution.py:297
  88.6 8.5 %collective-permute-start.11 = (bf16[272,1024]{1,0:T(8,128)(2,1)S(1)}, bf16[272,1024]{1,0:T(8,128)(2,1)S(1)}, u32[]{:S(2)}, u32[]{:S(2)}) collective-permute-start(bf16[272,1024]{1,0:T(8,128)(2,1)S(1)} %copy-done.1), channel_id=1, source_target_pairs={{0,1},{1,0},{2,3},{3,2},{4,5},{5,4},{6,7},{7,6},{8,9},{9,8},{10,11... | collective-permute-start | bytes 1671176 | tf_op jit(solution)/shard_map/ppermute | solution.py:363
  97.1 13.4 %collective-permute-done.11.far.far_b = bf16[272,1024]{1,0:T(8,128)(2,1)S(1)} collective-permute-done((bf16[272,1024]{1,0:T(8,128)(2,1)S(1)}, bf16[272,1024]{1,0:T(8,128)(2,1)S(1)}, u32[]{:S(2)}, u32[]{:S(2)}) %collective-permute-start.11) | collective-permute-done | bytes 557088 | tf_op jit(solution)/shard_map/ppermute | solution.py:363
  110.5 10.9 %collective-permute-done.10.far.far_a = bf16[256,1024]{1,0:T(8,128)(2,1)S(1)} collective-permute-done((bf16[256,1024]{1,0:T(8,128)(2,1)S(1)}, bf16[256,1024]{1,0:T(8,128)(2,1)S(1)}, u32[]{:S(2)}, u32[]{:S(2)}) %collective-permute-start.10) | collective-permute-done | bytes 524320 | tf_op jit(solution)/shard_map/ppermute | solution.py:362
  126.5 2.8 %collective-permute-done.27.right = f32[8,128]{1,0:T(8,128)S(1)} collective-permute-done((f32[8,128]{1,0:T(8,128)S(1)}, f32[8,128]{1,0:T(8,128)S(1)}, u32[]{:S(2)}, u32[]{:S(2)}) %collective-permute-start.27) | collective-permute-done | bytes 4128 | tf_op jit(solution)/shard_map/ppermute | solution.py:309
  131.0 1.8 shard_map.47
  135.4 3.4 %collective-permute-start.29 = (f32[8,128]{1,0:T(8,128)S(1)}, f32[8,128]{1,0:T(8,128)S(1)}, u32[]{:S(2)}, u32[]{:S(2)}) collective-permute-start(f32[8,128]{1,0:T(8,128)S(1)} %shard_map.52.own), channel_id=1, source_target_pairs={{0,1},{1,0},{2,3},{3,2},{4,5},{5,4},{6,7},{7,6},{8,9},{9,8},{10,11... | collective-permute-start | bytes 12296 | tf_op jit(solution)/shard_map/ppermute | solution.py:463
  141.2 2.1 collective-permute-done.30.second
  144.0 1.8 collective-permute-done.31.third
  146.5 3.0 %collective-permute-done.17.same = bf16[512,512]{1,0:T(8,128)(2,1)S(1)} collective-permute-done((bf16[512,512]{1,0:T(8,128)(2,1)S(1)}, bf16[512,512]{1,0:T(8,128)(2,1)S(1)}, u32[]{:S(2)}, u32[]{:S(2)}) %collective-permute-start.17) | collective-permute-done | bytes 524320 | tf_op jit(solution)/shard_map/ppermute | solution.py:338
  150.2 6.1 %collective-permute-done.18.cross = bf16[512,512]{1,0:T(8,128)(2,1)S(1)} collective-permute-done((bf16[512,512]{1,0:T(8,128)(2,1)S(1)}, bf16[512,512]{1,0:T(8,128)(2,1)S(1)}, u32[]{:S(2)}, u32[]{:S(2)}) %collective-permute-start.18) | collective-permute-done | bytes 524320 | tf_op jit(solution)/shard_map/ppermute | solution.py:338
  162.0 9.8 %collective-permute-done.21.refs_0_ = bf16[512,512]{1,0:T(8,128)(2,1)S(1)} collective-permute-done((bf16[512,512]{1,0:T(8,128)(2,1)S(1)}, bf16[512,512]{1,0:T(8,128)(2,1)S(1)}, u32[]{:S(2)}, u32[]{:S(2)}) %collective-permute-start.21) | collective-permute-done | bytes 524320 | tf_op jit(solution)/shard_map/ppermute | solution.py:338
  174.0 5.1 %shard_map.45.local_square = bf16[512,1024]{1,0:T(8,128)(2,1)S(1)} custom-call(s32[2]{0:T(128)S(1)} %pad_add_fusion.where, bf16[3,528,1024]{2,1,0:T(8,128)(2,1)S(1)} %get-tuple-element.16.panel, bf16[3,528,1024]{2,1,0:T(8,128)(2,1)S(1)} %collective-permute-done.12.other, bf16[256,1024]{1,0:T(8,128)(2,1)S(1)} %collective-permute-done.10.far.far_a, ...), custom_call_target="tpu_custom_call" | custom-call | flops 4294967296 | bytes 9437184 | tf_op jit(solution)/shard_map/pallas_call | solution.py:297
  179.1 1.8 shard_map.46.acc_in
  180.9 1.8 shard_map.48.acc
  182.7 12.7 %collective-permute-done.22.refs_1_ = bf16[512,512]{1,0:T(8,128)(2,1)S(1)} collective-permute-done((bf16[512,512]{1,0:T(8,128)(2,1)S(1)}, bf16[512,512]{1,0:T(8,128)(2,1)S(1)}, u32[]{:S(2)}, u32[]{:S(2)}) %collective-permute-start.22) | collective-permute-done | bytes 524320 | tf_op jit(solution)/shard_map/ppermute | solution.py:338
  195.4 6.7 %collective-permute-done.25.refs_3_ = bf16[512,512]{1,0:T(8,128)(2,1)S(1)} collective-permute-done((bf16[512,512]{1,0:T(8,128)(2,1)S(1)}, bf16[512,512]{1,0:T(8,128)(2,1)S(1)}, u32[]{:S(2)}, u32[]{:S(2)}) %collective-permute-start.25) | collective-permute-done | bytes 524320 | tf_op jit(solution)/shard_map/ppermute | solution.py:338
  202.1 4.4 %shard_map.49 = f32[512,1024]{1,0:T(8,128)} custom-call(s32[2]{0:T(128)S(1)} %pad_add_fusion.where, bf16[528,1024]{1,0:T(8,128)(2,1)S(1)} %fusion.2.own, bf16[256,1024]{1,0:T(8,128)(2,1)S(1)} %get-tuple-element.13.squared_a, bf16[256,1024]{1,0:T(8,128)(2,1)S(1)} %get-tuple-element.15.squared_b, f32[512,1024]{1,0:T(8,128)S(1)} %shard_map.48.acc, ...), custom_call_target="tpu_custom_call" | custom-call | flops 2147483648 | bytes 16777216 | tf_op jit(solution)/shard_map/pallas_call | solution.py:297
  (73 shorter events, 30.9 us)
Async XLA Ops:
  2.6 26.3 %collective-permute-start.4 = (bf16[512,1024]{1,0:T(8,128)(2,1)S(1)}, bf16[512,1024]{1,0:T(8,128)(2,1)}, u32[]{:S(2)}, u32[]{:S(2)}) collective-permute-start(bf16[512,1024]{1,0:T(8,128)(2,1)S(1)} %fusion.1.refs_0_), channel_id=1, source_target_pairs={{0,8},{4,12},{8,0},{12,4},{16,24},{20,28},{24,16},{28,20},{1,9},{5... | collective-permute-start | bytes 3145736 | tf_op jit(solution)/shard_map/ppermute | solution.py:309
  5.6 56.1 %collective-permute-start.6 = (bf16[512,1024]{1,0:T(8,128)(2,1)S(1)}, bf16[512,1024]{1,0:T(8,128)(2,1)}, u32[]{:S(2)}, u32[]{:S(2)}) collective-permute-start(bf16[512,1024]{1,0:T(8,128)(2,1)S(1)} %fusion.1.refs_0_), channel_id=1, source_target_pairs={{0,16},{4,20},{8,24},{12,28},{16,0},{20,4},{24,8},{28,12},{1,17},{... | collective-permute-start | bytes 3145736 | tf_op jit(solution)/shard_map/ppermute | solution.py:309
  28.9 32.8 %collective-permute-start.8 = (bf16[512,1024]{1,0:T(8,128)(2,1)}, bf16[512,1024]{1,0:T(8,128)(2,1)}, u32[]{:S(2)}, u32[]{:S(2)}) collective-permute-start(bf16[512,1024]{1,0:T(8,128)(2,1)} %collective-permute-done.4.refs_2_), channel_id=1, source_target_pairs={{0,16},{4,20},{8,24},{12,28},{16,0},{20,4},{24,8},{28,12},{1,17},{... | collective-permute-start | bytes 3145736 | tf_op jit(solution)/shard_map/ppermute | solution.py:309
  30.9 29.5 %collective-permute-start.2 = (bf16[272,1024]{1,0:T(8,128)(2,1)S(1)}, bf16[272,1024]{1,0:T(8,128)(2,1)S(1)}, u32[]{:S(2)}, u32[]{:S(2)}) collective-permute-start(bf16[272,1024]{1,0:T(8,128)(2,1)S(1)} %slice.13), channel_id=1, source_target_pairs={{0,3},{1,2},{2,1},{3,0},{4,7},{5,6},{6,5},{7,4},{8,11},{9,10},{10,... | collective-permute-start | bytes 1671176 | tf_op jit(solution)/shard_map/ppermute | solution.py:360
  34.6 24.9 %collective-permute-start.1 = (bf16[256,1024]{1,0:T(8,128)(2,1)S(1)}, bf16[256,1024]{1,0:T(8,128)(2,1)S(1)}, u32[]{:S(2)}, u32[]{:S(2)}) collective-permute-start(bf16[256,1024]{1,0:T(8,128)(2,1)S(1)} %slice.12), channel_id=1, source_target_pairs={{0,3},{1,2},{2,1},{3,0},{4,7},{5,6},{6,5},{7,4},{8,11},{9,10},{10,... | collective-permute-start | bytes 1572872 | tf_op jit(solution)/shard_map/ppermute | solution.py:359
  34.9 45.7 %collective-permute-start = (bf16[528,1024]{1,0:T(8,128)(2,1)S(1)}, bf16[528,1024]{1,0:T(8,128)(2,1)S(1)}, u32[]{:S(2)}, u32[]{:S(2)}) collective-permute-start(bf16[528,1024]{1,0:T(8,128)(2,1)S(1)} %fusion.2.own), channel_id=1, source_target_pairs={{0,1},{1,0},{2,3},{3,2},{4,5},{5,4},{6,7},{7,6},{8,9},{9,8},{10,11... | collective-permute-start | bytes 3244040 | tf_op jit(solution)/shard_map/ppermute | solution.py:361
  61.2 19.4 %collective-permute-start.5 = (bf16[512,1024]{1,0:T(8,128)(2,1)}, bf16[512,1024]{1,0:T(8,128)(2,1)}, u32[]{:S(2)}, u32[]{:S(2)}) collective-permute-start(bf16[512,1024]{1,0:T(8,128)(2,1)} %collective-permute-done.4.refs_2_), channel_id=1, source_target_pairs={{0,4},{4,0},{8,12},{12,8},{16,20},{20,16},{24,28},{28,24},{1,5},{5... | collective-permute-start | bytes 3145736 | tf_op jit(solution)/shard_map/ppermute | solution.py:309
  61.7 18.9 %collective-permute-start.7 = (bf16[512,1024]{1,0:T(8,128)(2,1)}, bf16[512,1024]{1,0:T(8,128)(2,1)}, u32[]{:S(2)}, u32[]{:S(2)}) collective-permute-start(bf16[512,1024]{1,0:T(8,128)(2,1)} %collective-permute-done.6.refs_4_), channel_id=1, source_target_pairs={{0,4},{4,0},{8,12},{12,8},{16,20},{20,16},{24,28},{28,24},{1,5},{5... | collective-permute-start | bytes 3145736 | tf_op jit(solution)/shard_map/ppermute | solution.py:309
  61.7 18.9 %collective-permute-start.9 = (bf16[512,1024]{1,0:T(8,128)(2,1)}, bf16[512,1024]{1,0:T(8,128)(2,1)}, u32[]{:S(2)}, u32[]{:S(2)}) collective-permute-start(bf16[512,1024]{1,0:T(8,128)(2,1)} %collective-permute-done.8.refs_6_), channel_id=1, source_target_pairs={{0,4},{4,0},{8,12},{12,8},{16,20},{20,16},{24,28},{28,24},{1,5},{5... | collective-permute-start | bytes 3145736 | tf_op jit(solution)/shard_map/ppermute | solution.py:309
  88.5 84.0 %collective-permute-start.12 = (bf16[3,528,1024]{2,1,0:T(8,128)(2,1)S(1)}, bf16[3,528,1024]{2,1,0:T(8,128)(2,1)S(1)}, u32[]{:S(2)}, u32[]{:S(2)}) collective-permute-start(bf16[3,528,1024]{2,1,0:T(8,128)(2,1)S(1)} %get-tuple-element.16.panel), channel_id=1, source_target_pairs={{0,4},{4,0},{8,12},{12,8},{16,20},{20,16},{24,28},{28,24},{1,5},{5... | collective-permute-start | bytes 9732104 | tf_op jit(solution)/shard_map/ppermute | solution.py:309
  88.6 22.0 %collective-permute-start.11 = (bf16[272,1024]{1,0:T(8,128)(2,1)S(1)}, bf16[272,1024]{1,0:T(8,128)(2,1)S(1)}, u32[]{:S(2)}, u32[]{:S(2)}) collective-permute-start(bf16[272,1024]{1,0:T(8,128)(2,1)S(1)} %copy-done.1), channel_id=1, source_target_pairs={{0,1},{1,0},{2,3},{3,2},{4,5},{5,4},{6,7},{7,6},{8,9},{9,8},{10,11... | collective-permute-start | bytes 1671176 | tf_op jit(solution)/shard_map/ppermute | solution.py:363
  97.1 24.4 %collective-permute-start.10 = (bf16[256,1024]{1,0:T(8,128)(2,1)S(1)}, bf16[256,1024]{1,0:T(8,128)(2,1)S(1)}, u32[]{:S(2)}, u32[]{:S(2)}) collective-permute-start(bf16[256,1024]{1,0:T(8,128)(2,1)S(1)} %copy-done.3), channel_id=1, source_target_pairs={{0,1},{1,0},{2,3},{3,2},{4,5},{5,4},{6,7},{7,6},{8,9},{9,8},{10,11... | collective-permute-start | bytes 1572872 | tf_op jit(solution)/shard_map/ppermute | solution.py:362
  110.5 28.2 %collective-permute-start.14 = (bf16[272,1024]{1,0:T(8,128)(2,1)S(1)}, bf16[272,1024]{1,0:T(8,128)(2,1)S(1)}, u32[]{:S(2)}, u32[]{:S(2)}) collective-permute-start(bf16[272,1024]{1,0:T(8,128)(2,1)S(1)} %collective-permute-done.11.far.far_b), channel_id=1, source_target_pairs={{0,4},{4,0},{8,12},{12,8},{16,20},{20,16},{24,28},{28,24},{1,5},{5... | collective-permute-start | bytes 1671176 | tf_op jit(solution)/shard_map/ppermute | solution.py:309
  132.8 16.7 %collective-permute-start.17 = (bf16[512,512]{1,0:T(8,128)(2,1)S(1)}, bf16[512,512]{1,0:T(8,128)(2,1)S(1)}, u32[]{:S(2)}, u32[]{:S(2)}) collective-permute-start(bf16[512,512]{1,0:T(8,128)(2,1)S(1)} %get-tuple-element.17), channel_id=1, source_target_pairs={{8,0},{12,4},{1,9},{5,13},{26,18},{30,22},{19,27},{23,31}} | collective-permute-start | bytes 1572872 | tf_op jit(solution)/shard_map/ppermute | solution.py:338
  134.1 22.2 %collective-permute-start.18 = (bf16[512,512]{1,0:T(8,128)(2,1)S(1)}, bf16[512,512]{1,0:T(8,128)(2,1)S(1)}, u32[]{:S(2)}, u32[]{:S(2)}) collective-permute-start(bf16[512,512]{1,0:T(8,128)(2,1)S(1)} %get-tuple-element.18), channel_id=1, source_target_pairs={{8,4},{12,0},{1,13},{5,9},{26,22},{30,18},{19,31},{23,27}} | collective-permute-start | bytes 1572872 | tf_op jit(solution)/shard_map/ppermute | solution.py:338
  143.3 15.4 %collective-permute-start.15 = (bf16[256,1024]{1,0:T(8,128)(2,1)S(1)}, bf16[256,1024]{1,0:T(8,128)(2,1)S(1)}, u32[]{:S(2)}, u32[]{:S(2)}) collective-permute-start(bf16[256,1024]{1,0:T(8,128)(2,1)S(1)} %get-tuple-element.13.squared_a), channel_id=1, source_target_pairs={{1,2},{2,3},{3,1},{5,6},{6,7},{7,5},{8,10},{10,11},{11,8},{12,14},... | collective-permute-start | bytes 1572872 | tf_op jit(solution)/shard_map/ppermute | solution.py:328
  145.8 14.3 %collective-permute-start.16 = (bf16[256,1024]{1,0:T(8,128)(2,1)S(1)}, bf16[256,1024]{1,0:T(8,128)(2,1)S(1)}, u32[]{:S(2)}, u32[]{:S(2)}) collective-permute-start(bf16[256,1024]{1,0:T(8,128)(2,1)S(1)} %get-tuple-element.13.squared_a), channel_id=1, source_target_pairs={{1,3},{2,1},{3,2},{5,7},{6,5},{7,6},{8,11},{10,8},{11,10},{12,15},... | collective-permute-start | bytes 1572872 | tf_op jit(solution)/shard_map/ppermute | solution.py:328
  149.5 11.9 %collective-permute-start.24 = (bf16[512,512]{1,0:T(8,128)(2,1)S(1)}, bf16[512,512]{1,0:T(8,128)(2,1)S(1)}, u32[]{:S(2)}, u32[]{:S(2)}) collective-permute-start(bf16[512,512]{1,0:T(8,128)(2,1)S(1)} %get-tuple-element.18), channel_id=1, source_target_pairs={{24,8},{28,12},{17,1},{21,5},{10,26},{14,30},{3,19},{7,23}} | collective-permute-start | bytes 1572872 | tf_op jit(solution)/shard_map/ppermute | solution.py:338
  156.2 15.6 %collective-permute-start.21 = (bf16[512,512]{1,0:T(8,128)(2,1)S(1)}, bf16[512,512]{1,0:T(8,128)(2,1)S(1)}, u32[]{:S(2)}, u32[]{:S(2)}) collective-permute-start(bf16[512,512]{1,0:T(8,128)(2,1)S(1)} %get-tuple-element.17), channel_id=1, source_target_pairs={{16,0},{20,4},{25,9},{29,13},{2,18},{6,22},{11,27},{15,31}} | collective-permute-start | bytes 1572872 | tf_op jit(solution)/shard_map/ppermute | solution.py:338
  158.7 36.7 %collective-permute-start.22 = (bf16[512,512]{1,0:T(8,128)(2,1)S(1)}, bf16[512,512]{1,0:T(8,128)(2,1)S(1)}, u32[]{:S(2)}, u32[]{:S(2)}) collective-permute-start(bf16[512,512]{1,0:T(8,128)(2,1)S(1)} %get-tuple-element.18), channel_id=1, source_target_pairs={{16,4},{20,0},{25,13},{29,9},{2,22},{6,18},{11,31},{15,27}} | collective-permute-start | bytes 1572872 | tf_op jit(solution)/shard_map/ppermute | solution.py:338
  160.0 35.4 %collective-permute-start.23 = (bf16[512,512]{1,0:T(8,128)(2,1)S(1)}, bf16[512,512]{1,0:T(8,128)(2,1)S(1)}, u32[]{:S(2)}, u32[]{:S(2)}) collective-permute-start(bf16[512,512]{1,0:T(8,128)(2,1)S(1)} %get-tuple-element.17), channel_id=1, source_target_pairs={{24,0},{28,4},{17,9},{21,13},{10,18},{14,22},{3,27},{7,31}} | collective-permute-start | bytes 1572872 | tf_op jit(solution)/shard_map/ppermute | solution.py:338
  161.3 34.1 %collective-permute-start.19 = (bf16[256,1024]{1,0:T(8,128)(2,1)S(1)}, bf16[256,1024]{1,0:T(8,128)(2,1)S(1)}, u32[]{:S(2)}, u32[]{:S(2)}) collective-permute-start(bf16[256,1024]{1,0:T(8,128)(2,1)S(1)} %get-tuple-element.15.squared_b), channel_id=1, source_target_pairs={{1,2},{2,3},{3,1},{5,6},{6,7},{7,5},{8,10},{10,11},{11,8},{12,14},... | collective-permute-start | bytes 1572872 | tf_op jit(solution)/shard_map/ppermute | solution.py:328
  171.8 23.6 %collective-permute-start.20 = (bf16[256,1024]{1,0:T(8,128)(2,1)S(1)}, bf16[256,1024]{1,0:T(8,128)(2,1)S(1)}, u32[]{:S(2)}, u32[]{:S(2)}) collective-permute-start(bf16[256,1024]{1,0:T(8,128)(2,1)S(1)} %get-tuple-element.15.squared_b), channel_id=1, source_target_pairs={{1,3},{2,1},{3,2},{5,7},{6,5},{7,6},{8,11},{10,8},{11,10},{12,15},... | collective-permute-start | bytes 1572872 | tf_op jit(solution)/shard_map/ppermute | solution.py:328
  172.5 29.5 %collective-permute-start.25 = (bf16[512,512]{1,0:T(8,128)(2,1)S(1)}, bf16[512,512]{1,0:T(8,128)(2,1)S(1)}, u32[]{:S(2)}, u32[]{:S(2)}) collective-permute-start(bf16[512,512]{1,0:T(8,128)(2,1)S(1)} %collective-permute-done.24), channel_id=1, source_target_pairs={{8,4},{12,0},{1,13},{5,9},{26,22},{30,18},{19,31},{23,27}} | collective-permute-start | bytes 1572872 | tf_op jit(solution)/shard_map/ppermute | solution.py:338
  (13 other events, 43.2 us)

commit v8 on v6

--- a/solution.py
+++ b/solution.py
@@ -1,3 +1,5 @@
+import functools
+
 import jax
 import jax.numpy as jnp
 from jax import lax
@@ -43,7 +45,6 @@
 
 NEAR = (0, 1, 3)
 LAST = 2
-EXTRA = 16
 
 
 def piece(left, right):
@@ -70,6 +71,16 @@
             b,
             (pl.ds(pl.multiple_of(a * B, B), B), pl.ds(pl.multiple_of(b * B, B), B)),
         )
+
+
+def mask_kernel(pattern, density, out, kept_ref):
+    rows, columns = out.shape
+    for a in range(rows // B):
+        for b in range(columns // B):
+            part = (slice(a * B, (a + 1) * B), slice(b * B, (b + 1) * B))
+            kept = pattern[a, b].astype(jnp.float32)
+            kept_ref[a : a + 1, part[1]] = jnp.full((1, B), kept, jnp.float32)
+            out[part] = (density[part].astype(jnp.float32) * kept).astype(jnp.bfloat16)
 
 
 def square_early_kernel(where, own, pair, cross, *refs):
@@ -95,11 +106,11 @@
         pltpu.make_async_copy(there, there, right_sem.at[slot + t]).wait()
 
 
-def square_late_kernel(where, own, acc_in, right, far, squared_ref, sum_ref):
+def square_late_kernel(where, kept_ref, own, acc_in, right, far, squared_ref, sum_ref):
     row, col = where[0], where[1]
     rows, columns = squared_ref.shape
     total = acc_in[...] + piece(far, right.at[pl.ds(2 * (col ^ LAST), 2)])
-    kept = own[rows : rows + EXTRA, :].astype(jnp.float32)
+    kept = kept_ref[...]
     sums = jnp.zeros((8, columns), jnp.float32)
     for a in range(rows // B):
         part = slice(a * B, (a + 1) * B)
@@ -129,8 +140,9 @@
     out[...] = left[...] + right[...]
 
 
-def add_planes_kernel(own, first, second, third, out):
-    out[...] = (own[...] + first[...]) + (second[...] + third[...])
+def add_planes_kernel(order, own, first, second, third, out):
+    total = (own[...] + first[...]) + (second[...] + third[...])
+    out[0, 0] = total[0, 0] / order
 
 
 def turn_kernel(where, squared, same_ref, cross_ref):
@@ -145,7 +157,8 @@
     blocks(half, half, body)
 
 
-def own_square_kernel(where, panel, other, far, far_other, out):
+def own_square_kernel(where, own_pattern, *refs):
+    patterns, (panel, other, far, far_other, out) = (own_pattern, *refs[:3]), refs[3:]
     row, col = where[0], where[1]
     core, chip = row % 2, row // 2
     rows = out.shape[0]
@@ -160,13 +173,16 @@
                 preferred_element_type=jnp.float32,
             )
             total = part if total is None else total + part
-        lanes = pl.ds(pl.multiple_of(h * rows, rows), rows)
-        near = panel[jnp.minimum(d, 2), rows : rows + EXTRA, lanes].astype(jnp.float32)
-        kept = jnp.where(d == LAST, far[rows : rows + EXTRA, lanes].astype(jnp.float32), near)
         for a in range(rows // B):
-            out[a * B : (a + 1) * B, lanes] = (
-                total[a * B : (a + 1) * B] * kept[a : a + 1]
-            ).astype(jnp.bfloat16)
+            for b in range(rows // B):
+                place = h * (rows // B) + b
+                kept = jnp.int32(0)
+                for i, pattern in enumerate(patterns):
+                    kept = jnp.where(d == i, pattern[a, place], kept)
+                lanes = pl.ds(pl.multiple_of(h * rows + b * B, B), B)
+                out[a * B : (a + 1) * B, lanes] = (
+                    total[a * B : (a + 1) * B, b * B : (b + 1) * B] * kept.astype(jnp.float32)
+                ).astype(jnp.bfloat16)
 
 
 def late_sources(row, col):
@@ -209,7 +225,7 @@
         acc[...] = acc_in[...]
 
 
-def cubic_late_kernel(where, own, squared, acc, turn1, turn2, right_all, *refs):
+def cubic_late_kernel(where, kept_ref, squared, acc, turn1, turn2, right_all, *refs):
     sides, purified_ref, scratch = refs[:4], refs[4], refs[5]
     row, col = where[0], where[1]
     core, chip = row % 2, row // 2
@@ -219,7 +235,7 @@
     def finish(first, second):
         scratch[...] = acc[...] + first
         total = scratch[...] + second()
-        kept = own[rows : rows + EXTRA, :].astype(jnp.float32)
+        kept = kept_ref[...]
         for a in range(rows // B):
             part = slice(a * B, (a + 1) * B)
             wide = squared[part, :].astype(jnp.float32)
@@ -246,12 +262,12 @@
 DMA = pltpu.SemaphoreType.DMA
 
 
-def call(kernel, specs, args, outs, scratch, flops, moved, grant=16):
+def call(kernel, specs, args, outs, scratch, flops, moved, grant=16, out_spec=WHOLE):
     return pl.pallas_call(
         kernel,
         out_shape=outs,
         in_specs=specs,
-        out_specs=jax.tree.map(lambda _: WHOLE, outs),
+        out_specs=jax.tree.map(lambda _: out_spec, outs),
         scratch_shapes=scratch,
         compiler_params=pltpu.CompilerParams(vmem_limit_bytes=grant << 20),
         cost_estimate=pl.CostEstimate(flops=flops, bytes_accessed=moved, transcendentals=0),
@@ -300,21 +316,27 @@
 
 
 def local(density, pattern):
-    masked = filtered(density.astype(jnp.float32), pattern).astype(jnp.bfloat16)
-    rows, columns = masked.shape
+    rows, columns = density.shape
     row, col = lax.axis_index("row"), lax.axis_index("col")
     where = jnp.stack([row, col]).astype(jnp.int32)
-    kept = jnp.repeat(pattern.astype(jnp.bfloat16), B, axis=1)
-    kept = jnp.pad(kept, ((0, EXTRA - kept.shape[0]), (0, 0)))
-    own = jnp.concatenate([masked, kept], axis=0)
+    tile = jax.ShapeDtypeStruct((rows, columns), jnp.bfloat16)
+    own, kept = call(
+        mask_kernel,
+        [SCALARS, WHOLE],
+        (pattern, density),
+        (tile, jax.ShapeDtypeStruct((8, columns), jnp.float32)),
+        [],
+        rows * columns,
+        4 * rows * columns,
+    )
     cross = lax.ppermute(own, "col", [(i, i ^ 3) for i in range(4)])
     pair = lax.ppermute(own, "col", [(i, i ^ 1) for i in range(4)])
     far = lax.ppermute(cross, "col", [(i, i ^ 1) for i in range(4)])
-    rights = column_gather(masked)
+    patterns = [lax.ppermute(pattern, "col", [(i, i ^ k) for i in range(4)]) for k in (1, 2, 3)]
+    rights = column_gather(own)
 
     flops = 2 * 2 * rows * rows * columns
     size = 2 * rows * columns
-    tile = jax.ShapeDtypeStruct((rows, columns), jnp.bfloat16)
     wide = jax.ShapeDtypeStruct((rows, columns), jnp.float32)
     partial, panel, right = call(
         square_early_kernel,
@@ -322,7 +344,7 @@
         (where, own, pair, cross, *rights),
         (
             wide,
-            jax.ShapeDtypeStruct((3, rows + EXTRA, columns), jnp.bfloat16),
+            jax.ShapeDtypeStruct((3, rows, columns), jnp.bfloat16),
             jax.ShapeDtypeStruct((8, rows, columns), jnp.bfloat16),
         ),
         [DMA((3,)), DMA((8,))],
@@ -332,8 +354,8 @@
     other = swap(panel, 1)
     squared, sums = call(
         square_late_kernel,
-        [SCALARS] + [WHOLE] * 4,
-        (where, own, partial, right, far),
+        [SCALARS] + [WHOLE] * 5,
+        (where, kept, own, partial, right, far),
         (tile, jax.ShapeDtypeStruct((8, B), jnp.float32)),
         [],
         flops,
@@ -369,8 +391,8 @@
     sides = to_corner(*turned)
     local_square = call(
         own_square_kernel,
-        [SCALARS] + [WHOLE] * 4,
-        (where, panel, other, far, swap(far, 1)),
+        [SCALARS] * 5 + [WHOLE] * 4,
+        (where, pattern, *patterns, panel, other, far, swap(far, 1)),
         tile,
         [],
         4 * flops,
@@ -397,26 +419,27 @@
         9 * size,
     )
     planes = [lax.ppermute(total, "col", [(i, i ^ k) for i in range(4)]) for k in (1, 2, 3)]
-    total = call(
-        add_planes_kernel,
+    occupation = call(
+        functools.partial(add_planes_kernel, rows * lax.axis_size("row")),
         [WHOLE] * 4,
         (total, *planes),
-        jax.ShapeDtypeStruct(total.shape, total.dtype),
+        jax.ShapeDtypeStruct((1, 1), jnp.float32),
         [],
         3 * total.size,
         20 * total.size,
         1,
+        SCALARS,
     )
     purified = call(
         cubic_late_kernel,
         [SCALARS] + [WHOLE] * 10,
-        (where, own, squared, cubic, *turns, right, *sides[2:]),
+        (where, kept, squared, cubic, *turns, right, *sides[2:]),
         wide,
         [pltpu.VMEM((rows, columns), jnp.float32)],
         2 * flops,
         16 * size,
     )
-    return (purified, total[0, 0] / (rows * lax.axis_size("row")))
+    return (purified, occupation.reshape(()))
 
 
 def solution(mesh):

time: 217 us -> 212 us (0.977)
  the two profiles are of different devices: /device:TPU:5 before, /device:TPU:3 now
where the time goes in v8:
time: 212 us
  waiting for transfers between devices  116 us (55%)
  starting transfers between devices  67.7 us (32%)
  Pallas kernels  25.1 us (12%)
    ppermute x12, waiting for transfers between devices, swap(): return lax.ppermute(x, 'row', [(i, i ^ k) for i in range(8)])  59.3 us
    pallas_call x12, Pallas kernels, call(): pl.pallas_call(kernel, out_shape=outs, in_specs=specs, out_specs=jax.tree...  25.1 us
    ppermute x1, waiting for transfers between devices, local(): far = lax.ppermute(cross, 'col', [(i, i ^ 1) for i in range(4)])  23.7 us
    ppermute x2, waiting for transfers between devices, rotate(): return lax.ppermute(x, ('row', 'col'), pairs)  21.8 us
    ppermute x1, starting transfers between devices, local(): far = lax.ppermute(cross, 'col', [(i, i ^ 1) for i in range(4)])  21.5 us
    ppermute x7, starting transfers between devices, in_plane(): return lax.ppermute(x, ('row', 'col'), pairs)  15.8 us
    ppermute x12, starting transfers between devices, swap(): return lax.ppermute(x, 'row', [(i, i ^ k) for i in range(8)])  10.3 us
    ppermute x2, starting transfers between devices, rotate(): return lax.ppermute(x, ('row', 'col'), pairs)  7.08 us
  transfers between devices with their start and end apart: 30, of which 15 were waited for; matrix products, arithmetic and copies ran while one was open for 0% of the time, Pallas kernels for 6%

profile of v8, /device:TPU:3, one launch (start us, length us, event | category | flops | bytes accessed | tf_op | source)
XLA Modules:
  0.0 212.0 jit_solution(17224034477012856438)
XLA Ops:
  6.2 21.4 %collective-permute-done.3.refs_2_ = bf16[512,1024]{1,0:T(8,128)(2,1)S(1)} collective-permute-done((bf16[512,1024]{1,0:T(8,128)(2,1)S(1)}, bf16[512,1024]{1,0:T(8,128)(2,1)S(1)}, u32[]{:S(2)}, u32[]{:S(2)}) %collective-permute-start.3) | collective-permute-done | bytes 1048608 | tf_op jit(solution)/shard_map/ppermute | solution.py:278
  28.8 3.3 %collective-permute-start.1 = (bf16[512,1024]{1,0:T(8,128)(2,1)S(1)}, bf16[512,1024]{1,0:T(8,128)(2,1)}, u32[]{:S(2)}, u32[]{:S(2)}) collective-permute-start(bf16[512,1024]{1,0:T(8,128)(2,1)S(1)} %get-tuple-element.12.own.refs_0_), channel_id=1, source_target_pairs={{0,3},{1,2},{2,1},{3,0},{4,7},{5,6},{6,5},{7,4},{8,11},{9,10},{10,... | collective-permute-start | bytes 3145736 | tf_op jit(solution)/shard_map/ppermute | solution.py:332
  32.1 2.0 collective-permute-start.2
  34.7 16.3 %collective-permute-done.7.refs_6_ = bf16[512,1024]{1,0:T(8,128)(2,1)} collective-permute-done((bf16[512,1024]{1,0:T(8,128)(2,1)S(1)}, bf16[512,1024]{1,0:T(8,128)(2,1)}, u32[]{:S(2)}, u32[]{:S(2)}) %collective-permute-start.7) | collective-permute-done | bytes 1048608 | tf_op jit(solution)/shard_map/ppermute | solution.py:278
  51.0 2.3 %collective-permute-start.8 = (bf16[512,1024]{1,0:T(8,128)(2,1)}, bf16[512,1024]{1,0:T(8,128)(2,1)}, u32[]{:S(2)}, u32[]{:S(2)}) collective-permute-start(bf16[512,1024]{1,0:T(8,128)(2,1)} %collective-permute-done.7.refs_6_), channel_id=1, source_target_pairs={{0,4},{4,0},{8,12},{12,8},{16,20},{20,16},{24,28},{28,24},{1,5},{5... | collective-permute-start | bytes 3145736 | tf_op jit(solution)/shard_map/ppermute | solution.py:278
  55.9 6.2 %shard_map.42 = (f32[512,1024]{1,0:T(8,128)S(1)}, bf16[3,512,1024]{2,1,0:T(8,128)(2,1)S(1)}, bf16[8,512,1024]{2,1,0:T(8,128)(2,1)S(1)}) custom-call(s32[2]{0:T(128)S(1)} %pad_add_fusion.where, bf16[512,1024]{1,0:T(8,128)(2,1)S(1)} %get-tuple-element.12.own.refs_0_, bf16[512,1024]{1,0:T(8,128)(2,1)S(1)} %collective-permute-done.pair, ...), custom_call_target="tpu_custom_call" | custom-call | flops 3221225472 | bytes 25165824 | tf_op jit(solution)/shard_map/pallas_call | solution.py:266
  62.8 21.5 %collective-permute-start.9 = (bf16[512,1024]{1,0:T(8,128)(2,1)}, bf16[512,1024]{1,0:T(8,128)(2,1)S(1)}, u32[]{:S(2)}, u32[]{:S(2)}) collective-permute-start(bf16[512,1024]{1,0:T(8,128)(2,1)} %collective-permute-done.1.cross), channel_id=1, source_target_pairs={{0,1},{1,0},{2,3},{3,2},{4,5},{5,4},{6,7},{7,6},{8,9},{9,8},{10,11... | collective-permute-start | bytes 3145736 | tf_op jit(solution)/shard_map/ppermute | solution.py:334
  84.2 23.7 %collective-permute-done.9.far.refs_5_ = bf16[512,1024]{1,0:T(8,128)(2,1)S(1)} collective-permute-done((bf16[512,1024]{1,0:T(8,128)(2,1)}, bf16[512,1024]{1,0:T(8,128)(2,1)S(1)}, u32[]{:S(2)}, u32[]{:S(2)}) %collective-permute-start.9) | collective-permute-done | bytes 1048608 | tf_op jit(solution)/shard_map/ppermute | solution.py:334
  108.6 2.2 %shard_map.43 = (bf16[512,1024]{1,0:T(8,128)(2,1)S(1)}, f32[8,128]{1,0:T(8,128)S(1)}) custom-call(s32[2]{0:T(128)S(1)} %pad_add_fusion.where, f32[8,1024]{1,0:T(8,128)S(1)} %get-tuple-element.11.kept_ref, bf16[512,1024]{1,0:T(8,128)(2,1)S(1)} %get-tuple-element.12.own.refs_0_, f32[512,1024]{1,0:T(8,128)S(1)} %get-tuple-element.13.acc_in, ...), custom_call_target="tpu_custom_call" | custom-call | flops 1073741824 | bytes 8388608 | tf_op jit(solution)/shard_map/pallas_call | solution.py:266
  112.6 2.6 %collective-permute-start.15 = (bf16[512,512]{1,0:T(8,128)(2,1)S(1)}, bf16[512,512]{1,0:T(8,128)(2,1)S(1)}, u32[]{:S(2)}, u32[]{:S(2)}) collective-permute-start(bf16[512,512]{1,0:T(8,128)(2,1)S(1)} %get-tuple-element.17), channel_id=1, source_target_pairs={{8,0},{12,4},{1,9},{5,13},{26,18},{30,22},{19,27},{23,31}} | collective-permute-start | bytes 1572872 | tf_op jit(solution)/shard_map/ppermute | solution.py:307
  117.9 2.3 %collective-permute-done.10.refs_0_ = s32[4,8]{1,0:T(4,128)S(1)} collective-permute-done((s32[4,8]{1,0:T(4,128)S(1)}, s32[4,8]{1,0:T(4,128)S(1)}, u32[]{:S(2)}, u32[]{:S(2)}) %collective-permute-start.10) | collective-permute-done | bytes 160 | tf_op jit(solution)/shard_map/ppermute | solution.py:335
  121.3 16.4 %collective-permute-done.25.right = f32[8,128]{1,0:T(8,128)S(1)} collective-permute-done((f32[8,128]{1,0:T(8,128)S(1)}, f32[8,128]{1,0:T(8,128)S(1)}, u32[]{:S(2)}, u32[]{:S(2)}) %collective-permute-start.25) | collective-permute-done | bytes 4128 | tf_op jit(solution)/shard_map/ppermute | solution.py:278
  137.7 3.3 %collective-permute-done.11.refs_1_ = s32[4,8]{1,0:T(4,128)S(1)} collective-permute-done((s32[4,8]{1,0:T(4,128)S(1)}, s32[4,8]{1,0:T(4,128)S(1)}, u32[]{:S(2)}, u32[]{:S(2)}) %collective-permute-start.11) | collective-permute-done | bytes 160 | tf_op jit(solution)/shard_map/ppermute | solution.py:335
  141.0 2.4 %collective-permute-done.26.right = f32[8,128]{1,0:T(8,128)S(1)} collective-permute-done((f32[8,128]{1,0:T(8,128)S(1)}, f32[8,128]{1,0:T(8,128)S(1)}, u32[]{:S(2)}, u32[]{:S(2)}) %collective-permute-start.26) | collective-permute-done | bytes 4128 | tf_op jit(solution)/shard_map/ppermute | solution.py:278
  143.5 2.8 %collective-permute-start.12 = (s32[4,8]{1,0:T(4,128)S(1)}, s32[4,8]{1,0:T(4,128)S(1)}, u32[]{:S(2)}, u32[]{:S(2)}) collective-permute-start(s32[4,8]{1,0:T(4,128)S(1)} %copy-done.2), channel_id=1, source_target_pairs={{0,3},{1,2},{2,1},{3,0},{4,7},{5,6},{6,5},{7,4},{8,11},{9,10},{10,... | collective-permute-start | bytes 392 | tf_op jit(solution)/shard_map/ppermute | solution.py:335
  150.8 2.2 %collective-permute-start.29 = (f32[8,128]{1,0:T(8,128)S(1)}, f32[8,128]{1,0:T(8,128)S(1)}, u32[]{:S(2)}, u32[]{:S(2)}) collective-permute-start(f32[8,128]{1,0:T(8,128)S(1)} %shard_map.51.own), channel_id=1, source_target_pairs={{0,3},{1,2},{2,1},{3,0},{4,7},{5,6},{6,5},{7,4},{8,11},{9,10},{10,... | collective-permute-start | bytes 12296 | tf_op jit(solution)/shard_map/ppermute | solution.py:421
  156.4 3.8 %collective-permute-start.17 = (bf16[512,1024]{1,0:T(8,128)(2,1)S(1)}, bf16[512,1024]{1,0:T(8,128)(2,1)S(1)}, u32[]{:S(2)}, u32[]{:S(2)}) collective-permute-start(bf16[512,1024]{1,0:T(8,128)(2,1)S(1)} %get-tuple-element.15.squared), channel_id=1, source_target_pairs={{1,2},{2,3},{3,1},{5,6},{6,7},{7,5},{8,10},{10,11},{11,8},{12,14},... | collective-permute-start | bytes 3145736 | tf_op jit(solution)/shard_map/ppermute | solution.py:297
  160.2 3.3 %collective-permute-start.18 = (bf16[512,1024]{1,0:T(8,128)(2,1)S(1)}, bf16[512,1024]{1,0:T(8,128)(2,1)S(1)}, u32[]{:S(2)}, u32[]{:S(2)}) collective-permute-start(bf16[512,1024]{1,0:T(8,128)(2,1)S(1)} %get-tuple-element.15.squared), channel_id=1, source_target_pairs={{1,3},{2,1},{3,2},{5,7},{6,5},{7,6},{8,11},{10,8},{11,10},{12,15},... | collective-permute-start | bytes 3145736 | tf_op jit(solution)/shard_map/ppermute | solution.py:297
  165.7 8.5 %collective-permute-start.23 = (bf16[512,512]{1,0:T(8,128)(2,1)S(1)}, bf16[512,512]{1,0:T(8,128)(2,1)S(1)}, u32[]{:S(2)}, u32[]{:S(2)}) collective-permute-start(bf16[512,512]{1,0:T(8,128)(2,1)S(1)} %collective-permute-done.22), channel_id=1, source_target_pairs={{8,4},{12,0},{1,13},{5,9},{26,22},{30,18},{19,31},{23,27}} | collective-permute-start | bytes 1572872 | tf_op jit(solution)/shard_map/ppermute | solution.py:307
  174.3 5.2 %shard_map.44.local_square = bf16[512,1024]{1,0:T(8,128)(2,1)S(1)} custom-call(s32[2]{0:T(128)S(1)} %pad_add_fusion.where, s32[4,8]{1,0:T(4,128)S(1)} %copy-done.2, s32[4,8]{1,0:T(4,128)S(1)} %collective-permute-done.10.refs_0_, s32[4,8]{1,0:T(4,128)S(1)} %collective-permute-done.11.refs_1_, s32[4,8]{1,0:T(4,128)S(1)} %collective-permute-done.12.refs_2_, ...), custom_call_target="tpu_custom_call" | custom-call | flops 4294967296 | bytes 9437184 | tf_op jit(solution)/shard_map/pallas_call | solution.py:266
  179.5 3.1 %shard_map.45.acc_in = f32[512,1024]{1,0:T(8,128)S(1)} custom-call(s32[2]{0:T(128)S(1)} %pad_add_fusion.where, bf16[512,1024]{1,0:T(8,128)(2,1)S(1)} %get-tuple-element.15.squared, bf16[512,1024]{1,0:T(8,128)(2,1)S(1)} %shard_map.44.local_square, bf16[8,512,1024]{2,1,0:T(8,128)(2,1)S(1)} %get-tuple-element.14.right.right_all), custom_call_target="tpu_custom_call" | custom-call | flops 2147483648 | bytes 8388608 | tf_op jit(solution)/shard_map/pallas_call | solution.py:266
  183.4 2.5 %collective-permute-done.23.refs_3_ = bf16[512,512]{1,0:T(8,128)(2,1)S(1)} collective-permute-done((bf16[512,512]{1,0:T(8,128)(2,1)S(1)}, bf16[512,512]{1,0:T(8,128)(2,1)S(1)}, u32[]{:S(2)}, u32[]{:S(2)}) %collective-permute-start.23) | collective-permute-done | bytes 524320 | tf_op jit(solution)/shard_map/ppermute | solution.py:307
  185.9 21.8 %collective-permute-done.18.turn2 = bf16[512,1024]{1,0:T(8,128)(2,1)S(1)} collective-permute-done((bf16[512,1024]{1,0:T(8,128)(2,1)S(1)}, bf16[512,1024]{1,0:T(8,128)(2,1)S(1)}, u32[]{:S(2)}, u32[]{:S(2)}) %collective-permute-start.18) | collective-permute-done | bytes 1048608 | tf_op jit(solution)/shard_map/ppermute | solution.py:297
  207.6 4.3 %shard_map.48 = f32[512,1024]{1,0:T(8,128)} custom-call(s32[2]{0:T(128)S(1)} %pad_add_fusion.where, f32[8,1024]{1,0:T(8,128)S(1)} %get-tuple-element.11.kept_ref, bf16[512,1024]{1,0:T(8,128)(2,1)S(1)} %get-tuple-element.15.squared, f32[512,1024]{1,0:T(8,128)S(1)} %shard_map.47.acc, bf16[512,1024]{1,0:T(8,128)(2,1)S(1)} %collective-permute-done.17.turn1, ...), custom_call_target="tpu_custom_call" | custom-call | flops 2147483648 | bytes 16777216 | tf_op jit(solution)/shard_map/pallas_call | solution.py:266
  (55 shorter events, 28.0 us)
Async XLA Ops:
  3.4 24.2 %collective-permute-start.3 = (bf16[512,1024]{1,0:T(8,128)(2,1)S(1)}, bf16[512,1024]{1,0:T(8,128)(2,1)S(1)}, u32[]{:S(2)}, u32[]{:S(2)}) collective-permute-start(bf16[512,1024]{1,0:T(8,128)(2,1)S(1)} %get-tuple-element.12.own.refs_0_), channel_id=1, source_target_pairs={{0,8},{4,12},{8,0},{12,4},{16,24},{20,28},{24,16},{28,20},{1,9},{5... | collective-permute-start | bytes 3145736 | tf_op jit(solution)/shard_map/ppermute | solution.py:278
  3.5 30.7 %collective-permute-start = (bf16[512,1024]{1,0:T(8,128)(2,1)S(1)}, bf16[512,1024]{1,0:T(8,128)(2,1)S(1)}, u32[]{:S(2)}, u32[]{:S(2)}) collective-permute-start(bf16[512,1024]{1,0:T(8,128)(2,1)S(1)} %get-tuple-element.12.own.refs_0_), channel_id=1, source_target_pairs={{0,1},{1,0},{2,3},{3,2},{4,5},{5,4},{6,7},{7,6},{8,9},{9,8},{10,11... | collective-permute-start | bytes 3145736 | tf_op jit(solution)/shard_map/ppermute | solution.py:333
  5.0 29.2 %collective-permute-start.5 = (bf16[512,1024]{1,0:T(8,128)(2,1)S(1)}, bf16[512,1024]{1,0:T(8,128)(2,1)}, u32[]{:S(2)}, u32[]{:S(2)}) collective-permute-start(bf16[512,1024]{1,0:T(8,128)(2,1)S(1)} %get-tuple-element.12.own.refs_0_), channel_id=1, source_target_pairs={{0,16},{4,20},{8,24},{12,28},{16,0},{20,4},{24,8},{28,12},{1,17},{... | collective-permute-start | bytes 3145736 | tf_op jit(solution)/shard_map/ppermute | solution.py:278
  27.6 23.4 %collective-permute-start.7 = (bf16[512,1024]{1,0:T(8,128)(2,1)S(1)}, bf16[512,1024]{1,0:T(8,128)(2,1)}, u32[]{:S(2)}, u32[]{:S(2)}) collective-permute-start(bf16[512,1024]{1,0:T(8,128)(2,1)S(1)} %collective-permute-done.3.refs_2_), channel_id=1, source_target_pairs={{0,16},{4,20},{8,24},{12,28},{16,0},{20,4},{24,8},{28,12},{1,17},{... | collective-permute-start | bytes 3145736 | tf_op jit(solution)/shard_map/ppermute | solution.py:278
  28.8 25.1 %collective-permute-start.1 = (bf16[512,1024]{1,0:T(8,128)(2,1)S(1)}, bf16[512,1024]{1,0:T(8,128)(2,1)}, u32[]{:S(2)}, u32[]{:S(2)}) collective-permute-start(bf16[512,1024]{1,0:T(8,128)(2,1)S(1)} %get-tuple-element.12.own.refs_0_), channel_id=1, source_target_pairs={{0,3},{1,2},{2,1},{3,0},{4,7},{5,6},{6,5},{7,4},{8,11},{9,10},{10,... | collective-permute-start | bytes 3145736 | tf_op jit(solution)/shard_map/ppermute | solution.py:332
  32.1 21.8 %collective-permute-start.2 = (bf16[512,1024]{1,0:T(8,128)(2,1)S(1)}, bf16[512,1024]{1,0:T(8,128)(2,1)}, u32[]{:S(2)}, u32[]{:S(2)}) collective-permute-start(bf16[512,1024]{1,0:T(8,128)(2,1)S(1)} %get-tuple-element.12.own.refs_0_), channel_id=1, source_target_pairs={{0,4},{4,0},{8,12},{12,8},{16,20},{20,16},{24,28},{28,24},{1,5},{5... | collective-permute-start | bytes 3145736 | tf_op jit(solution)/shard_map/ppermute | solution.py:278
  34.1 19.8 %collective-permute-start.4 = (bf16[512,1024]{1,0:T(8,128)(2,1)S(1)}, bf16[512,1024]{1,0:T(8,128)(2,1)}, u32[]{:S(2)}, u32[]{:S(2)}) collective-permute-start(bf16[512,1024]{1,0:T(8,128)(2,1)S(1)} %collective-permute-done.3.refs_2_), channel_id=1, source_target_pairs={{0,4},{4,0},{8,12},{12,8},{16,20},{20,16},{24,28},{28,24},{1,5},{5... | collective-permute-start | bytes 3145736 | tf_op jit(solution)/shard_map/ppermute | solution.py:278
  34.1 19.8 %collective-permute-start.6 = (bf16[512,1024]{1,0:T(8,128)(2,1)}, bf16[512,1024]{1,0:T(8,128)(2,1)}, u32[]{:S(2)}, u32[]{:S(2)}) collective-permute-start(bf16[512,1024]{1,0:T(8,128)(2,1)} %collective-permute-done.5.refs_4_), channel_id=1, source_target_pairs={{0,4},{4,0},{8,12},{12,8},{16,20},{20,16},{24,28},{28,24},{1,5},{5... | collective-permute-start | bytes 3145736 | tf_op jit(solution)/shard_map/ppermute | solution.py:278
  51.0 4.9 %collective-permute-start.8 = (bf16[512,1024]{1,0:T(8,128)(2,1)}, bf16[512,1024]{1,0:T(8,128)(2,1)}, u32[]{:S(2)}, u32[]{:S(2)}) collective-permute-start(bf16[512,1024]{1,0:T(8,128)(2,1)} %collective-permute-done.7.refs_6_), channel_id=1, source_target_pairs={{0,4},{4,0},{8,12},{12,8},{16,20},{20,16},{24,28},{28,24},{1,5},{5... | collective-permute-start | bytes 3145736 | tf_op jit(solution)/shard_map/ppermute | solution.py:278
  62.1 103.6 %collective-permute-start.13 = (bf16[3,512,1024]{2,1,0:T(8,128)(2,1)S(1)}, bf16[3,512,1024]{2,1,0:T(8,128)(2,1)S(1)}, u32[]{:S(2)}, u32[]{:S(2)}) collective-permute-start(bf16[3,512,1024]{2,1,0:T(8,128)(2,1)S(1)} %get-tuple-element.16.refs_3_), channel_id=1, source_target_pairs={{0,4},{4,0},{8,12},{12,8},{16,20},{20,16},{24,28},{28,24},{1,5},{5... | collective-permute-start | bytes 9437192 | tf_op jit(solution)/shard_map/ppermute | solution.py:278
  62.8 45.1 %collective-permute-start.9 = (bf16[512,1024]{1,0:T(8,128)(2,1)}, bf16[512,1024]{1,0:T(8,128)(2,1)S(1)}, u32[]{:S(2)}, u32[]{:S(2)}) collective-permute-start(bf16[512,1024]{1,0:T(8,128)(2,1)} %collective-permute-done.1.cross), channel_id=1, source_target_pairs={{0,1},{1,0},{2,3},{3,2},{4,5},{5,4},{6,7},{7,6},{8,9},{9,8},{10,11... | collective-permute-start | bytes 3145736 | tf_op jit(solution)/shard_map/ppermute | solution.py:334
  107.9 41.0 %collective-permute-start.14 = (bf16[512,1024]{1,0:T(8,128)(2,1)S(1)}, bf16[512,1024]{1,0:T(8,128)(2,1)S(1)}, u32[]{:S(2)}, u32[]{:S(2)}) collective-permute-start(bf16[512,1024]{1,0:T(8,128)(2,1)S(1)} %collective-permute-done.9.far.refs_5_), channel_id=1, source_target_pairs={{0,4},{4,0},{8,12},{12,8},{16,20},{20,16},{24,28},{28,24},{1,5},{5... | collective-permute-start | bytes 3145736 | tf_op jit(solution)/shard_map/ppermute | solution.py:278
  112.6 43.8 %collective-permute-start.15 = (bf16[512,512]{1,0:T(8,128)(2,1)S(1)}, bf16[512,512]{1,0:T(8,128)(2,1)S(1)}, u32[]{:S(2)}, u32[]{:S(2)}) collective-permute-start(bf16[512,512]{1,0:T(8,128)(2,1)S(1)} %get-tuple-element.17), channel_id=1, source_target_pairs={{8,0},{12,4},{1,9},{5,13},{26,18},{30,22},{19,27},{23,31}} | collective-permute-start | bytes 1572872 | tf_op jit(solution)/shard_map/ppermute | solution.py:307
  115.2 45.1 %collective-permute-start.16 = (bf16[512,512]{1,0:T(8,128)(2,1)S(1)}, bf16[512,512]{1,0:T(8,128)(2,1)S(1)}, u32[]{:S(2)}, u32[]{:S(2)}) collective-permute-start(bf16[512,512]{1,0:T(8,128)(2,1)S(1)} %get-tuple-element.18), channel_id=1, source_target_pairs={{8,4},{12,0},{1,13},{5,9},{26,22},{30,18},{19,31},{23,27}} | collective-permute-start | bytes 1572872 | tf_op jit(solution)/shard_map/ppermute | solution.py:307
  120.2 17.5 %collective-permute-start.25 = (f32[8,128]{1,0:T(8,128)S(1)}, f32[8,128]{1,0:T(8,128)S(1)}, u32[]{:S(2)}, u32[]{:S(2)}) collective-permute-start(f32[8,128]{1,0:T(8,128)S(1)} %shard_map.49.left), channel_id=1, source_target_pairs={{0,8},{4,12},{8,0},{12,4},{16,24},{20,28},{24,16},{28,20},{1,9},{5... | collective-permute-start | bytes 12296 | tf_op jit(solution)/shard_map/ppermute | solution.py:278
  143.5 4.2 %collective-permute-start.12 = (s32[4,8]{1,0:T(4,128)S(1)}, s32[4,8]{1,0:T(4,128)S(1)}, u32[]{:S(2)}, u32[]{:S(2)}) collective-permute-start(s32[4,8]{1,0:T(4,128)S(1)} %copy-done.2), channel_id=1, source_target_pairs={{0,3},{1,2},{2,1},{3,0},{4,7},{5,6},{6,5},{7,4},{8,11},{9,10},{10,... | collective-permute-start | bytes 392 | tf_op jit(solution)/shard_map/ppermute | solution.py:335
  150.8 4.3 %collective-permute-start.29 = (f32[8,128]{1,0:T(8,128)S(1)}, f32[8,128]{1,0:T(8,128)S(1)}, u32[]{:S(2)}, u32[]{:S(2)}) collective-permute-start(f32[8,128]{1,0:T(8,128)S(1)} %shard_map.51.own), channel_id=1, source_target_pairs={{0,3},{1,2},{2,1},{3,0},{4,7},{5,6},{6,5},{7,4},{8,11},{9,10},{10,... | collective-permute-start | bytes 12296 | tf_op jit(solution)/shard_map/ppermute | solution.py:421
  153.0 11.1 %collective-permute-start.19 = (bf16[512,512]{1,0:T(8,128)(2,1)S(1)}, bf16[512,512]{1,0:T(8,128)(2,1)S(1)}, u32[]{:S(2)}, u32[]{:S(2)}) collective-permute-start(bf16[512,512]{1,0:T(8,128)(2,1)S(1)} %get-tuple-element.17), channel_id=1, source_target_pairs={{16,0},{20,4},{25,9},{29,13},{2,18},{6,22},{11,27},{15,31}} | collective-permute-start | bytes 1572872 | tf_op jit(solution)/shard_map/ppermute | solution.py:307
  155.1 9.9 %collective-permute-start.22 = (bf16[512,512]{1,0:T(8,128)(2,1)S(1)}, bf16[512,512]{1,0:T(8,128)(2,1)S(1)}, u32[]{:S(2)}, u32[]{:S(2)}) collective-permute-start(bf16[512,512]{1,0:T(8,128)(2,1)S(1)} %get-tuple-element.18), channel_id=1, source_target_pairs={{24,8},{28,12},{17,1},{21,5},{10,26},{14,30},{3,19},{7,23}} | collective-permute-start | bytes 1572872 | tf_op jit(solution)/shard_map/ppermute | solution.py:307
  156.4 29.5 %collective-permute-start.17 = (bf16[512,1024]{1,0:T(8,128)(2,1)S(1)}, bf16[512,1024]{1,0:T(8,128)(2,1)S(1)}, u32[]{:S(2)}, u32[]{:S(2)}) collective-permute-start(bf16[512,1024]{1,0:T(8,128)(2,1)S(1)} %get-tuple-element.15.squared), channel_id=1, source_target_pairs={{1,2},{2,3},{3,1},{5,6},{6,7},{7,5},{8,10},{10,11},{11,8},{12,14},... | collective-permute-start | bytes 3145736 | tf_op jit(solution)/shard_map/ppermute | solution.py:297
  160.2 47.4 %collective-permute-start.18 = (bf16[512,1024]{1,0:T(8,128)(2,1)S(1)}, bf16[512,1024]{1,0:T(8,128)(2,1)S(1)}, u32[]{:S(2)}, u32[]{:S(2)}) collective-permute-start(bf16[512,1024]{1,0:T(8,128)(2,1)S(1)} %get-tuple-element.15.squared), channel_id=1, source_target_pairs={{1,3},{2,1},{3,2},{5,7},{6,5},{7,6},{8,11},{10,8},{11,10},{12,15},... | collective-permute-start | bytes 3145736 | tf_op jit(solution)/shard_map/ppermute | solution.py:297
  164.1 19.3 %collective-permute-start.20 = (bf16[512,512]{1,0:T(8,128)(2,1)S(1)}, bf16[512,512]{1,0:T(8,128)(2,1)S(1)}, u32[]{:S(2)}, u32[]{:S(2)}) collective-permute-start(bf16[512,512]{1,0:T(8,128)(2,1)S(1)} %get-tuple-element.18), channel_id=1, source_target_pairs={{16,4},{20,0},{25,13},{29,9},{2,22},{6,18},{11,31},{15,27}} | collective-permute-start | bytes 1572872 | tf_op jit(solution)/shard_map/ppermute | solution.py:307
  165.0 18.4 %collective-permute-start.21 = (bf16[512,512]{1,0:T(8,128)(2,1)S(1)}, bf16[512,512]{1,0:T(8,128)(2,1)S(1)}, u32[]{:S(2)}, u32[]{:S(2)}) collective-permute-start(bf16[512,512]{1,0:T(8,128)(2,1)S(1)} %get-tuple-element.17), channel_id=1, source_target_pairs={{24,0},{28,4},{17,9},{21,13},{10,18},{14,22},{3,27},{7,31}} | collective-permute-start | bytes 1572872 | tf_op jit(solution)/shard_map/ppermute | solution.py:307
  165.7 20.2 %collective-permute-start.23 = (bf16[512,512]{1,0:T(8,128)(2,1)S(1)}, bf16[512,512]{1,0:T(8,128)(2,1)S(1)}, u32[]{:S(2)}, u32[]{:S(2)}) collective-permute-start(bf16[512,512]{1,0:T(8,128)(2,1)S(1)} %collective-permute-done.22), channel_id=1, source_target_pairs={{8,4},{12,0},{1,13},{5,9},{26,22},{30,18},{19,31},{23,27}} | collective-permute-start | bytes 1572872 | tf_op jit(solution)/shard_map/ppermute | solution.py:307
  (9 other events, 27.8 us)

commit v9 on v8

--- a/solution.py
+++ b/solution.py
@@ -213,8 +213,9 @@
     )
 
 
-def cubic_middle_kernel(where, acc_in, right_all, same, cross, acc):
-    row, col = where[0], where[1]
+def cubic_middle_kernel(where, acc_in, turn, right_all, same, cross, acc):
+    row, col = where[0], where[1]
+    source = late_sources(row, col)[0]
 
     @pl.when(row // 2 == col)
     def _():
@@ -222,38 +223,43 @@
 
     @pl.when(row // 2 != col)
     def _():
+        acc[...] = acc_in[...] + piece(turn, right_all.at[pl.ds(2 * source, 2)])
+
+
+def cubic_corner_kernel(where, acc_in, right_all, *refs):
+    sides, acc, scratch = refs[:4], refs[4], refs[5]
+    row, col = where[0], where[1]
+    core = row % 2
+
+    @pl.when(row // 2 == col)
+    def _():
+        scratch[...] = acc_in[...] + side_piece(sides[2:], right_all, col ^ 3, core)
+        acc[...] = scratch[...] + side_piece(sides[:2], right_all, col ^ 2, core)
+
+    @pl.when(row // 2 != col)
+    def _():
         acc[...] = acc_in[...]
 
 
-def cubic_late_kernel(where, kept_ref, squared, acc, turn1, turn2, right_all, *refs):
-    sides, purified_ref, scratch = refs[:4], refs[4], refs[5]
-    row, col = where[0], where[1]
-    core, chip = row % 2, row // 2
+def cubic_late_kernel(where, kept_ref, squared, acc, turn, right_all, purified_ref):
+    row, col = where[0], where[1]
     rows, _ = squared.shape
-    sources = late_sources(row, col)
-
-    def finish(first, second):
-        scratch[...] = acc[...] + first
-        total = scratch[...] + second()
+    source = late_sources(row, col)[1]
+
+    def finish(total):
         kept = kept_ref[...]
         for a in range(rows // B):
             part = slice(a * B, (a + 1) * B)
             wide = squared[part, :].astype(jnp.float32)
             purified_ref[part, :] = 3.0 * wide - 2.0 * (total[part] * kept[a : a + 1])
 
-    @pl.when(chip != col)
-    def _():
-        finish(
-            piece(turn1, right_all.at[pl.ds(2 * sources[0], 2)]),
-            lambda: piece(turn2, right_all.at[pl.ds(2 * sources[1], 2)]),
-        )
-
-    @pl.when(chip == col)
-    def _():
-        finish(
-            side_piece(sides[:2], right_all, col ^ 2, core),
-            lambda: side_piece(sides[2:], right_all, col ^ 3, core),
-        )
+    @pl.when(row // 2 != col)
+    def _():
+        finish(acc[...] + piece(turn, right_all.at[pl.ds(2 * source, 2)]))
+
+    @pl.when(row // 2 == col)
+    def _():
+        finish(acc)
 
 
 ANYWHERE = pl.BlockSpec(memory_space=pl.ANY)
@@ -411,8 +417,8 @@
     )
     cubic = call(
         cubic_middle_kernel,
-        [SCALARS] + [WHOLE] * 4,
-        (where, cubic, right, *sides[:2]),
+        [SCALARS] + [WHOLE] * 5,
+        (where, cubic, turns[0], right, *sides[:2]),
         wide,
         [],
         flops,
@@ -430,14 +436,23 @@
         1,
         SCALARS,
     )
-    purified = call(
-        cubic_late_kernel,
-        [SCALARS] + [WHOLE] * 10,
-        (where, kept, squared, cubic, *turns, right, *sides[2:]),
+    cubic = call(
+        cubic_corner_kernel,
+        [SCALARS] + [WHOLE] * 6,
+        (where, cubic, right, *sides[2:]),
         wide,
         [pltpu.VMEM((rows, columns), jnp.float32)],
         2 * flops,
-        16 * size,
+        12 * size,
+    )
+    purified = call(
+        cubic_late_kernel,
+        [SCALARS] + [WHOLE] * 5,
+        (where, kept, squared, cubic, turns[1], right),
+        wide,
+        [],
+        flops,
+        12 * size,
     )
     return (purified, occupation.reshape(()))
 

time: 212 us -> 222 us (1.047)
  the two profiles are of different devices: /device:TPU:3 before, /device:TPU:0 now
where the time goes in v9:
time: 222 us
  waiting for transfers between devices  116 us (52%)
  starting transfers between devices  77.2 us (35%)
  Pallas kernels  25.4 us (11%)
    ppermute x12, waiting for transfers between devices, swap(): return lax.ppermute(x, 'row', [(i, i ^ k) for i in range(8)])  45.9 us
    ppermute x7, waiting for transfers between devices, in_plane(): return lax.ppermute(x, ('row', 'col'), pairs)  34 us
    ppermute x12, starting transfers between devices, swap(): return lax.ppermute(x, 'row', [(i, i ^ k) for i in range(8)])  26.6 us
    pallas_call x13, Pallas kernels, call(): pl.pallas_call(kernel, out_shape=outs, in_specs=specs, out_specs=jax.tree...  25.4 us
    ppermute x1, waiting for transfers between devices, local(): far = lax.ppermute(cross, 'col', [(i, i ^ 1) for i in range(4)])  24 us
    ppermute x1, starting transfers between devices, local(): far = lax.ppermute(cross, 'col', [(i, i ^ 1) for i in range(4)])  21.8 us
    ppermute x3, starting transfers between devices, local(): lax.ppermute(pattern, 'col', [(i, i ^ k) for i in range(4)])  8.82 us
    ppermute x7, starting transfers between devices, in_plane(): return lax.ppermute(x, ('row', 'col'), pairs)  8.41 us
  transfers between devices with their start and end apart: 30, of which 16 were waited for; matrix products, arithmetic and copies ran while one was open for 0% of the time, Pallas kernels for 7%

profile of v9, /device:TPU:0, one launch (start us, length us, event | category | flops | bytes accessed | tf_op | source)
XLA Modules:
  0.0 221.9 jit_solution(12398945707957920398)
XLA Ops:
  3.4 3.0 %collective-permute-start.3 = (bf16[512,1024]{1,0:T(8,128)(2,1)S(1)}, bf16[512,1024]{1,0:T(8,128)(2,1)S(1)}, u32[]{:S(2)}, u32[]{:S(2)}) collective-permute-start(bf16[512,1024]{1,0:T(8,128)(2,1)S(1)} %get-tuple-element.12.own.refs_0_), channel_id=1, source_target_pairs={{0,8},{4,12},{8,0},{12,4},{16,24},{20,28},{24,16},{28,20},{1,9},{5... | collective-permute-start | bytes 3145736 | tf_op jit(solution)/shard_map/ppermute | solution.py:284
  9.5 20.1 %collective-permute-done.3.refs_2_ = bf16[512,1024]{1,0:T(8,128)(2,1)S(1)} collective-permute-done((bf16[512,1024]{1,0:T(8,128)(2,1)S(1)}, bf16[512,1024]{1,0:T(8,128)(2,1)S(1)}, u32[]{:S(2)}, u32[]{:S(2)}) %collective-permute-start.3) | collective-permute-done | bytes 1048608 | tf_op jit(solution)/shard_map/ppermute | solution.py:284
  31.3 3.6 %collective-permute-start.1 = (bf16[512,1024]{1,0:T(8,128)(2,1)S(1)}, bf16[512,1024]{1,0:T(8,128)(2,1)}, u32[]{:S(2)}, u32[]{:S(2)}) collective-permute-start(bf16[512,1024]{1,0:T(8,128)(2,1)S(1)} %get-tuple-element.12.own.refs_0_), channel_id=1, source_target_pairs={{0,3},{1,2},{2,1},{3,0},{4,7},{5,6},{6,5},{7,4},{8,11},{9,10},{10,... | collective-permute-start | bytes 3145736 | tf_op jit(solution)/shard_map/ppermute | solution.py:338
  35.5 19.4 %collective-permute-done.7.refs_6_ = bf16[512,1024]{1,0:T(8,128)(2,1)} collective-permute-done((bf16[512,1024]{1,0:T(8,128)(2,1)S(1)}, bf16[512,1024]{1,0:T(8,128)(2,1)}, u32[]{:S(2)}, u32[]{:S(2)}) %collective-permute-start.7) | collective-permute-done | bytes 1048608 | tf_op jit(solution)/shard_map/ppermute | solution.py:284
  55.0 2.3 %collective-permute-done.1.cross = bf16[512,1024]{1,0:T(8,128)(2,1)} collective-permute-done((bf16[512,1024]{1,0:T(8,128)(2,1)S(1)}, bf16[512,1024]{1,0:T(8,128)(2,1)}, u32[]{:S(2)}, u32[]{:S(2)}) %collective-permute-start.1) | collective-permute-done | bytes 1048608 | tf_op jit(solution)/shard_map/ppermute | solution.py:338
  57.9 5.9 %shard_map.42 = (f32[512,1024]{1,0:T(8,128)S(1)}, bf16[3,512,1024]{2,1,0:T(8,128)(2,1)S(1)}, bf16[8,512,1024]{2,1,0:T(8,128)(2,1)S(1)}) custom-call(s32[2]{0:T(128)S(1)} %pad_add_fusion.where, bf16[512,1024]{1,0:T(8,128)(2,1)S(1)} %get-tuple-element.12.own.refs_0_, bf16[512,1024]{1,0:T(8,128)(2,1)S(1)} %collective-permute-done.pair, ...), custom_call_target="tpu_custom_call" | custom-call | flops 3221225472 | bytes 25165824 | tf_op jit(solution)/shard_map/pallas_call | solution.py:272
  64.0 21.8 %collective-permute-start.9 = (bf16[512,1024]{1,0:T(8,128)(2,1)}, bf16[512,1024]{1,0:T(8,128)(2,1)S(1)}, u32[]{:S(2)}, u32[]{:S(2)}) collective-permute-start(bf16[512,1024]{1,0:T(8,128)(2,1)} %collective-permute-done.1.cross), channel_id=1, source_target_pairs={{0,1},{1,0},{2,3},{3,2},{4,5},{5,4},{6,7},{7,6},{8,9},{9,8},{10,11... | collective-permute-start | bytes 3145736 | tf_op jit(solution)/shard_map/ppermute | solution.py:340
  85.7 24.0 %collective-permute-done.9.far.refs_5_ = bf16[512,1024]{1,0:T(8,128)(2,1)S(1)} collective-permute-done((bf16[512,1024]{1,0:T(8,128)(2,1)}, bf16[512,1024]{1,0:T(8,128)(2,1)S(1)}, u32[]{:S(2)}, u32[]{:S(2)}) %collective-permute-start.9) | collective-permute-done | bytes 1048608 | tf_op jit(solution)/shard_map/ppermute | solution.py:340
  109.7 2.2 %shard_map.43 = (bf16[512,1024]{1,0:T(8,128)(2,1)S(1)}, f32[8,128]{1,0:T(8,128)S(1)}) custom-call(s32[2]{0:T(128)S(1)} %pad_add_fusion.where, f32[8,1024]{1,0:T(8,128)S(1)} %get-tuple-element.11.kept_ref, bf16[512,1024]{1,0:T(8,128)(2,1)S(1)} %get-tuple-element.12.own.refs_0_, f32[512,1024]{1,0:T(8,128)S(1)} %get-tuple-element.13.acc_in, ...), custom_call_target="tpu_custom_call" | custom-call | flops 1073741824 | bytes 8388608 | tf_op jit(solution)/shard_map/pallas_call | solution.py:272
  117.2 5.0 %collective-permute-start.10 = (s32[4,8]{1,0:T(4,128)S(1)}, s32[4,8]{1,0:T(4,128)S(1)}, u32[]{:S(2)}, u32[]{:S(2)}) collective-permute-start(s32[4,8]{1,0:T(4,128)S(1)} %copy-done.2), channel_id=1, source_target_pairs={{0,1},{1,0},{2,3},{3,2},{4,5},{5,4},{6,7},{7,6},{8,9},{9,8},{10,11... | collective-permute-start | bytes 392 | tf_op jit(solution)/shard_map/ppermute | solution.py:341
  123.7 18.7 %collective-permute-start.25 = (f32[8,128]{1,0:T(8,128)S(1)}, f32[8,128]{1,0:T(8,128)S(1)}, u32[]{:S(2)}, u32[]{:S(2)}) collective-permute-start(f32[8,128]{1,0:T(8,128)S(1)} %shard_map.50.left), channel_id=1, source_target_pairs={{0,8},{4,12},{8,0},{12,4},{16,24},{20,28},{24,16},{28,20},{1,9},{5... | collective-permute-start | bytes 12296 | tf_op jit(solution)/shard_map/ppermute | solution.py:284
  145.7 2.8 %collective-permute-done.11.refs_1_ = s32[4,8]{1,0:T(4,128)S(1)} collective-permute-done((s32[4,8]{1,0:T(4,128)S(1)}, s32[4,8]{1,0:T(4,128)S(1)}, u32[]{:S(2)}, u32[]{:S(2)}) %collective-permute-start.11) | collective-permute-done | bytes 160 | tf_op jit(solution)/shard_map/ppermute | solution.py:341
  148.7 3.4 %collective-permute-done.26.right = f32[8,128]{1,0:T(8,128)S(1)} collective-permute-done((f32[8,128]{1,0:T(8,128)S(1)}, f32[8,128]{1,0:T(8,128)S(1)}, u32[]{:S(2)}, u32[]{:S(2)}) %collective-permute-start.26) | collective-permute-done | bytes 4128 | tf_op jit(solution)/shard_map/ppermute | solution.py:284
  152.1 2.2 collective-permute-start.12
  154.3 3.2 %collective-permute-done.12.refs_2_ = s32[4,8]{1,0:T(4,128)S(1)} collective-permute-done((s32[4,8]{1,0:T(4,128)S(1)}, s32[4,8]{1,0:T(4,128)S(1)}, u32[]{:S(2)}, u32[]{:S(2)}) %collective-permute-start.12) | collective-permute-done | bytes 160 | tf_op jit(solution)/shard_map/ppermute | solution.py:341
  158.2 2.1 collective-permute-start.28
  161.1 2.2 collective-permute-start.29
  168.5 10.9 %collective-permute-done.17.cross = bf16[512,512]{1,0:T(8,128)(2,1)S(1)} collective-permute-done((bf16[512,512]{1,0:T(8,128)(2,1)S(1)}, bf16[512,512]{1,0:T(8,128)(2,1)S(1)}, u32[]{:S(2)}, u32[]{:S(2)}) %collective-permute-start.17) | collective-permute-done | bytes 524320 | tf_op jit(solution)/shard_map/ppermute | solution.py:313
  184.6 5.2 %shard_map.44.local_square = bf16[512,1024]{1,0:T(8,128)(2,1)S(1)} custom-call(s32[2]{0:T(128)S(1)} %pad_add_fusion.where, s32[4,8]{1,0:T(4,128)S(1)} %copy-done.2, s32[4,8]{1,0:T(4,128)S(1)} %collective-permute-done.10.refs_0_, s32[4,8]{1,0:T(4,128)S(1)} %collective-permute-done.11.refs_1_, s32[4,8]{1,0:T(4,128)S(1)} %collective-permute-done.12.refs_2_, ...), custom_call_target="tpu_custom_call" | custom-call | flops 4294967296 | bytes 9437184 | tf_op jit(solution)/shard_map/pallas_call | solution.py:272
  191.6 2.0 shard_map.47.acc_in
  193.6 13.7 %collective-permute-done.18.refs_0_ = bf16[512,512]{1,0:T(8,128)(2,1)S(1)} collective-permute-done((bf16[512,512]{1,0:T(8,128)(2,1)S(1)}, bf16[512,512]{1,0:T(8,128)(2,1)S(1)}, u32[]{:S(2)}, u32[]{:S(2)}) %collective-permute-start.18) | collective-permute-done | bytes 524320 | tf_op jit(solution)/shard_map/ppermute | solution.py:313
  207.3 9.4 %collective-permute-done.19.refs_1_ = bf16[512,512]{1,0:T(8,128)(2,1)S(1)} collective-permute-done((bf16[512,512]{1,0:T(8,128)(2,1)S(1)}, bf16[512,512]{1,0:T(8,128)(2,1)S(1)}, u32[]{:S(2)}, u32[]{:S(2)}) %collective-permute-start.19) | collective-permute-done | bytes 524320 | tf_op jit(solution)/shard_map/ppermute | solution.py:313
  216.7 2.9 %shard_map.48.acc = f32[512,1024]{1,0:T(8,128)S(1)} custom-call(s32[2]{0:T(128)S(1)} %pad_add_fusion.where, f32[512,1024]{1,0:T(8,128)S(1)} %shard_map.47.acc_in, bf16[8,512,1024]{2,1,0:T(8,128)(2,1)S(1)} %get-tuple-element.14.right.right_all, bf16[512,512]{1,0:T(8,128)(2,1)S(1)} %collective-permute-done.18.refs_0_, ...), custom_call_target="tpu_custom_call" | custom-call | flops 2147483648 | bytes 12582912 | tf_op jit(solution)/shard_map/pallas_call | solution.py:272
  219.6 2.2 %shard_map.49 = f32[512,1024]{1,0:T(8,128)} custom-call(s32[2]{0:T(128)S(1)} %pad_add_fusion.where, f32[8,1024]{1,0:T(8,128)S(1)} %get-tuple-element.11.kept_ref, bf16[512,1024]{1,0:T(8,128)(2,1)S(1)} %get-tuple-element.15.squared, f32[512,1024]{1,0:T(8,128)S(1)} %shard_map.48.acc, bf16[512,1024]{1,0:T(8,128)(2,1)S(1)} %collective-permute-done.23.turn, ...), custom_call_target="tpu_custom_call" | custom-call | flops 1073741824 | bytes 12582912 | tf_op jit(solution)/shard_map/pallas_call | solution.py:272
  (56 shorter events, 33.0 us)
Async XLA Ops:
  3.4 26.2 %collective-permute-start.3 = (bf16[512,1024]{1,0:T(8,128)(2,1)S(1)}, bf16[512,1024]{1,0:T(8,128)(2,1)S(1)}, u32[]{:S(2)}, u32[]{:S(2)}) collective-permute-start(bf16[512,1024]{1,0:T(8,128)(2,1)S(1)} %get-tuple-element.12.own.refs_0_), channel_id=1, source_target_pairs={{0,8},{4,12},{8,0},{12,4},{16,24},{20,28},{24,16},{28,20},{1,9},{5... | collective-permute-start | bytes 3145736 | tf_op jit(solution)/shard_map/ppermute | solution.py:284
  6.4 28.5 %collective-permute-start = (bf16[512,1024]{1,0:T(8,128)(2,1)S(1)}, bf16[512,1024]{1,0:T(8,128)(2,1)S(1)}, u32[]{:S(2)}, u32[]{:S(2)}) collective-permute-start(bf16[512,1024]{1,0:T(8,128)(2,1)S(1)} %get-tuple-element.12.own.refs_0_), channel_id=1, source_target_pairs={{0,1},{1,0},{2,3},{3,2},{4,5},{5,4},{6,7},{7,6},{8,9},{9,8},{10,11... | collective-permute-start | bytes 3145736 | tf_op jit(solution)/shard_map/ppermute | solution.py:339
  8.0 27.5 %collective-permute-start.5 = (bf16[512,1024]{1,0:T(8,128)(2,1)S(1)}, bf16[512,1024]{1,0:T(8,128)(2,1)}, u32[]{:S(2)}, u32[]{:S(2)}) collective-permute-start(bf16[512,1024]{1,0:T(8,128)(2,1)S(1)} %get-tuple-element.12.own.refs_0_), channel_id=1, source_target_pairs={{0,16},{4,20},{8,24},{12,28},{16,0},{20,4},{24,8},{28,12},{1,17},{... | collective-permute-start | bytes 3145736 | tf_op jit(solution)/shard_map/ppermute | solution.py:284
  29.6 25.3 %collective-permute-start.7 = (bf16[512,1024]{1,0:T(8,128)(2,1)S(1)}, bf16[512,1024]{1,0:T(8,128)(2,1)}, u32[]{:S(2)}, u32[]{:S(2)}) collective-permute-start(bf16[512,1024]{1,0:T(8,128)(2,1)S(1)} %collective-permute-done.3.refs_2_), channel_id=1, source_target_pairs={{0,16},{4,20},{8,24},{12,28},{16,0},{20,4},{24,8},{28,12},{1,17},{... | collective-permute-start | bytes 3145736 | tf_op jit(solution)/shard_map/ppermute | solution.py:284
  31.3 25.9 %collective-permute-start.1 = (bf16[512,1024]{1,0:T(8,128)(2,1)S(1)}, bf16[512,1024]{1,0:T(8,128)(2,1)}, u32[]{:S(2)}, u32[]{:S(2)}) collective-permute-start(bf16[512,1024]{1,0:T(8,128)(2,1)S(1)} %get-tuple-element.12.own.refs_0_), channel_id=1, source_target_pairs={{0,3},{1,2},{2,1},{3,0},{4,7},{5,6},{6,5},{7,4},{8,11},{9,10},{10,... | collective-permute-start | bytes 3145736 | tf_op jit(solution)/shard_map/ppermute | solution.py:338
  34.9 22.3 %collective-permute-start.2 = (bf16[512,1024]{1,0:T(8,128)(2,1)S(1)}, bf16[512,1024]{1,0:T(8,128)(2,1)}, u32[]{:S(2)}, u32[]{:S(2)}) collective-permute-start(bf16[512,1024]{1,0:T(8,128)(2,1)S(1)} %get-tuple-element.12.own.refs_0_), channel_id=1, source_target_pairs={{0,4},{4,0},{8,12},{12,8},{16,20},{20,16},{24,28},{28,24},{1,5},{5... | collective-permute-start | bytes 3145736 | tf_op jit(solution)/shard_map/ppermute | solution.py:284
  34.9 22.3 %collective-permute-start.4 = (bf16[512,1024]{1,0:T(8,128)(2,1)S(1)}, bf16[512,1024]{1,0:T(8,128)(2,1)}, u32[]{:S(2)}, u32[]{:S(2)}) collective-permute-start(bf16[512,1024]{1,0:T(8,128)(2,1)S(1)} %collective-permute-done.3.refs_2_), channel_id=1, source_target_pairs={{0,4},{4,0},{8,12},{12,8},{16,20},{20,16},{24,28},{28,24},{1,5},{5... | collective-permute-start | bytes 3145736 | tf_op jit(solution)/shard_map/ppermute | solution.py:284
  35.5 21.8 %collective-permute-start.6 = (bf16[512,1024]{1,0:T(8,128)(2,1)}, bf16[512,1024]{1,0:T(8,128)(2,1)}, u32[]{:S(2)}, u32[]{:S(2)}) collective-permute-start(bf16[512,1024]{1,0:T(8,128)(2,1)} %collective-permute-done.5.refs_4_), channel_id=1, source_target_pairs={{0,4},{4,0},{8,12},{12,8},{16,20},{20,16},{24,28},{28,24},{1,5},{5... | collective-permute-start | bytes 3145736 | tf_op jit(solution)/shard_map/ppermute | solution.py:284
  63.8 119.5 %collective-permute-start.13 = (bf16[3,512,1024]{2,1,0:T(8,128)(2,1)S(1)}, bf16[3,512,1024]{2,1,0:T(8,128)(2,1)S(1)}, u32[]{:S(2)}, u32[]{:S(2)}) collective-permute-start(bf16[3,512,1024]{2,1,0:T(8,128)(2,1)S(1)} %get-tuple-element.16.refs_3_), channel_id=1, source_target_pairs={{0,4},{4,0},{8,12},{12,8},{16,20},{20,16},{24,28},{28,24},{1,5},{5... | collective-permute-start | bytes 9437192 | tf_op jit(solution)/shard_map/ppermute | solution.py:284
  64.0 45.7 %collective-permute-start.9 = (bf16[512,1024]{1,0:T(8,128)(2,1)}, bf16[512,1024]{1,0:T(8,128)(2,1)S(1)}, u32[]{:S(2)}, u32[]{:S(2)}) collective-permute-start(bf16[512,1024]{1,0:T(8,128)(2,1)} %collective-permute-done.1.cross), channel_id=1, source_target_pairs={{0,1},{1,0},{2,3},{3,2},{4,5},{5,4},{6,7},{7,6},{8,9},{9,8},{10,11... | collective-permute-start | bytes 3145736 | tf_op jit(solution)/shard_map/ppermute | solution.py:340
  109.7 48.5 %collective-permute-start.14 = (bf16[512,1024]{1,0:T(8,128)(2,1)S(1)}, bf16[512,1024]{1,0:T(8,128)(2,1)S(1)}, u32[]{:S(2)}, u32[]{:S(2)}) collective-permute-start(bf16[512,1024]{1,0:T(8,128)(2,1)S(1)} %collective-permute-done.9.far.refs_5_), channel_id=1, source_target_pairs={{0,4},{4,0},{8,12},{12,8},{16,20},{20,16},{24,28},{28,24},{1,5},{5... | collective-permute-start | bytes 3145736 | tf_op jit(solution)/shard_map/ppermute | solution.py:284
  111.9 70.0 %collective-permute-start.15 = (bf16[512,1024]{1,0:T(8,128)(2,1)S(1)}, bf16[512,1024]{1,0:T(8,128)(2,1)S(1)}, u32[]{:S(2)}, u32[]{:S(2)}) collective-permute-start(bf16[512,1024]{1,0:T(8,128)(2,1)S(1)} %get-tuple-element.15.squared), channel_id=1, source_target_pairs={{1,2},{2,3},{3,1},{5,6},{6,7},{7,5},{8,10},{10,11},{11,8},{12,14},... | collective-permute-start | bytes 3145736 | tf_op jit(solution)/shard_map/ppermute | solution.py:303
  114.5 52.7 %collective-permute-start.16 = (bf16[512,512]{1,0:T(8,128)(2,1)S(1)}, bf16[512,512]{1,0:T(8,128)(2,1)S(1)}, u32[]{:S(2)}, u32[]{:S(2)}) collective-permute-start(bf16[512,512]{1,0:T(8,128)(2,1)S(1)} %get-tuple-element.17), channel_id=1, source_target_pairs={{8,0},{12,4},{1,9},{5,13},{26,18},{30,22},{19,27},{23,31}} | collective-permute-start | bytes 1572872 | tf_op jit(solution)/shard_map/ppermute | solution.py:313
  117.2 6.5 %collective-permute-start.10 = (s32[4,8]{1,0:T(4,128)S(1)}, s32[4,8]{1,0:T(4,128)S(1)}, u32[]{:S(2)}, u32[]{:S(2)}) collective-permute-start(s32[4,8]{1,0:T(4,128)S(1)} %copy-done.2), channel_id=1, source_target_pairs={{0,1},{1,0},{2,3},{3,2},{4,5},{5,4},{6,7},{7,6},{8,9},{9,8},{10,11... | collective-permute-start | bytes 392 | tf_op jit(solution)/shard_map/ppermute | solution.py:341
  123.7 20.3 %collective-permute-start.25 = (f32[8,128]{1,0:T(8,128)S(1)}, f32[8,128]{1,0:T(8,128)S(1)}, u32[]{:S(2)}, u32[]{:S(2)}) collective-permute-start(f32[8,128]{1,0:T(8,128)S(1)} %shard_map.50.left), channel_id=1, source_target_pairs={{0,8},{4,12},{8,0},{12,4},{16,24},{20,28},{24,16},{28,20},{1,9},{5... | collective-permute-start | bytes 12296 | tf_op jit(solution)/shard_map/ppermute | solution.py:284
  152.1 5.4 %collective-permute-start.12 = (s32[4,8]{1,0:T(4,128)S(1)}, s32[4,8]{1,0:T(4,128)S(1)}, u32[]{:S(2)}, u32[]{:S(2)}) collective-permute-start(s32[4,8]{1,0:T(4,128)S(1)} %copy-done.2), channel_id=1, source_target_pairs={{0,3},{1,2},{2,1},{3,0},{4,7},{5,6},{6,5},{7,4},{8,11},{9,10},{10,... | collective-permute-start | bytes 392 | tf_op jit(solution)/shard_map/ppermute | solution.py:341
  161.1 5.4 %collective-permute-start.29 = (f32[8,128]{1,0:T(8,128)S(1)}, f32[8,128]{1,0:T(8,128)S(1)}, u32[]{:S(2)}, u32[]{:S(2)}) collective-permute-start(f32[8,128]{1,0:T(8,128)S(1)} %shard_map.52.own), channel_id=1, source_target_pairs={{0,3},{1,2},{2,1},{3,0},{4,7},{5,6},{6,5},{7,4},{8,11},{9,10},{10,... | collective-permute-start | bytes 12296 | tf_op jit(solution)/shard_map/ppermute | solution.py:427
  163.3 16.1 %collective-permute-start.17 = (bf16[512,512]{1,0:T(8,128)(2,1)S(1)}, bf16[512,512]{1,0:T(8,128)(2,1)S(1)}, u32[]{:S(2)}, u32[]{:S(2)}) collective-permute-start(bf16[512,512]{1,0:T(8,128)(2,1)S(1)} %get-tuple-element.18), channel_id=1, source_target_pairs={{8,4},{12,0},{1,13},{5,9},{26,22},{30,18},{19,31},{23,27}} | collective-permute-start | bytes 1572872 | tf_op jit(solution)/shard_map/ppermute | solution.py:313
  166.5 14.2 %collective-permute-start.21 = (bf16[512,512]{1,0:T(8,128)(2,1)S(1)}, bf16[512,512]{1,0:T(8,128)(2,1)S(1)}, u32[]{:S(2)}, u32[]{:S(2)}) collective-permute-start(bf16[512,512]{1,0:T(8,128)(2,1)S(1)} %get-tuple-element.18), channel_id=1, source_target_pairs={{24,8},{28,12},{17,1},{21,5},{10,26},{14,30},{3,19},{7,23}} | collective-permute-start | bytes 1572872 | tf_op jit(solution)/shard_map/ppermute | solution.py:313
  167.2 52.4 %collective-permute-start.23 = (bf16[512,1024]{1,0:T(8,128)(2,1)S(1)}, bf16[512,1024]{1,0:T(8,128)(2,1)S(1)}, u32[]{:S(2)}, u32[]{:S(2)}) collective-permute-start(bf16[512,1024]{1,0:T(8,128)(2,1)S(1)} %get-tuple-element.15.squared), channel_id=1, source_target_pairs={{1,3},{2,1},{3,2},{5,7},{6,5},{7,6},{8,11},{10,8},{11,10},{12,15},... | collective-permute-start | bytes 3145736 | tf_op jit(solution)/shard_map/ppermute | solution.py:303
  179.4 27.9 %collective-permute-start.18 = (bf16[512,512]{1,0:T(8,128)(2,1)S(1)}, bf16[512,512]{1,0:T(8,128)(2,1)S(1)}, u32[]{:S(2)}, u32[]{:S(2)}) collective-permute-start(bf16[512,512]{1,0:T(8,128)(2,1)S(1)} %get-tuple-element.17), channel_id=1, source_target_pairs={{16,0},{20,4},{25,9},{29,13},{2,18},{6,22},{11,27},{15,31}} | collective-permute-start | bytes 1572872 | tf_op jit(solution)/shard_map/ppermute | solution.py:313
  180.7 36.1 %collective-permute-start.19 = (bf16[512,512]{1,0:T(8,128)(2,1)S(1)}, bf16[512,512]{1,0:T(8,128)(2,1)S(1)}, u32[]{:S(2)}, u32[]{:S(2)}) collective-permute-start(bf16[512,512]{1,0:T(8,128)(2,1)S(1)} %get-tuple-element.18), channel_id=1, source_target_pairs={{16,4},{20,0},{25,13},{29,9},{2,22},{6,18},{11,31},{15,27}} | collective-permute-start | bytes 1572872 | tf_op jit(solution)/shard_map/ppermute | solution.py:313
  182.0 34.7 %collective-permute-start.20 = (bf16[512,512]{1,0:T(8,128)(2,1)S(1)}, bf16[512,512]{1,0:T(8,128)(2,1)S(1)}, u32[]{:S(2)}, u32[]{:S(2)}) collective-permute-start(bf16[512,512]{1,0:T(8,128)(2,1)S(1)} %get-tuple-element.17), channel_id=1, source_target_pairs={{24,0},{28,4},{17,9},{21,13},{10,18},{14,22},{3,27},{7,31}} | collective-permute-start | bytes 1572872 | tf_op jit(solution)/shard_map/ppermute | solution.py:313
  183.3 33.4 %collective-permute-start.22 = (bf16[512,512]{1,0:T(8,128)(2,1)S(1)}, bf16[512,512]{1,0:T(8,128)(2,1)S(1)}, u32[]{:S(2)}, u32[]{:S(2)}) collective-permute-start(bf16[512,512]{1,0:T(8,128)(2,1)S(1)} %collective-permute-done.21), channel_id=1, source_target_pairs={{8,4},{12,0},{1,13},{5,9},{26,22},{30,18},{19,31},{23,27}} | collective-permute-start | bytes 1572872 | tf_op jit(solution)/shard_map/ppermute | solution.py:313
  (9 other events, 30.6 us)
